TPU v7x, 1024 devices: a whole 4x4x32 slice. The times are simulated.
1024 devices in a mesh: gx: 32 (over z), gy: 4 (over x_lo, core), gz: 8 (over x_hi, y).
Axes of the slice: x: 4 (x_hi: 2, x_lo: 2; x = x_hi * 2 + x_lo), y: 4, z: 32, core: 2. Of those that a mesh axis runs over, the one named last changes fastest.
Arguments:
- orbitals: float32 [32, 4, 8, 96, 4096], P('gx', 'gy', 'gz'), may hold values from -6 to 6
- potential: float32 [256, 32, 64], P('gx', 'gy', 'gz'), may hold values from -1.5 to 1.5
- coefficients: float32 [32, 4, 8, 96, 256], P('gx', 'gy', 'gz'), may hold values from -0.6 to 0.6
Outputs:
- filtered_coefficients: float32 [32, 4, 8, 96, 256], P('gx', 'gy', 'gz')
All inputs are finite; a program needn't handle non-finite values.
Results may differ from a plain program's by a relative error of at most 0.0003.
Values sent between devices are 32-bit elements; how exact they have to be, the bound alone decides.
No kernel may reach another device: no remote copies, remote signals or barrier semaphores. Data moves between devices by JAX's collectives and lax.ppermute only.
A program may use at most 32 MiB of HBM per device.

v0:
```python
import jax
import jax.numpy as jnp
from jax import lax
from jax.sharding import PartitionSpec as P

CHEB = 2
NEWTON = 6
DG_STEPS = 3


cutoff = 1.0


def passed_along(shard, axis, by):
    devices = lax.axis_size(axis)
    return lax.ppermute(shard, axis, [(i, (i + by) % devices) for i in range(devices)])


def extended(cells, sides, width):
    for axis, dim in sides:
        count = lax.axis_size(axis)
        head = lax.slice_in_dim(cells, 0, width, axis=dim)
        tail = lax.slice_in_dim(cells, cells.shape[dim] - width, cells.shape[dim], axis=dim)
        cells = jnp.concatenate(
            [
                lax.ppermute(tail, axis, [(i, (i + 1) % count) for i in range(count)]),
                cells,
                lax.ppermute(head, axis, [((i + 1) % count, i) for i in range(count)]),
            ],
            axis=dim,
        )
    return cells


def matmul(left, right):
    return jnp.dot(left, right, precision=lax.Precision.HIGHEST, preferred_element_type=jnp.float32)


def box_masks(length):
    position = jnp.arange(length**3, dtype=jnp.int32)
    coordinates = (position // (length * length), position // length % length, position % length)
    mask_list = []
    for coordinate, stride in zip(coordinates, (length * length, length, 1)):
        mask_list.append(
            (
                stride,
                (coordinate > 0).astype(jnp.float32),
                (coordinate < length - 1).astype(jnp.float32),
            )
        )
    return mask_list


def apply_box(vectors, potential_flat, length):
    area = length * length
    cells = length**3
    padded = jnp.pad(vectors, ((0, 0), (area, area)))
    total = jnp.zeros_like(vectors)
    for stride, lower_ok, upper_ok in box_masks(length):
        total = (
            total
            + lower_ok * padded[:, area - stride : area - stride + cells]
            + upper_ok * padded[:, area + stride : area + stride + cells]
        )
    return (3.0 + potential_flat) * vectors - 0.5 * total


def chebyshev(operator, initial, degree, centre, half_width):
    prior_vectors = initial
    current = (operator(initial) - centre * initial) / half_width
    for repeat in range(degree - 1):
        following = 2.0 * (operator(current) - centre * current) / half_width - prior_vectors
        prior_vectors, current = (current, following)
    return current


def inverse_root(intersection, newton_count):
    sigma = jnp.sqrt(jnp.sum(intersection * intersection))
    identity = jnp.eye(intersection.shape[0], dtype=jnp.float32)
    current = intersection / sigma
    inverse = identity
    for repeat in range(newton_count):
        factor = 1.5 * identity - 0.5 * matmul(inverse, current)
        current = matmul(current, factor)
        inverse = matmul(factor, inverse)
    return inverse / jnp.sqrt(sigma)


def element_basis(orbital_rows, ext_potential, length, centre, half_width):
    doubled = 2 * length
    potential_flat = ext_potential.reshape(doubled**3)

    def extended_operator(vectors):
        return apply_box(vectors, potential_flat, doubled)

    filtered = chebyshev(extended_operator, orbital_rows, CHEB, centre, half_width)
    lower = length // 2
    restricted = filtered.reshape(-1, doubled, doubled, doubled)[
        :, lower : lower + length, lower : lower + length, lower : lower + length
    ]
    restricted = restricted.reshape(-1, length**3)
    intersection = matmul(restricted, restricted.T)
    basis = matmul(inverse_root(intersection, NEWTON), restricted)
    own_potential = ext_potential[
        lower : lower + length, lower : lower + length, lower : lower + length
    ].reshape(length**3)
    diagonal_block = matmul(basis, apply_box(basis, own_potential, length).T)
    return (basis, diagonal_block)


def face_layers(basis, length):
    cube = basis.reshape(-1, length, length, length)
    flat = length * length
    return (
        cube[:, 0, :, :].reshape(-1, flat),
        cube[:, length - 1, :, :].reshape(-1, flat),
        cube[:, :, 0, :].reshape(-1, flat),
        cube[:, :, length - 1, :].reshape(-1, flat),
        cube[:, :, :, 0].reshape(-1, flat),
        cube[:, :, :, length - 1].reshape(-1, flat),
    )


def per_device(orbitals, potential, coefficients):
    length = potential.shape[0]
    spectrum_top = 6.0 + lax.pmax(jnp.max(potential), ("gx", "gy", "gz"))
    centre = (spectrum_top + cutoff) / 2.0
    half_width = (spectrum_top - cutoff) / 2.0
    along_x = jnp.concatenate([passed_along(potential, "gx", 1), potential], axis=0)
    along_y = jnp.concatenate([passed_along(along_x, "gy", 1), along_x], axis=1)
    ext_potential = jnp.concatenate([passed_along(along_y, "gz", 1), along_y], axis=2)
    basis, diagonal_block = element_basis(
        orbitals[0, 0, 0], ext_potential, length, centre, half_width
    )
    faces = face_layers(basis, length)
    flat = length * length
    spatial = basis.T.reshape(length, length, length, basis.shape[0])
    grown_basis = extended(spatial, (("gx", 0), ("gy", 1), ("gz", 2)), 1)
    inner = slice(1, length + 1)
    neighbour_faces = (
        grown_basis[0, inner, inner].reshape(flat, -1),
        grown_basis[length + 1, inner, inner].reshape(flat, -1),
        grown_basis[inner, 0, inner].reshape(flat, -1),
        grown_basis[inner, length + 1, inner].reshape(flat, -1),
        grown_basis[inner, inner, 0].reshape(flat, -1),
        grown_basis[inner, inner, length + 1].reshape(flat, -1),
    )
    couplings = [
        -0.5 * matmul(own_face, other_face) for own_face, other_face in zip(faces, neighbour_faces)
    ]

    def galerkin(vectors):
        grown_rows = extended(
            vectors.reshape((1, 1, 1) + vectors.shape), (("gx", 0), ("gy", 1), ("gz", 2)), 1
        )
        result = matmul(diagonal_block, vectors)
        neighbour_rows = (
            grown_rows[0, 1, 1],
            grown_rows[2, 1, 1],
            grown_rows[1, 0, 1],
            grown_rows[1, 2, 1],
            grown_rows[1, 1, 0],
            grown_rows[1, 1, 2],
        )
        for coupling, rows_in in zip(couplings, neighbour_rows):
            result = result + matmul(coupling, rows_in)
        return result

    filtered = chebyshev(galerkin, coefficients[0, 0, 0], DG_STEPS, centre, half_width)
    return filtered.reshape(coefficients.shape)


def solution(mesh):
    placed = (P("gx", "gy", "gz", None, None), P("gx", "gy", "gz"), P("gx", "gy", "gz", None, None))
    return jax.shard_map(
        per_device,
        mesh=mesh,
        in_specs=placed,
        out_specs=P("gx", "gy", "gz", None, None),
        check_vma=False,
    )
```

profile of v0, /device:TPU:1, one launch (start us, length us, event | category | flops | bytes accessed | tf_op | source)
XLA Modules:
  0.0 383.5 jit_solution(14580930732869382495)
XLA Ops:
  0.0 4.4 %collective-permute-start.4 = (f32[1,1,1,96,256]{4,3,2,1,0:T(8,128)}, f32[1,1,1,96,256]{4,3,2,1,0:T(8,128)S(1)}, u32[]{:S(2)}, u32[]{:S(2)}) collective-permute-start(f32[1,1,1,96,256]{4,3,2,1,0:T(8,128)} %param.5), channel_id=1, source_target_pairs={{0,32},{32,64},{64,96},{96,128},{128,160},{160,192},{192,224},{224... | collective-permute-start | bytes 294920 | tf_op jit(solution)/shard_map/ppermute | solution.py:26
  4.4 16.8 %collective-permute-start.6 = (f32[1,1,1,96,256]{4,3,2,1,0:T(8,128)}, f32[1,1,1,96,256]{4,3,2,1,0:T(8,128)S(1)}, u32[]{:S(2)}, u32[]{:S(2)}) collective-permute-start(f32[1,1,1,96,256]{4,3,2,1,0:T(8,128)} %param.5), channel_id=1, source_target_pairs={{32,0},{64,32},{96,64},{128,96},{160,128},{192,160},{224,192},{256... | collective-permute-start | bytes 294920 | tf_op jit(solution)/shard_map/ppermute | solution.py:28
  23.1 4.1 %collective-permute-done = f32[8,8,8]{2,1,0:T(8,128)S(1)} collective-permute-done((f32[8,8,8]{2,1,0:T(8,128)}, f32[8,8,8]{2,1,0:T(8,128)S(1)}, u32[]{:S(2)}, u32[]{:S(2)}) %collective-permute-start) | collective-permute-done | bytes 2080 | tf_op jit(solution)/shard_map/ppermute | solution.py:16
  28.6 5.1 %collective-permute-start.1 = (f32[16,8,8]{2,1,0:T(8,128)S(1)}, f32[16,8,8]{2,1,0:T(8,128)S(1)}, u32[]{:S(2)}, u32[]{:S(2)}) collective-permute-start(f32[16,8,8]{2,1,0:T(8,128)S(1)} %get-tuple-element.15), channel_id=1, source_target_pairs={{0,8},{8,16},{16,24},{24,0},{1,9},{9,17},{17,25},{25,1},{2,10},{10... | collective-permute-start | bytes 12296 | tf_op jit(solution)/shard_map/ppermute | solution.py:16
  35.0 3.2 collective-permute-start.2
  38.3 154.1 %pmax.7 = f32[]{:T(128)} all-reduce(f32[]{:T(128)} %get-tuple-element.16), channel_id=1, replica_groups=mesh['gx'=32,'gy'=4,'gz'=8] {'gx','gy','gz'}, use_global_device_ids=true, to_apply=%region_1.0 | all-reduce | flops 1 | bytes 8 | tf_op jit(solution)/shard_map/pmax | solution.py:126
  193.9 7.5 %fusion.9 = f32[96,4096]{1,0:T(8,128)S(1)} fusion(f32[96,4096]{1,0:T(8,128)} %bitcast.198, f32[]{:T(128)S(6)} %div.95, f32[]{:T(128)S(6)} %div.94, f32[4096]{0:T(1024)S(1)} %get-tuple-element.22, f32[4096]{0:T(1024)S(1)} %get-tuple-element.21, f32[4096]{0:T(1024)S(1)} %get-tuple-element.23, f32[4096]{0:T(1024)S(1)} %get-tuple-element.24, ...), kind=kLoop, calls=%fused_computation.21 | loop fusion | flops 6684672 | bytes 3260424 | tf_op jit(solution)/shard_map/div | solution.py:70
  213.1 4.4 %collective-permute-start.5 = (f32[1,8,8,96]{3,2,1,0:T(8,128)S(1)}, f32[1,8,8,96]{3,2,1,0:T(8,128)S(1)}, u32[]{:S(2)}, u32[]{:S(2)}) collective-permute-start(f32[1,8,8,96]{3,2,1,0:T(8,128)S(1)} %bitcast.223), channel_id=1, source_target_pairs={{32,0},{64,32},{96,64},{128,96},{160,128},{192,160},{224,192},{256... | collective-permute-start | bytes 73736 | tf_op jit(solution)/shard_map/ppermute | solution.py:28
  223.5 3.8 collective-permute-start.7
  229.9 2.7 collective-permute-done.9
  234.6 7.0 %collective-permute-start.13 = (f32[10,10,1,96]{3,2,0,1:T(1,128)S(1)}, f32[10,10,1,96]{3,2,0,1:T(1,128)S(1)}, u32[]{:S(2)}, u32[]{:S(2)}) collective-permute-start(f32[10,10,1,96]{3,2,0,1:T(1,128)S(1)} %get-tuple-element.8), channel_id=1, source_target_pairs={{1,0},{2,1},{3,2},{4,3},{5,4},{6,5},{7,6},{0,7},{9,8},{10,9},{11,1... | collective-permute-start | bytes 115208 | tf_op jit(solution)/shard_map/ppermute | solution.py:28
  248.1 5.1 %collective-permute-done.10 = f32[3,1,1,96,256]{4,3,2,1,0:T(8,128)S(1)} collective-permute-done((f32[3,1,1,96,256]{4,3,2,1,0:T(8,128)S(1)}, f32[3,1,1,96,256]{4,3,2,1,0:T(8,128)S(1)}, u32[]{:S(2)}, u32[]{:S(2)}) %collective-permute-start.10) | collective-permute-done | bytes 294944 | tf_op jit(solution)/shard_map/ppermute | solution.py:28
  255.4 7.0 %collective-permute-start.14 = (f32[3,3,1,96,256]{4,3,2,1,0:T(8,128)S(1)}, f32[3,3,1,96,256]{4,3,2,1,0:T(8,128)S(1)}, u32[]{:S(2)}, u32[]{:S(2)}) collective-permute-start(f32[3,3,1,96,256]{4,3,2,1,0:T(8,128)S(1)} %pad_maximum_fusion), channel_id=1, source_target_pairs={{1,0},{2,1},{3,2},{4,3},{5,4},{6,5},{7,6},{0,7},{9,8},{10,9},{11,1... | collective-permute-start | bytes 2654216 | tf_op jit(solution)/shard_map/ppermute | solution.py:28
  263.2 16.7 %collective-permute-done.12 = f32[3,3,1,96,256]{4,3,2,1,0:T(8,128)S(1)} collective-permute-done((f32[3,3,1,96,256]{4,3,2,1,0:T(8,128)S(1)}, f32[3,3,1,96,256]{4,3,2,1,0:T(8,128)S(1)}, u32[]{:S(2)}, u32[]{:S(2)}) %collective-permute-start.12) | collective-permute-done | bytes 884768 | tf_op jit(solution)/shard_map/ppermute | solution.py:26
  284.3 4.6 %collective-permute-start.16 = (f32[1,1,1,96,256]{4,3,2,1,0:T(8,128)S(1)}, f32[1,1,1,96,256]{4,3,2,1,0:T(8,128)S(1)}, u32[]{:S(2)}, u32[]{:S(2)}) collective-permute-start(f32[1,1,1,96,256]{4,3,2,1,0:T(8,128)S(1)} %bitcast.200), channel_id=1, source_target_pairs={{32,0},{64,32},{96,64},{128,96},{160,128},{192,160},{224,192},{256... | collective-permute-start | bytes 294920 | tf_op jit(solution)/shard_map/ppermute | solution.py:28
  290.5 4.0 %collective-permute-start.17 = (f32[3,1,1,96,256]{4,3,2,1,0:T(8,128)S(1)}, f32[3,1,1,96,256]{4,3,2,1,0:T(8,128)S(1)}, u32[]{:S(2)}, u32[]{:S(2)}) collective-permute-start(f32[3,1,1,96,256]{4,3,2,1,0:T(8,128)S(1)} %pad_maximum_fusion.3), channel_id=1, source_target_pairs={{0,8},{8,16},{16,24},{24,0},{1,9},{9,17},{17,25},{25,1},{2,10},{10... | collective-permute-start | bytes 884744 | tf_op jit(solution)/shard_map/ppermute | solution.py:26
  298.1 4.5 %collective-permute-done.18 = f32[3,1,1,96,256]{4,3,2,1,0:T(8,128)S(1)} collective-permute-done((f32[3,1,1,96,256]{4,3,2,1,0:T(8,128)S(1)}, f32[3,1,1,96,256]{4,3,2,1,0:T(8,128)S(1)}, u32[]{:S(2)}, u32[]{:S(2)}) %collective-permute-start.18) | collective-permute-done | bytes 294944 | tf_op jit(solution)/shard_map/ppermute | solution.py:28
  305.0 8.2 %collective-permute-start.20 = (f32[3,3,1,96,256]{4,3,2,1,0:T(8,128)S(1)}, f32[3,3,1,96,256]{4,3,2,1,0:T(8,128)S(1)}, u32[]{:S(2)}, u32[]{:S(2)}) collective-permute-start(f32[3,3,1,96,256]{4,3,2,1,0:T(8,128)S(1)} %pad_maximum_fusion.1), channel_id=1, source_target_pairs={{1,0},{2,1},{3,2},{4,3},{5,4},{6,5},{7,6},{0,7},{9,8},{10,9},{11,1... | collective-permute-start | bytes 2654216 | tf_op jit(solution)/shard_map/ppermute | solution.py:28
  313.9 16.2 %collective-permute-done.19 = f32[3,3,1,96,256]{4,3,2,1,0:T(8,128)S(1)} collective-permute-done((f32[3,3,1,96,256]{4,3,2,1,0:T(8,128)S(1)}, f32[3,3,1,96,256]{4,3,2,1,0:T(8,128)S(1)}, u32[]{:S(2)}, u32[]{:S(2)}) %collective-permute-start.19) | collective-permute-done | bytes 884768 | tf_op jit(solution)/shard_map/ppermute | solution.py:26
  334.7 5.2 %collective-permute-start.22 = (f32[1,1,1,96,256]{4,3,2,1,0:T(8,128)S(1)}, f32[1,1,1,96,256]{4,3,2,1,0:T(8,128)S(1)}, u32[]{:S(2)}, u32[]{:S(2)}) collective-permute-start(f32[1,1,1,96,256]{4,3,2,1,0:T(8,128)S(1)} %bitcast.206), channel_id=1, source_target_pairs={{32,0},{64,32},{96,64},{128,96},{160,128},{192,160},{224,192},{256... | collective-permute-start | bytes 294920 | tf_op jit(solution)/shard_map/ppermute | solution.py:28
  342.1 2.9 collective-permute-start.23
  348.6 4.9 %collective-permute-done.24 = f32[3,1,1,96,256]{4,3,2,1,0:T(8,128)S(1)} collective-permute-done((f32[3,1,1,96,256]{4,3,2,1,0:T(8,128)S(1)}, f32[3,1,1,96,256]{4,3,2,1,0:T(8,128)S(1)}, u32[]{:S(2)}, u32[]{:S(2)}) %collective-permute-start.24) | collective-permute-done | bytes 294944 | tf_op jit(solution)/shard_map/ppermute | solution.py:28
  355.7 7.6 %collective-permute-start.26 = (f32[3,3,1,96,256]{4,3,2,1,0:T(8,128)S(1)}, f32[3,3,1,96,256]{4,3,2,1,0:T(8,128)S(1)}, u32[]{:S(2)}, u32[]{:S(2)}) collective-permute-start(f32[3,3,1,96,256]{4,3,2,1,0:T(8,128)S(1)} %pad_maximum_fusion.2), channel_id=1, source_target_pairs={{1,0},{2,1},{3,2},{4,3},{5,4},{6,5},{7,6},{0,7},{9,8},{10,9},{11,1... | collective-permute-start | bytes 2654216 | tf_op jit(solution)/shard_map/ppermute | solution.py:28
  364.0 16.3 %collective-permute-done.25 = f32[3,3,1,96,256]{4,3,2,1,0:T(8,128)S(1)} collective-permute-done((f32[3,3,1,96,256]{4,3,2,1,0:T(8,128)S(1)}, f32[3,3,1,96,256]{4,3,2,1,0:T(8,128)S(1)}, u32[]{:S(2)}, u32[]{:S(2)}) %collective-permute-start.25) | collective-permute-done | bytes 884768 | tf_op jit(solution)/shard_map/ppermute | solution.py:26
  (117 shorter events, 64.6 us)
Async XLA Ops:
  0.0 241.9 %collective-permute-start.4 = (f32[1,1,1,96,256]{4,3,2,1,0:T(8,128)}, f32[1,1,1,96,256]{4,3,2,1,0:T(8,128)S(1)}, u32[]{:S(2)}, u32[]{:S(2)}) collective-permute-start(f32[1,1,1,96,256]{4,3,2,1,0:T(8,128)} %param.5), channel_id=1, source_target_pairs={{0,32},{32,64},{64,96},{96,128},{128,160},{160,192},{192,224},{224... | collective-permute-start | bytes 294920 | tf_op jit(solution)/shard_map/ppermute | solution.py:26
  4.4 237.6 %collective-permute-start.6 = (f32[1,1,1,96,256]{4,3,2,1,0:T(8,128)}, f32[1,1,1,96,256]{4,3,2,1,0:T(8,128)S(1)}, u32[]{:S(2)}, u32[]{:S(2)}) collective-permute-start(f32[1,1,1,96,256]{4,3,2,1,0:T(8,128)} %param.5), channel_id=1, source_target_pairs={{32,0},{64,32},{96,64},{128,96},{160,128},{192,160},{224,192},{256... | collective-permute-start | bytes 294920 | tf_op jit(solution)/shard_map/ppermute | solution.py:28
  28.6 6.4 %collective-permute-start.1 = (f32[16,8,8]{2,1,0:T(8,128)S(1)}, f32[16,8,8]{2,1,0:T(8,128)S(1)}, u32[]{:S(2)}, u32[]{:S(2)}) collective-permute-start(f32[16,8,8]{2,1,0:T(8,128)S(1)} %get-tuple-element.15), channel_id=1, source_target_pairs={{0,8},{8,16},{16,24},{24,0},{1,9},{9,17},{17,25},{25,1},{2,10},{10... | collective-permute-start | bytes 12296 | tf_op jit(solution)/shard_map/ppermute | solution.py:16
  35.0 158.6 %collective-permute-start.2 = (f32[16,16,8]{2,1,0:T(8,128)S(1)}, f32[16,16,8]{2,1,0:T(8,128)S(1)}, u32[]{:S(2)}, u32[]{:S(2)}) collective-permute-start(f32[16,16,8]{2,1,0:T(8,128)S(1)} %pad_maximum_fusion.5), channel_id=1, source_target_pairs={{0,1},{1,2},{2,3},{3,4},{4,5},{5,6},{6,7},{7,0},{8,9},{9,10},{10,1... | collective-permute-start | bytes 24584 | tf_op jit(solution)/shard_map/ppermute | solution.py:16
  213.1 7.7 %collective-permute-start.5 = (f32[1,8,8,96]{3,2,1,0:T(8,128)S(1)}, f32[1,8,8,96]{3,2,1,0:T(8,128)S(1)}, u32[]{:S(2)}, u32[]{:S(2)}) collective-permute-start(f32[1,8,8,96]{3,2,1,0:T(8,128)S(1)} %bitcast.223), channel_id=1, source_target_pairs={{32,0},{64,32},{96,64},{128,96},{160,128},{192,160},{224,192},{256... | collective-permute-start | bytes 73736 | tf_op jit(solution)/shard_map/ppermute | solution.py:28
  223.5 6.5 %collective-permute-start.7 = (f32[10,1,8,96]{3,2,0,1:T(8,128)S(1)}, f32[10,1,8,96]{3,2,0,1:T(8,128)S(1)}, u32[]{:S(2)}, u32[]{:S(2)}) collective-permute-start(f32[10,1,8,96]{3,2,0,1:T(8,128)S(1)} %get-tuple-element.9), channel_id=1, source_target_pairs={{0,8},{8,16},{16,24},{24,0},{1,9},{9,17},{17,25},{25,1},{2,10},{10... | collective-permute-start | bytes 92168 | tf_op jit(solution)/shard_map/ppermute | solution.py:26
  232.7 14.3 %collective-permute-start.11 = (f32[10,10,1,96]{3,2,0,1:T(1,128)S(1)}, f32[10,10,1,96]{3,2,0,1:T(1,128)S(1)}, u32[]{:S(2)}, u32[]{:S(2)}) collective-permute-start(f32[10,10,1,96]{3,2,0,1:T(1,128)S(1)} %get-tuple-element.7), channel_id=1, source_target_pairs={{0,1},{1,2},{2,3},{3,4},{4,5},{5,6},{6,7},{7,0},{8,9},{9,10},{10,1... | collective-permute-start | bytes 115208 | tf_op jit(solution)/shard_map/ppermute | solution.py:26
  234.6 12.4 %collective-permute-start.13 = (f32[10,10,1,96]{3,2,0,1:T(1,128)S(1)}, f32[10,10,1,96]{3,2,0,1:T(1,128)S(1)}, u32[]{:S(2)}, u32[]{:S(2)}) collective-permute-start(f32[10,10,1,96]{3,2,0,1:T(1,128)S(1)} %get-tuple-element.8), channel_id=1, source_target_pairs={{1,0},{2,1},{3,2},{4,3},{5,4},{6,5},{7,6},{0,7},{9,8},{10,9},{11,1... | collective-permute-start | bytes 115208 | tf_op jit(solution)/shard_map/ppermute | solution.py:28
  241.9 6.1 %collective-permute-start.8 = (f32[3,1,1,96,256]{4,3,2,1,0:T(8,128)S(1)}, f32[3,1,1,96,256]{4,3,2,1,0:T(8,128)S(1)}, u32[]{:S(2)}, u32[]{:S(2)}) collective-permute-start(f32[3,1,1,96,256]{4,3,2,1,0:T(8,128)S(1)} %constant_dynamic-update-slice_fusion.2), channel_id=1, source_target_pairs={{0,8},{8,16},{16,24},{24,0},{1,9},{9,17},{17,25},{25,1},{2,10},{10... | collective-permute-start | bytes 884744 | tf_op jit(solution)/shard_map/ppermute | solution.py:26
  244.4 8.8 %collective-permute-start.10 = (f32[3,1,1,96,256]{4,3,2,1,0:T(8,128)S(1)}, f32[3,1,1,96,256]{4,3,2,1,0:T(8,128)S(1)}, u32[]{:S(2)}, u32[]{:S(2)}) collective-permute-start(f32[3,1,1,96,256]{4,3,2,1,0:T(8,128)S(1)} %constant_dynamic-update-slice_fusion.2), channel_id=1, source_target_pairs={{8,0},{16,8},{24,16},{0,24},{9,1},{17,9},{25,17},{1,25},{10,2},{18... | collective-permute-start | bytes 884744 | tf_op jit(solution)/shard_map/ppermute | solution.py:28
  253.2 26.7 %collective-permute-start.12 = (f32[3,3,1,96,256]{4,3,2,1,0:T(8,128)S(1)}, f32[3,3,1,96,256]{4,3,2,1,0:T(8,128)S(1)}, u32[]{:S(2)}, u32[]{:S(2)}) collective-permute-start(f32[3,3,1,96,256]{4,3,2,1,0:T(8,128)S(1)} %pad_maximum_fusion), channel_id=1, source_target_pairs={{0,1},{1,2},{2,3},{3,4},{4,5},{5,6},{6,7},{7,0},{8,9},{9,10},{10,1... | collective-permute-start | bytes 2654216 | tf_op jit(solution)/shard_map/ppermute | solution.py:26
  255.4 26.4 %collective-permute-start.14 = (f32[3,3,1,96,256]{4,3,2,1,0:T(8,128)S(1)}, f32[3,3,1,96,256]{4,3,2,1,0:T(8,128)S(1)}, u32[]{:S(2)}, u32[]{:S(2)}) collective-permute-start(f32[3,3,1,96,256]{4,3,2,1,0:T(8,128)S(1)} %pad_maximum_fusion), channel_id=1, source_target_pairs={{1,0},{2,1},{3,2},{4,3},{5,4},{6,5},{7,6},{0,7},{9,8},{10,9},{11,1... | collective-permute-start | bytes 2654216 | tf_op jit(solution)/shard_map/ppermute | solution.py:28
  282.3 7.0 %collective-permute-start.15 = (f32[1,1,1,96,256]{4,3,2,1,0:T(8,128)S(1)}, f32[1,1,1,96,256]{4,3,2,1,0:T(8,128)S(1)}, u32[]{:S(2)}, u32[]{:S(2)}) collective-permute-start(f32[1,1,1,96,256]{4,3,2,1,0:T(8,128)S(1)} %bitcast.199), channel_id=1, source_target_pairs={{0,32},{32,64},{64,96},{96,128},{128,160},{160,192},{192,224},{224... | collective-permute-start | bytes 294920 | tf_op jit(solution)/shard_map/ppermute | solution.py:26
  284.3 6.2 %collective-permute-start.16 = (f32[1,1,1,96,256]{4,3,2,1,0:T(8,128)S(1)}, f32[1,1,1,96,256]{4,3,2,1,0:T(8,128)S(1)}, u32[]{:S(2)}, u32[]{:S(2)}) collective-permute-start(f32[1,1,1,96,256]{4,3,2,1,0:T(8,128)S(1)} %bitcast.200), channel_id=1, source_target_pairs={{32,0},{64,32},{96,64},{128,96},{160,128},{192,160},{224,192},{256... | collective-permute-start | bytes 294920 | tf_op jit(solution)/shard_map/ppermute | solution.py:28
  290.5 7.6 %collective-permute-start.17 = (f32[3,1,1,96,256]{4,3,2,1,0:T(8,128)S(1)}, f32[3,1,1,96,256]{4,3,2,1,0:T(8,128)S(1)}, u32[]{:S(2)}, u32[]{:S(2)}) collective-permute-start(f32[3,1,1,96,256]{4,3,2,1,0:T(8,128)S(1)} %pad_maximum_fusion.3), channel_id=1, source_target_pairs={{0,8},{8,16},{16,24},{24,0},{1,9},{9,17},{17,25},{25,1},{2,10},{10... | collective-permute-start | bytes 884744 | tf_op jit(solution)/shard_map/ppermute | solution.py:26
  294.5 8.1 %collective-permute-start.18 = (f32[3,1,1,96,256]{4,3,2,1,0:T(8,128)S(1)}, f32[3,1,1,96,256]{4,3,2,1,0:T(8,128)S(1)}, u32[]{:S(2)}, u32[]{:S(2)}) collective-permute-start(f32[3,1,1,96,256]{4,3,2,1,0:T(8,128)S(1)} %pad_maximum_fusion.3), channel_id=1, source_target_pairs={{8,0},{16,8},{24,16},{0,24},{9,1},{17,9},{25,17},{1,25},{10,2},{18... | collective-permute-start | bytes 884744 | tf_op jit(solution)/shard_map/ppermute | solution.py:28
  302.6 27.5 %collective-permute-start.19 = (f32[3,3,1,96,256]{4,3,2,1,0:T(8,128)S(1)}, f32[3,3,1,96,256]{4,3,2,1,0:T(8,128)S(1)}, u32[]{:S(2)}, u32[]{:S(2)}) collective-permute-start(f32[3,3,1,96,256]{4,3,2,1,0:T(8,128)S(1)} %pad_maximum_fusion.1), channel_id=1, source_target_pairs={{0,1},{1,2},{2,3},{3,4},{4,5},{5,6},{6,7},{7,0},{8,9},{9,10},{10,1... | collective-permute-start | bytes 2654216 | tf_op jit(solution)/shard_map/ppermute | solution.py:26
  305.0 27.3 %collective-permute-start.20 = (f32[3,3,1,96,256]{4,3,2,1,0:T(8,128)S(1)}, f32[3,3,1,96,256]{4,3,2,1,0:T(8,128)S(1)}, u32[]{:S(2)}, u32[]{:S(2)}) collective-permute-start(f32[3,3,1,96,256]{4,3,2,1,0:T(8,128)S(1)} %pad_maximum_fusion.1), channel_id=1, source_target_pairs={{1,0},{2,1},{3,2},{4,3},{5,4},{6,5},{7,6},{0,7},{9,8},{10,9},{11,1... | collective-permute-start | bytes 2654216 | tf_op jit(solution)/shard_map/ppermute | solution.py:28
  332.8 8.4 %collective-permute-start.21 = (f32[1,1,1,96,256]{4,3,2,1,0:T(8,128)S(1)}, f32[1,1,1,96,256]{4,3,2,1,0:T(8,128)S(1)}, u32[]{:S(2)}, u32[]{:S(2)}) collective-permute-start(f32[1,1,1,96,256]{4,3,2,1,0:T(8,128)S(1)} %bitcast.205), channel_id=1, source_target_pairs={{0,32},{32,64},{64,96},{96,128},{128,160},{160,192},{192,224},{224... | collective-permute-start | bytes 294920 | tf_op jit(solution)/shard_map/ppermute | solution.py:26
  334.7 7.4 %collective-permute-start.22 = (f32[1,1,1,96,256]{4,3,2,1,0:T(8,128)S(1)}, f32[1,1,1,96,256]{4,3,2,1,0:T(8,128)S(1)}, u32[]{:S(2)}, u32[]{:S(2)}) collective-permute-start(f32[1,1,1,96,256]{4,3,2,1,0:T(8,128)S(1)} %bitcast.206), channel_id=1, source_target_pairs={{32,0},{64,32},{96,64},{128,96},{160,128},{192,160},{224,192},{256... | collective-permute-start | bytes 294920 | tf_op jit(solution)/shard_map/ppermute | solution.py:28
  342.1 6.5 %collective-permute-start.23 = (f32[3,1,1,96,256]{4,3,2,1,0:T(8,128)S(1)}, f32[3,1,1,96,256]{4,3,2,1,0:T(8,128)S(1)}, u32[]{:S(2)}, u32[]{:S(2)}) collective-permute-start(f32[3,1,1,96,256]{4,3,2,1,0:T(8,128)S(1)} %pad_maximum_fusion.4), channel_id=1, source_target_pairs={{0,8},{8,16},{16,24},{24,0},{1,9},{9,17},{17,25},{25,1},{2,10},{10... | collective-permute-start | bytes 884744 | tf_op jit(solution)/shard_map/ppermute | solution.py:26
  345.0 8.5 %collective-permute-start.24 = (f32[3,1,1,96,256]{4,3,2,1,0:T(8,128)S(1)}, f32[3,1,1,96,256]{4,3,2,1,0:T(8,128)S(1)}, u32[]{:S(2)}, u32[]{:S(2)}) collective-permute-start(f32[3,1,1,96,256]{4,3,2,1,0:T(8,128)S(1)} %pad_maximum_fusion.4), channel_id=1, source_target_pairs={{8,0},{16,8},{24,16},{0,24},{9,1},{17,9},{25,17},{1,25},{10,2},{18... | collective-permute-start | bytes 884744 | tf_op jit(solution)/shard_map/ppermute | solution.py:28
  353.6 26.8 %collective-permute-start.25 = (f32[3,3,1,96,256]{4,3,2,1,0:T(8,128)S(1)}, f32[3,3,1,96,256]{4,3,2,1,0:T(8,128)S(1)}, u32[]{:S(2)}, u32[]{:S(2)}) collective-permute-start(f32[3,3,1,96,256]{4,3,2,1,0:T(8,128)S(1)} %pad_maximum_fusion.2), channel_id=1, source_target_pairs={{0,1},{1,2},{2,3},{3,4},{4,5},{5,6},{6,7},{7,0},{8,9},{9,10},{10,1... | collective-permute-start | bytes 2654216 | tf_op jit(solution)/shard_map/ppermute | solution.py:26
  355.7 26.7 %collective-permute-start.26 = (f32[3,3,1,96,256]{4,3,2,1,0:T(8,128)S(1)}, f32[3,3,1,96,256]{4,3,2,1,0:T(8,128)S(1)}, u32[]{:S(2)}, u32[]{:S(2)}) collective-permute-start(f32[3,3,1,96,256]{4,3,2,1,0:T(8,128)S(1)} %pad_maximum_fusion.2), channel_id=1, source_target_pairs={{1,0},{2,1},{3,2},{4,3},{5,4},{6,5},{7,6},{0,7},{9,8},{10,9},{11,1... | collective-permute-start | bytes 2654216 | tf_op jit(solution)/shard_map/ppermute | solution.py:28
  (5 other events, 33.2 us)
where the time goes:
time: 385 us; the launch traced here: 384 us
  blocking collectives  154 us (40%)
  starting transfers between devices  110 us (29%)
  waiting for transfers between devices  88 us (23%)
  matrix products  13.8 us (4%)
  other arithmetic  11.1 us (3%)
    pmax x1, blocking collectives, per_device(): spectrum_top = 6.0 + lax.pmax(jnp.max(potential), ('gx', 'gy', 'gz'))  154 us
    ppermute x12, starting transfers between devices, extended(): lax.ppermute(head, axis, [((i + 1) % count, i) for i in range(count)])  68.8 us
    ppermute x12, waiting for transfers between devices, extended(): lax.ppermute(tail, axis, [(i, (i + 1) % count) for i in range(count)])  58.1 us
    ppermute x12, starting transfers between devices, extended(): lax.ppermute(tail, axis, [(i, (i + 1) % count) for i in range(count)])  31.1 us
    ppermute x12, waiting for transfers between devices, extended(): lax.ppermute(head, axis, [((i + 1) % count, i) for i in range(count)])  24.5 us
    dot_general x47, matrix products, matmul(): jnp.dot(left, right, precision=lax.Precision.HIGHEST, preferred_element_t...  13.8 us
    ppermute x3, starting transfers between devices, passed_along(): lax.ppermute(shard, axis, [(i, (i + by) % devices) for i in range(devices)])  10.2 us
  transfers between devices with their start and end apart: 27, of which 20 were waited for; matrix products, arithmetic and copies ran while one was open for 7% of the time, Pallas kernels for 0%

commit v1 on v0

v1 whole, which is shorter than its diff:
```python
import jax
import jax.numpy as jnp
from jax import lax
from jax.experimental import pallas as pl
from jax.experimental.pallas import tpu as pltpu
from jax.sharding import PartitionSpec as P

NEWTON = 6
DG_STEPS = 3
ROWS = 96
EDGE = 8
FLAT = EDGE * EDGE
COLS = 256
FACES = 6
BODY = FACES * FLAT
WIDTH = 512
cutoff = 1.0


def shifted(shard, axis, by):
    count = lax.axis_size(axis)
    return lax.ppermute(shard, axis, [(i, (i + by) % count) for i in range(count)])


def split(value):
    high = value.astype(jnp.bfloat16)
    low = (value - high.astype(jnp.float32)).astype(jnp.bfloat16)
    return high, low


def dot3(left, right, dims=(((1,), (0,)), ((), ()))):
    lh, ll = left
    rh, rl = right

    def one(a, b):
        return lax.dot_general(a, b, dims, preferred_element_type=jnp.float32)

    return one(lh, rh) + (one(lh, rl) + one(ll, rh))


def exact(left, right, dims=(((1,), (0,)), ((), ()))):
    return lax.dot_general(
        left, right, dims, precision=lax.Precision.HIGHEST, preferred_element_type=jnp.float32
    )


def lane_roll(value, by):
    return pltpu.roll(value, by % value.shape[-1], axis=value.ndim - 1)


def lanes(shape):
    return lax.broadcasted_iota(jnp.int32, shape, len(shape) - 1)


def basis_kernel(tiles_ref, orbitals_ref, vectors_ref, df_ref, ft_ref, scal_ref, traces_ref,
                 w_ref, restricted_ref, bt_ref):
    gy = lax.axis_index("gy")
    gz = lax.axis_index("gz")
    ny = lax.axis_size("gy")
    nz = lax.axis_size("gz")
    py = lax.rem(gy + ny - 1, ny)
    pz = lax.rem(gz + nz - 1, nz)
    near = lanes((8, 128)) % 16 < 8
    tallest = jnp.max(jnp.max(tiles_ref[...], axis=0)[5:6])
    top = 6.0 + tallest
    centre = (top + cutoff) / 2.0
    half_width = (top - cutoff) / 2.0
    scal_ref[0] = centre
    scal_ref[1] = half_width
    own_x, prior_x = [], []
    for row in (py, gy):
        low = tiles_ref[row * nz + pz]
        high = tiles_ref[row * nz + gz]
        own_x.append(jnp.where(near, low, lane_roll(high, 8)))
        prior_x.append(jnp.where(near, lane_roll(low, -8), high))
    own_x = jnp.concatenate(own_x, axis=1)
    prior_x = jnp.concatenate(prior_x, axis=1)
    planes = {}
    for plane in range(3, 13):
        source, row = (prior_x, plane) if plane < 8 else (own_x, plane - 8)
        planes[plane] = jnp.broadcast_to(source[row : row + 1], (8, 256))
        w_ref[plane - 3] = planes[plane] + (3.0 - centre)
    first_half = lanes((8, 128)) % 16 < 8

    def packed(even, odd):
        return jnp.where(first_half, lane_roll(even, -68)[:, :128], lane_roll(odd, -60)[:, :128])

    inverse = 1.0 / half_width

    def around(value):
        return (
            lane_roll(value, 1) + lane_roll(value, -1) + lane_roll(value, 16) + lane_roll(value, -16)
        )

    def filter_rows(step, carry):
        rows = pl.ds(pl.multiple_of(step * 8, 8), 8)
        start = {p: orbitals_ref[rows, p * 256 : (p + 1) * 256] for p in range(2, 14)}
        once = {}
        for p in range(3, 13):
            total = around(start[p]) + (start[p - 1] + start[p + 1])
            once[p] = (w_ref[p - 3] * start[p] - 0.5 * total) * inverse
        twice = {}
        for p in range(4, 12):
            total = around(once[p]) + (once[p - 1] + once[p + 1])
            twice[p] = (w_ref[p - 3] * once[p] - 0.5 * total) * (2.0 * inverse) - start[p]
        for q in range(4):
            restricted_ref[rows, q * 128 : (q + 1) * 128] = packed(twice[4 + 2 * q], twice[5 + 2 * q])
        return carry

    lax.fori_loop(0, ROWS // 8, filter_rows, 0)
    restricted = restricted_ref[...]
    halves = split(restricted)
    intersection = exact(restricted, restricted, (((1,), (1,)), ((), ())))
    sigma = jnp.sqrt(jnp.sum(intersection * intersection))
    identity = (
        lax.broadcasted_iota(jnp.int32, (ROWS, ROWS), 0) == lanes((ROWS, ROWS))
    ).astype(jnp.float32)
    current = intersection / sigma
    factor = 1.5 * identity - 0.5 * current
    current = exact(current, factor)
    root = factor
    for _ in range(NEWTON - 1):
        factor = 1.5 * identity - 0.5 * exact(root, current)
        current = exact(current, factor)
        root = exact(factor, root)
    root = root / jnp.sqrt(sigma)
    basis = dot3(split(root), halves)

    own = jnp.concatenate([packed(planes[4 + 2 * q], planes[5 + 2 * q]) for q in range(4)], axis=1)
    own = own[:1] + 3.0
    cell = lanes((ROWS, WIDTH))
    z = cell % 8
    y = cell // 16 % 8
    x = cell // 128 * 2 + cell // 8 % 2
    odd = x % 2 == 1

    def gate(ok, value):
        return jnp.where(ok, value, 0.0)

    total = gate(z > 0, lane_roll(basis, 1)) + gate(z < 7, lane_roll(basis, -1))
    total = total + gate(y > 0, lane_roll(basis, 16)) + gate(y < 7, lane_roll(basis, -16))
    total = total + jnp.where(odd, lane_roll(basis, 8), lane_roll(basis, -8))
    total = total + gate(
        (x > 0) & (x < 7), jnp.where(odd, lane_roll(basis, -120), lane_roll(basis, 120))
    )
    applied = own * basis - 0.5 * total
    diagonal = dot3(split(basis), split(applied), (((1,), (1,)), ((), ())))

    bt_ref[...] = jnp.concatenate([basis, jnp.zeros((128 - ROWS, WIDTH), jnp.float32)], axis=0).T
    pieces = [
        jnp.concatenate([bt_ref[yy * 16 : yy * 16 + 8] for yy in range(8)], axis=0),
        jnp.concatenate([bt_ref[392 + yy * 16 : 400 + yy * 16] for yy in range(8)], axis=0),
        jnp.concatenate([bt_ref[q * 128 : q * 128 + 16] for q in range(4)], axis=0),
        jnp.concatenate([bt_ref[q * 128 + 112 : q * 128 + 128] for q in range(4)], axis=0),
        bt_ref[pl.ds(0, FLAT, stride=8)],
        bt_ref[pl.ds(7, FLAT, stride=8)],
    ]
    faces_t = jnp.concatenate(pieces, axis=0)
    ft_ref[...] = faces_t[:, :ROWS]
    df_ref[:, :BODY] = -0.5 * faces_t.T[:ROWS]
    df_ref[:, BODY : BODY + ROWS] = diagonal
    df_ref[:, BODY + ROWS :] = jnp.zeros((ROWS, WIDTH - BODY - ROWS), jnp.float32)
    traces = dot3(split(faces_t[:, :ROWS]), split(vectors_ref[...]))
    for face in range(FACES):
        traces_ref[face] = traces[face * FLAT : (face + 1) * FLAT]


def step_kernel(first, last, scal_ref, df_ref, ft_ref, now_ref, prior_ref, *refs):
    halo_refs, out_refs = refs[:FACES], refs[FACES:]
    now = now_ref[...]
    stacked = jnp.concatenate(
        [r[...] for r in halo_refs] + [now, jnp.zeros((WIDTH - BODY - ROWS, COLS), jnp.float32)], axis=0
    )
    result = dot3(split(df_ref[...]), split(stacked))
    centre, half_width = scal_ref[0], scal_ref[1]
    if first:
        following = (result - centre * now) / half_width
    else:
        following = 2.0 * (result - centre * now) / half_width - prior_ref[...]
    out_refs[0][...] = following
    if not last:
        traces = dot3(split(ft_ref[...]), split(following))
        for face in range(FACES):
            out_refs[1][face] = traces[face * FLAT : (face + 1) * FLAT]


def vmem():
    return pl.BlockSpec(memory_space=pltpu.VMEM)


def smem():
    return pl.BlockSpec(memory_space=pltpu.SMEM)


def per_device(orbitals, potential, coefficients):
    nx = lax.axis_size("gx")
    plane = lax.axis_size("gy") * lax.axis_size("gz")
    spread = jnp.pad(potential, ((0, 0), (0, 0), (0, 8))).reshape(8, 128)
    below = shifted(spread, "gx", 1)
    peak = jnp.broadcast_to(jnp.max(potential), (nx, 1, 128))
    peak = jnp.max(lax.all_to_all(peak, "gx", 0, 0))
    near = lanes((8, 128)) % 16 < 8
    row = lax.broadcasted_iota(jnp.int32, (8, 128), 0)
    block = jnp.where(near, jnp.where(row == 5, peak, spread), jnp.roll(below, 8, axis=1))
    tiles = lax.all_to_all(jnp.broadcast_to(block, (plane, 8, 128)), ("gy", "gz"), 0, 0)

    f32 = jnp.float32
    rows = orbitals.reshape(ROWS, -1)
    start = coefficients.reshape(ROWS, COLS)
    df, ft, scal, traces = pl.pallas_call(
        basis_kernel,
        out_shape=(
            jax.ShapeDtypeStruct((ROWS, WIDTH), f32),
            jax.ShapeDtypeStruct((BODY, ROWS), f32),
            jax.ShapeDtypeStruct((2,), f32),
            jax.ShapeDtypeStruct((FACES, FLAT, COLS), f32),
        ),
        in_specs=[vmem(), vmem(), vmem()],
        out_specs=(vmem(), vmem(), smem(), vmem()),
        scratch_shapes=[
            pltpu.VMEM((10, 8, 256), f32),
            pltpu.VMEM((ROWS, WIDTH), f32),
            pltpu.VMEM((WIDTH, 128), f32),
        ],
        name="basis",
    )(tiles, rows, start)

    prior, now = start, start
    for step in range(DG_STEPS):
        halos = []
        for at, axis in enumerate(("gx", "gy", "gz")):
            halos.append(shifted(traces[2 * at + 1], axis, 1))
            halos.append(shifted(traces[2 * at], axis, -1))
        last = step == DG_STEPS - 1
        shapes = [jax.ShapeDtypeStruct((ROWS, COLS), f32)]
        if not last:
            shapes.append(jax.ShapeDtypeStruct((FACES, FLAT, COLS), f32))

        def body(*refs, step=step, last=last):
            step_kernel(step == 0, last, *refs)

        results = pl.pallas_call(
            body,
            out_shape=tuple(shapes),
            in_specs=[smem()] + [vmem()] * (4 + FACES),
            out_specs=tuple(vmem() for _ in shapes),
            name=f"step{step}",
        )(scal, df, ft, now, prior, *halos)
        prior, now = now, results[0]
        if not last:
            traces = results[1]
    return now.reshape(coefficients.shape)


def solution(mesh):
    placed = (P("gx", "gy", "gz", None, None), P("gx", "gy", "gz"), P("gx", "gy", "gz", None, None))
    return jax.shard_map(
        per_device,
        mesh=mesh,
        in_specs=placed,
        out_specs=P("gx", "gy", "gz", None, None),
        check_vma=False,
    )
```

time: 385 us -> 163 us (0.42)
  blocking collectives: 154 us -> 16.5 us
  waiting for transfers between devices: 88 us -> 27.5 us
  starting transfers between devices: 110 us -> 88.7 us
  Pallas kernels: 0 us -> 17.8 us
  matrix products: 13.8 us -> 0 us
  other arithmetic: 11.1 us -> 2.76 us
    pmax x1 -> x0, blocking collectives: 154 us -> none  [per_device(): spectrum_top = 6.0 + lax.pmax(jnp.max(potential), ('gx', 'gy', 'gz'))]
    ppermute x27 -> x19, waiting for transfers between devices: 88 us -> 13.1 us  [shifted(): lax.ppermute(shard, axis, [(i, (i + by) % count) for i in range(count)])]
    ppermute x27 -> x19, starting transfers between devices: 110 us -> 59.4 us  [shifted(): lax.ppermute(shard, axis, [(i, (i + by) % count) for i in range(count)])]
    all_to_all x0 -> x1, starting transfers between devices: none -> 29.3 us  [per_device(): peak = jnp.max(lax.all_to_all(peak, 'gx', 0, 0))]
    pallas_call x0 -> x4, Pallas kernels: none -> 17.8 us  [the longest x1 10.2 us: per_device(): pl.pallas_call(basis_kernel, out_shape=(jax.ShapeDtypeStruct((ROWS, WIDTH...]
    all_to_all x0 -> x1, blocking collectives: none -> 16.5 us  [per_device(): lax.all_to_all(jnp.broadcast_to(block, (plane, 8, 128)), ('gy', 'gz'), 0, 0)]
    all_to_all x0 -> x1, waiting for transfers between devices: none -> 14.4 us  [per_device(): peak = jnp.max(lax.all_to_all(peak, 'gx', 0, 0))]
    dot_general x47 -> x0, matrix products: 13.8 us -> none  [matmul(): jnp.dot(left, right, precision=lax.Precision.HIGHEST, preferred_element_t...]
  transfers between devices with their start and end apart: 27 -> 20, of which waited for: 20 -> 8; matrix products, arithmetic and copies ran while one was open for 7% -> 1% of each run, Pallas kernels for 0% -> 0%
where the time goes in v1:
time: 163 us; the launch traced here: 161 us
  starting transfers between devices  88.7 us (54%)
  waiting for transfers between devices  27.5 us (17%)
  Pallas kernels  17.8 us (11%)
  blocking collectives  16.5 us (10%)
  local copies, waits for them, and re-layouts  7.08 us (4%)
  other arithmetic  2.76 us (2%)
    ppermute x19, starting transfers between devices, shifted(): lax.ppermute(shard, axis, [(i, (i + by) % count) for i in range(count)])  59.4 us
    all_to_all x1, starting transfers between devices, per_device(): peak = jnp.max(lax.all_to_all(peak, 'gx', 0, 0))  29.3 us
    all_to_all x1, blocking collectives, per_device(): lax.all_to_all(jnp.broadcast_to(block, (plane, 8, 128)), ('gy', 'gz'), 0, 0)  16.5 us
    all_to_all x1, waiting for transfers between devices, per_device(): peak = jnp.max(lax.all_to_all(peak, 'gx', 0, 0))  14.4 us
    ppermute x19, waiting for transfers between devices, shifted(): lax.ppermute(shard, axis, [(i, (i + by) % count) for i in range(count)])  13.1 us
    pallas_call x1, Pallas kernels, per_device(): pl.pallas_call(basis_kernel, out_shape=(jax.ShapeDtypeStruct((ROWS, WIDTH...  10.2 us
    pallas_call x3, Pallas kernels, per_device(): pl.pallas_call(body, out_shape=tuple(shapes), in_specs=[smem()] + [vmem()...  7.54 us
  transfers between devices with their start and end apart: 20, of which 8 were waited for; matrix products, arithmetic and copies ran while one was open for 1% of the time, Pallas kernels for 0%

profile of v1, /device:TPU:1, one launch (start us, length us, event | category | flops | bytes accessed | tf_op | source)
XLA Modules:
  0.0 160.8 jit_solution(7365739988284661560)
XLA Ops:
  2.7 29.3 %all-to-all-start = ((f32[32,1,128]{2,1,0:T(1,128)}), f32[32,1,128]{2,1,0:T(1,128)S(1)}, u32[]{:S(2)}, u32[]{:S(2)}) async-start(f32[32,1,128]{2,1,0:T(1,128)} %broadcast_in_dim.10), calls=%async_computation | async-start | bytes 32768 | tf_op jit(solution)/shard_map/all_to_all | solution.py:201
  32.8 3.1 %collective-permute-start = (f32[8,128]{1,0:T(8,128)S(1)}, f32[8,128]{1,0:T(8,128)S(1)}, u32[]{:S(2)}, u32[]{:S(2)}) collective-permute-start(f32[8,128]{1,0:T(8,128)S(1)} %reshape.12), channel_id=1, source_target_pairs={{0,32},{32,64},{64,96},{96,128},{128,160},{160,192},{192,224},{224... | collective-permute-start | bytes 12296 | tf_op jit(solution)/shard_map/ppermute | solution.py:22
  36.0 2.7 %collective-permute-done = f32[8,128]{1,0:T(8,128)S(1)} collective-permute-done((f32[8,128]{1,0:T(8,128)S(1)}, f32[8,128]{1,0:T(8,128)S(1)}, u32[]{:S(2)}, u32[]{:S(2)}) %collective-permute-start) | collective-permute-done | bytes 4128 | tf_op jit(solution)/shard_map/ppermute | solution.py:22
  38.7 14.4 %all-to-all-done = f32[32,1,128]{2,1,0:T(1,128)S(1)} async-done(((f32[32,1,128]{2,1,0:T(1,128)}), f32[32,1,128]{2,1,0:T(1,128)S(1)}, u32[]{:S(2)}, u32[]{:S(2)}) %all-to-all-start) | async-done | bytes 16416 | tf_op jit(solution)/shard_map/all_to_all | solution.py:201
  54.5 16.5 %all_to_all.10.tiles_ref = f32[32,8,128]{2,1,0:T(8,128)} all-to-all(f32[32,8,128]{2,1,0:T(8,128)S(1)} %broadcast_in_dim.12), channel_id=1, replica_groups=mesh['gx'=32,'gy'=4,'gz'=8] {'gy','gz'}, dimensions={0} | all-to-all | bytes 262144 | tf_op jit(solution)/shard_map/all_to_all | solution.py:205
  71.0 10.2 %basis.1 = (f32[96,512]{1,0:T(8,128)}, f32[384,96]{1,0:T(8,128)}, f32[2]{0:T(128)}, f32[6,64,256]{2,1,0:T(8,128)}) custom-call(f32[32,8,128]{2,1,0:T(8,128)} %all_to_all.10.tiles_ref, f32[96,4096]{1,0:T(8,128)} %bitcast.45, f32[96,256]{1,0:T(8,128)} %bitcast.41), custom_call_target="tpu_custom_call" | custom-call | tf_op jit(solution)/shard_map/basis/pallas_call | solution.py:210
  82.3 3.9 %collective-permute-start.6 = (f32[64,256]{1,0:T(8,128)S(1)}, f32[64,256]{1,0:T(8,128)S(1)}, u32[]{:S(2)}, u32[]{:S(2)}) collective-permute-start(f32[64,256]{1,0:T(8,128)S(1)} %get-tuple-element.33), channel_id=1, source_target_pairs={{0,7},{1,0},{2,1},{3,2},{4,3},{5,4},{6,5},{7,6},{8,15},{9,8},{10,9... | collective-permute-start | bytes 196616 | tf_op jit(solution)/shard_map/ppermute | solution.py:22
  88.1 2.8 %collective-permute-start.4 = (f32[64,256]{1,0:T(8,128)S(1)}, f32[64,256]{1,0:T(8,128)S(1)}, u32[]{:S(2)}, u32[]{:S(2)}) collective-permute-start(f32[64,256]{1,0:T(8,128)S(1)} %get-tuple-element.35), channel_id=1, source_target_pairs={{0,24},{8,0},{16,8},{24,16},{1,25},{9,1},{17,9},{25,17},{2,26},{10... | collective-permute-start | bytes 196616 | tf_op jit(solution)/shard_map/ppermute | solution.py:22
  90.9 2.8 %collective-permute-start.3 = (f32[64,256]{1,0:T(8,128)S(1)}, f32[64,256]{1,0:T(8,128)S(1)}, u32[]{:S(2)}, u32[]{:S(2)}) collective-permute-start(f32[64,256]{1,0:T(8,128)S(1)} %get-tuple-element.36), channel_id=1, source_target_pairs={{0,8},{8,16},{16,24},{24,0},{1,9},{9,17},{17,25},{25,1},{2,10},{10... | collective-permute-start | bytes 196616 | tf_op jit(solution)/shard_map/ppermute | solution.py:22
  95.7 3.4 %collective-permute-start.1 = (f32[64,256]{1,0:T(8,128)S(1)}, f32[64,256]{1,0:T(8,128)S(1)}, u32[]{:S(2)}, u32[]{:S(2)}) collective-permute-start(f32[64,256]{1,0:T(8,128)S(1)} %get-tuple-element.38), channel_id=1, source_target_pairs={{0,32},{32,64},{64,96},{96,128},{128,160},{160,192},{192,224},{224... | collective-permute-start | bytes 196616 | tf_op jit(solution)/shard_map/ppermute | solution.py:22
  99.6 2.9 %collective-permute-done.1.refs_5_ = f32[64,256]{1,0:T(8,128)S(1)} collective-permute-done((f32[64,256]{1,0:T(8,128)S(1)}, f32[64,256]{1,0:T(8,128)S(1)}, u32[]{:S(2)}, u32[]{:S(2)}) %collective-permute-start.1) | collective-permute-done | bytes 65568 | tf_op jit(solution)/shard_map/ppermute | solution.py:22
  103.2 2.7 %step0.1 = (f32[96,256]{1,0:T(8,128)}, f32[6,64,256]{2,1,0:T(8,128)}) custom-call(f32[2]{0:T(128)} %get-tuple-element.13.refs_0_, f32[96,512]{1,0:T(8,128)} %get-tuple-element.14.refs_1_, f32[384,96]{1,0:T(8,128)} %get-tuple-element.15.refs_2_, f32[96,256]{1,0:T(8,128)} %bitcast.42, f32[96,256]{1,0:T(8,128)} %bitcast.43, f32[64,256]{1,0:T(8,128)} %copy-done.10, ...), custom_call_target="tpu_custom_call" | custom-call | tf_op jit(solution)/shard_map/step0/pallas_call | solution.py:242
  106.9 6.9 %collective-permute-start.12 = (f32[64,256]{1,0:T(8,128)S(1)}, f32[64,256]{1,0:T(8,128)S(1)}, u32[]{:S(2)}, u32[]{:S(2)}) collective-permute-start(f32[64,256]{1,0:T(8,128)S(1)} %get-tuple-element.27), channel_id=1, source_target_pairs={{0,7},{1,0},{2,1},{3,2},{4,3},{5,4},{6,5},{7,6},{8,15},{9,8},{10,9... | collective-permute-start | bytes 196616 | tf_op jit(solution)/shard_map/ppermute | solution.py:22
  115.7 3.0 %collective-permute-start.10 = (f32[64,256]{1,0:T(8,128)S(1)}, f32[64,256]{1,0:T(8,128)S(1)}, u32[]{:S(2)}, u32[]{:S(2)}) collective-permute-start(f32[64,256]{1,0:T(8,128)S(1)} %get-tuple-element.29), channel_id=1, source_target_pairs={{0,24},{8,0},{16,8},{24,16},{1,25},{9,1},{17,9},{25,17},{2,26},{10... | collective-permute-start | bytes 196616 | tf_op jit(solution)/shard_map/ppermute | solution.py:22
  118.7 2.5 %collective-permute-start.9 = (f32[64,256]{1,0:T(8,128)S(1)}, f32[64,256]{1,0:T(8,128)S(1)}, u32[]{:S(2)}, u32[]{:S(2)}) collective-permute-start(f32[64,256]{1,0:T(8,128)S(1)} %get-tuple-element.30), channel_id=1, source_target_pairs={{0,8},{8,16},{16,24},{24,0},{1,9},{9,17},{17,25},{25,1},{2,10},{10... | collective-permute-start | bytes 196616 | tf_op jit(solution)/shard_map/ppermute | solution.py:22
  123.2 3.4 %collective-permute-start.7 = (f32[64,256]{1,0:T(8,128)S(1)}, f32[64,256]{1,0:T(8,128)S(1)}, u32[]{:S(2)}, u32[]{:S(2)}) collective-permute-start(f32[64,256]{1,0:T(8,128)S(1)} %get-tuple-element.32), channel_id=1, source_target_pairs={{0,32},{32,64},{64,96},{96,128},{128,160},{160,192},{192,224},{224... | collective-permute-start | bytes 196616 | tf_op jit(solution)/shard_map/ppermute | solution.py:22
  127.0 3.2 %collective-permute-done.7.refs_5_ = f32[64,256]{1,0:T(8,128)S(1)} collective-permute-done((f32[64,256]{1,0:T(8,128)S(1)}, f32[64,256]{1,0:T(8,128)S(1)}, u32[]{:S(2)}, u32[]{:S(2)}) %collective-permute-start.7) | collective-permute-done | bytes 65568 | tf_op jit(solution)/shard_map/ppermute | solution.py:22
  130.8 2.7 %step1.1 = (f32[96,256]{1,0:T(8,128)}, f32[6,64,256]{2,1,0:T(8,128)}) custom-call(f32[2]{0:T(128)} %get-tuple-element.13.refs_0_, f32[96,512]{1,0:T(8,128)} %get-tuple-element.14.refs_1_, f32[384,96]{1,0:T(8,128)} %get-tuple-element.15.refs_2_, f32[96,256]{1,0:T(8,128)} %get-tuple-element.17.refs_3_.refs_4_, f32[96,256]{1,0:T(8,128)} %bitcast.44, ...), custom_call_target="tpu_custom_call" | custom-call | tf_op jit(solution)/shard_map/step1/pallas_call | solution.py:242
  134.5 7.1 %collective-permute-start.18 = (f32[64,256]{1,0:T(8,128)S(1)}, f32[64,256]{1,0:T(8,128)S(1)}, u32[]{:S(2)}, u32[]{:S(2)}) collective-permute-start(f32[64,256]{1,0:T(8,128)S(1)} %get-tuple-element.21), channel_id=1, source_target_pairs={{0,7},{1,0},{2,1},{3,2},{4,3},{5,4},{6,5},{7,6},{8,15},{9,8},{10,9... | collective-permute-start | bytes 196616 | tf_op jit(solution)/shard_map/ppermute | solution.py:22
  143.6 3.0 %collective-permute-start.16 = (f32[64,256]{1,0:T(8,128)S(1)}, f32[64,256]{1,0:T(8,128)S(1)}, u32[]{:S(2)}, u32[]{:S(2)}) collective-permute-start(f32[64,256]{1,0:T(8,128)S(1)} %get-tuple-element.23), channel_id=1, source_target_pairs={{0,24},{8,0},{16,8},{24,16},{1,25},{9,1},{17,9},{25,17},{2,26},{10... | collective-permute-start | bytes 196616 | tf_op jit(solution)/shard_map/ppermute | solution.py:22
  146.5 2.6 %collective-permute-start.15 = (f32[64,256]{1,0:T(8,128)S(1)}, f32[64,256]{1,0:T(8,128)S(1)}, u32[]{:S(2)}, u32[]{:S(2)}) collective-permute-start(f32[64,256]{1,0:T(8,128)S(1)} %get-tuple-element.24), channel_id=1, source_target_pairs={{0,8},{8,16},{16,24},{24,0},{1,9},{9,17},{17,25},{25,1},{2,10},{10... | collective-permute-start | bytes 196616 | tf_op jit(solution)/shard_map/ppermute | solution.py:22
  151.1 3.4 %collective-permute-start.13 = (f32[64,256]{1,0:T(8,128)S(1)}, f32[64,256]{1,0:T(8,128)S(1)}, u32[]{:S(2)}, u32[]{:S(2)}) collective-permute-start(f32[64,256]{1,0:T(8,128)S(1)} %get-tuple-element.26), channel_id=1, source_target_pairs={{0,32},{32,64},{64,96},{96,128},{128,160},{160,192},{192,224},{224... | collective-permute-start | bytes 196616 | tf_op jit(solution)/shard_map/ppermute | solution.py:22
  154.8 3.2 %collective-permute-done.13.refs_5_ = f32[64,256]{1,0:T(8,128)S(1)} collective-permute-done((f32[64,256]{1,0:T(8,128)S(1)}, f32[64,256]{1,0:T(8,128)S(1)}, u32[]{:S(2)}, u32[]{:S(2)}) %collective-permute-start.13) | collective-permute-done | bytes 65568 | tf_op jit(solution)/shard_map/ppermute | solution.py:22
  158.6 2.1 %step2.1 = f32[96,256]{1,0:T(8,128)} custom-call(f32[2]{0:T(128)} %get-tuple-element.13.refs_0_, f32[96,512]{1,0:T(8,128)} %get-tuple-element.14.refs_1_, f32[384,96]{1,0:T(8,128)} %get-tuple-element.15.refs_2_, f32[96,256]{1,0:T(8,128)} %get-tuple-element.19.refs_3_, f32[96,256]{1,0:T(8,128)} %get-tuple-element.17.refs_3_.refs_4_, f32[64,256]{1,0:T(8,128)} %copy-done.17, ...), custom_call_target="tpu_custom_call" | custom-call | tf_op jit(solution)/shard_map/step2/pallas_call | solution.py:242
  (71 shorter events, 22.5 us)
Async XLA Ops:
  2.7 50.5 %all-to-all-start = ((f32[32,1,128]{2,1,0:T(1,128)}), f32[32,1,128]{2,1,0:T(1,128)S(1)}, u32[]{:S(2)}, u32[]{:S(2)}) async-start(f32[32,1,128]{2,1,0:T(1,128)} %broadcast_in_dim.10), calls=%async_computation | async-start | bytes 32768 | tf_op jit(solution)/shard_map/all_to_all | solution.py:201
  32.8 5.8 %collective-permute-start = (f32[8,128]{1,0:T(8,128)S(1)}, f32[8,128]{1,0:T(8,128)S(1)}, u32[]{:S(2)}, u32[]{:S(2)}) collective-permute-start(f32[8,128]{1,0:T(8,128)S(1)} %reshape.12), channel_id=1, source_target_pairs={{0,32},{32,64},{64,96},{96,128},{128,160},{160,192},{192,224},{224... | collective-permute-start | bytes 12296 | tf_op jit(solution)/shard_map/ppermute | solution.py:22
  82.3 13.4 %collective-permute-start.6 = (f32[64,256]{1,0:T(8,128)S(1)}, f32[64,256]{1,0:T(8,128)S(1)}, u32[]{:S(2)}, u32[]{:S(2)}) collective-permute-start(f32[64,256]{1,0:T(8,128)S(1)} %get-tuple-element.33), channel_id=1, source_target_pairs={{0,7},{1,0},{2,1},{3,2},{4,3},{5,4},{6,5},{7,6},{8,15},{9,8},{10,9... | collective-permute-start | bytes 196616 | tf_op jit(solution)/shard_map/ppermute | solution.py:22
  86.2 12.8 %collective-permute-start.5 = (f32[64,256]{1,0:T(8,128)S(1)}, f32[64,256]{1,0:T(8,128)S(1)}, u32[]{:S(2)}, u32[]{:S(2)}) collective-permute-start(f32[64,256]{1,0:T(8,128)S(1)} %get-tuple-element.34), channel_id=1, source_target_pairs={{0,1},{1,2},{2,3},{3,4},{4,5},{5,6},{6,7},{7,0},{8,9},{9,10},{10,1... | collective-permute-start | bytes 196616 | tf_op jit(solution)/shard_map/ppermute | solution.py:22
  88.1 10.9 %collective-permute-start.4 = (f32[64,256]{1,0:T(8,128)S(1)}, f32[64,256]{1,0:T(8,128)S(1)}, u32[]{:S(2)}, u32[]{:S(2)}) collective-permute-start(f32[64,256]{1,0:T(8,128)S(1)} %get-tuple-element.35), channel_id=1, source_target_pairs={{0,24},{8,0},{16,8},{24,16},{1,25},{9,1},{17,9},{25,17},{2,26},{10... | collective-permute-start | bytes 196616 | tf_op jit(solution)/shard_map/ppermute | solution.py:22
  90.9 8.1 %collective-permute-start.3 = (f32[64,256]{1,0:T(8,128)S(1)}, f32[64,256]{1,0:T(8,128)S(1)}, u32[]{:S(2)}, u32[]{:S(2)}) collective-permute-start(f32[64,256]{1,0:T(8,128)S(1)} %get-tuple-element.36), channel_id=1, source_target_pairs={{0,8},{8,16},{16,24},{24,0},{1,9},{9,17},{17,25},{25,1},{2,10},{10... | collective-permute-start | bytes 196616 | tf_op jit(solution)/shard_map/ppermute | solution.py:22
  93.7 5.9 %collective-permute-start.2 = (f32[64,256]{1,0:T(8,128)S(1)}, f32[64,256]{1,0:T(8,128)S(1)}, u32[]{:S(2)}, u32[]{:S(2)}) collective-permute-start(f32[64,256]{1,0:T(8,128)S(1)} %get-tuple-element.37), channel_id=1, source_target_pairs={{0,992},{32,0},{64,32},{96,64},{128,96},{160,128},{192,160},{224,1... | collective-permute-start | bytes 196616 | tf_op jit(solution)/shard_map/ppermute | solution.py:22
  95.7 6.9 %copy-start = (f32[64,256]{1,0:T(8,128)}, f32[64,256]{1,0:T(8,128)S(1)}, u32[]{:S(2)}) copy-start(f32[64,256]{1,0:T(8,128)S(1)} %collective-permute-done.6.refs_10_) | copy-start | bytes 196612
  95.7 6.9 %collective-permute-start.1 = (f32[64,256]{1,0:T(8,128)S(1)}, f32[64,256]{1,0:T(8,128)S(1)}, u32[]{:S(2)}, u32[]{:S(2)}) collective-permute-start(f32[64,256]{1,0:T(8,128)S(1)} %get-tuple-element.38), channel_id=1, source_target_pairs={{0,32},{32,64},{64,96},{96,128},{128,160},{160,192},{192,224},{224... | collective-permute-start | bytes 196616 | tf_op jit(solution)/shard_map/ppermute | solution.py:22
  106.9 16.3 %collective-permute-start.12 = (f32[64,256]{1,0:T(8,128)S(1)}, f32[64,256]{1,0:T(8,128)S(1)}, u32[]{:S(2)}, u32[]{:S(2)}) collective-permute-start(f32[64,256]{1,0:T(8,128)S(1)} %get-tuple-element.27), channel_id=1, source_target_pairs={{0,7},{1,0},{2,1},{3,2},{4,3},{5,4},{6,5},{7,6},{8,15},{9,8},{10,9... | collective-permute-start | bytes 196616 | tf_op jit(solution)/shard_map/ppermute | solution.py:22
  113.8 12.8 %collective-permute-start.11 = (f32[64,256]{1,0:T(8,128)S(1)}, f32[64,256]{1,0:T(8,128)S(1)}, u32[]{:S(2)}, u32[]{:S(2)}) collective-permute-start(f32[64,256]{1,0:T(8,128)S(1)} %get-tuple-element.28), channel_id=1, source_target_pairs={{0,1},{1,2},{2,3},{3,4},{4,5},{5,6},{6,7},{7,0},{8,9},{9,10},{10,1... | collective-permute-start | bytes 196616 | tf_op jit(solution)/shard_map/ppermute | solution.py:22
  115.7 10.9 %collective-permute-start.10 = (f32[64,256]{1,0:T(8,128)S(1)}, f32[64,256]{1,0:T(8,128)S(1)}, u32[]{:S(2)}, u32[]{:S(2)}) collective-permute-start(f32[64,256]{1,0:T(8,128)S(1)} %get-tuple-element.29), channel_id=1, source_target_pairs={{0,24},{8,0},{16,8},{24,16},{1,25},{9,1},{17,9},{25,17},{2,26},{10... | collective-permute-start | bytes 196616 | tf_op jit(solution)/shard_map/ppermute | solution.py:22
  118.7 7.9 %collective-permute-start.9 = (f32[64,256]{1,0:T(8,128)S(1)}, f32[64,256]{1,0:T(8,128)S(1)}, u32[]{:S(2)}, u32[]{:S(2)}) collective-permute-start(f32[64,256]{1,0:T(8,128)S(1)} %get-tuple-element.30), channel_id=1, source_target_pairs={{0,8},{8,16},{16,24},{24,0},{1,9},{9,17},{17,25},{25,1},{2,10},{10... | collective-permute-start | bytes 196616 | tf_op jit(solution)/shard_map/ppermute | solution.py:22
  121.3 5.7 %collective-permute-start.8 = (f32[64,256]{1,0:T(8,128)S(1)}, f32[64,256]{1,0:T(8,128)S(1)}, u32[]{:S(2)}, u32[]{:S(2)}) collective-permute-start(f32[64,256]{1,0:T(8,128)S(1)} %get-tuple-element.31), channel_id=1, source_target_pairs={{0,992},{32,0},{64,32},{96,64},{128,96},{160,128},{192,160},{224,1... | collective-permute-start | bytes 196616 | tf_op jit(solution)/shard_map/ppermute | solution.py:22
  123.2 6.9 %copy-start.1 = (f32[64,256]{1,0:T(8,128)}, f32[64,256]{1,0:T(8,128)S(1)}, u32[]{:S(2)}) copy-start(f32[64,256]{1,0:T(8,128)S(1)} %collective-permute-done.12.refs_10_) | copy-start | bytes 196612
  123.2 6.9 %collective-permute-start.7 = (f32[64,256]{1,0:T(8,128)S(1)}, f32[64,256]{1,0:T(8,128)S(1)}, u32[]{:S(2)}, u32[]{:S(2)}) collective-permute-start(f32[64,256]{1,0:T(8,128)S(1)} %get-tuple-element.32), channel_id=1, source_target_pairs={{0,32},{32,64},{64,96},{96,128},{128,160},{160,192},{192,224},{224... | collective-permute-start | bytes 196616 | tf_op jit(solution)/shard_map/ppermute | solution.py:22
  134.5 16.6 %collective-permute-start.18 = (f32[64,256]{1,0:T(8,128)S(1)}, f32[64,256]{1,0:T(8,128)S(1)}, u32[]{:S(2)}, u32[]{:S(2)}) collective-permute-start(f32[64,256]{1,0:T(8,128)S(1)} %get-tuple-element.21), channel_id=1, source_target_pairs={{0,7},{1,0},{2,1},{3,2},{4,3},{5,4},{6,5},{7,6},{8,15},{9,8},{10,9... | collective-permute-start | bytes 196616 | tf_op jit(solution)/shard_map/ppermute | solution.py:22
  141.6 12.8 %collective-permute-start.17 = (f32[64,256]{1,0:T(8,128)S(1)}, f32[64,256]{1,0:T(8,128)S(1)}, u32[]{:S(2)}, u32[]{:S(2)}) collective-permute-start(f32[64,256]{1,0:T(8,128)S(1)} %get-tuple-element.22), channel_id=1, source_target_pairs={{0,1},{1,2},{2,3},{3,4},{4,5},{5,6},{6,7},{7,0},{8,9},{9,10},{10,1... | collective-permute-start | bytes 196616 | tf_op jit(solution)/shard_map/ppermute | solution.py:22
  143.6 10.9 %collective-permute-start.16 = (f32[64,256]{1,0:T(8,128)S(1)}, f32[64,256]{1,0:T(8,128)S(1)}, u32[]{:S(2)}, u32[]{:S(2)}) collective-permute-start(f32[64,256]{1,0:T(8,128)S(1)} %get-tuple-element.23), channel_id=1, source_target_pairs={{0,24},{8,0},{16,8},{24,16},{1,25},{9,1},{17,9},{25,17},{2,26},{10... | collective-permute-start | bytes 196616 | tf_op jit(solution)/shard_map/ppermute | solution.py:22
  146.5 8.0 %collective-permute-start.15 = (f32[64,256]{1,0:T(8,128)S(1)}, f32[64,256]{1,0:T(8,128)S(1)}, u32[]{:S(2)}, u32[]{:S(2)}) collective-permute-start(f32[64,256]{1,0:T(8,128)S(1)} %get-tuple-element.24), channel_id=1, source_target_pairs={{0,8},{8,16},{16,24},{24,0},{1,9},{9,17},{17,25},{25,1},{2,10},{10... | collective-permute-start | bytes 196616 | tf_op jit(solution)/shard_map/ppermute | solution.py:22
  149.1 5.7 %collective-permute-start.14 = (f32[64,256]{1,0:T(8,128)S(1)}, f32[64,256]{1,0:T(8,128)S(1)}, u32[]{:S(2)}, u32[]{:S(2)}) collective-permute-start(f32[64,256]{1,0:T(8,128)S(1)} %get-tuple-element.25), channel_id=1, source_target_pairs={{0,992},{32,0},{64,32},{96,64},{128,96},{160,128},{192,160},{224,1... | collective-permute-start | bytes 196616 | tf_op jit(solution)/shard_map/ppermute | solution.py:22
  151.1 6.9 %copy-start.12 = (f32[64,256]{1,0:T(8,128)}, f32[64,256]{1,0:T(8,128)S(1)}, u32[]{:S(2)}) copy-start(f32[64,256]{1,0:T(8,128)S(1)} %collective-permute-done.18.refs_10_) | copy-start | bytes 196612
  151.1 6.9 %collective-permute-start.13 = (f32[64,256]{1,0:T(8,128)S(1)}, f32[64,256]{1,0:T(8,128)S(1)}, u32[]{:S(2)}, u32[]{:S(2)}) collective-permute-start(f32[64,256]{1,0:T(8,128)S(1)} %get-tuple-element.26), channel_id=1, source_target_pairs={{0,32},{32,64},{64,96},{96,128},{128,160},{160,192},{192,224},{224... | collective-permute-start | bytes 196616 | tf_op jit(solution)/shard_map/ppermute | solution.py:22
  154.5 3.5 %copy-start.13 = (f32[64,256]{1,0:T(8,128)}, f32[64,256]{1,0:T(8,128)S(1)}, u32[]{:S(2)}) copy-start(f32[64,256]{1,0:T(8,128)S(1)} %collective-permute-done.17.refs_9_) | copy-start | bytes 196612
  (14 other events, 39.1 us)

commit v2 on v1

v2 whole, which is shorter than its diff:
```python
import jax
import jax.numpy as jnp
from jax import lax
from jax.experimental import pallas as pl
from jax.experimental.pallas import tpu as pltpu
from jax.sharding import PartitionSpec as P

NEWTON = 6
DG_STEPS = 3
SHIFT = 3.0
ROWS = 96
EDGE = 8
FLAT = EDGE * EDGE
COLS = 256
FACES = 6
CUBE = 8
GRANT = 16 << 20
BODY = FACES * FLAT
WIDTH = 512
cutoff = 1.0


def shifted(shard, axis, by):
    count = lax.axis_size(axis)
    return lax.ppermute(shard, axis, [(i, (i + by) % count) for i in range(count)])


def split(value):
    high = value.astype(jnp.bfloat16)
    low = (value - high.astype(jnp.float32)).astype(jnp.bfloat16)
    return high, low


def dot3(left, right, dims=(((1,), (0,)), ((), ()))):
    lh, ll = left
    rh, rl = right

    def one(a, b):
        return lax.dot_general(a, b, dims, preferred_element_type=jnp.float32)

    return one(lh, rh) + (one(lh, rl) + one(ll, rh))


def exact(left, right, dims=(((1,), (0,)), ((), ()))):
    return lax.dot_general(
        left, right, dims, precision=lax.Precision.HIGHEST, preferred_element_type=jnp.float32
    )


def lane_roll(value, by):
    return pltpu.roll(value, by % value.shape[-1], axis=value.ndim - 1)


def lanes(shape):
    return lax.broadcasted_iota(jnp.int32, shape, len(shape) - 1)


AXES = ("gx", "gy", "gz")


def parities():
    return [lax.rem(lax.axis_index(axis), 2) for axis in AXES]


def place():
    a, b, c = parities()
    return CUBE - 1 - (a * 4 + b * 2 + c)


def cubes():
    sizes = [lax.axis_size(axis) for axis in AXES]
    groups = []
    for i in range(sizes[0] // 2):
        for j in range(sizes[1] // 2):
            for k in range(sizes[2] // 2):
                group = []
                for spot in range(CUBE):
                    at = [
                        (2 * base + 1 + (spot >> (2 - axis) & 1)) % sizes[axis]
                        for axis, base in enumerate((i, j, k))
                    ]
                    group.append((at[0] * sizes[1] + at[1]) * sizes[2] + at[2])
                groups.append(group)
    return groups


def swapped(shard, axis):
    return lax.ppermute(shard, axis, [(i, i ^ 1) for i in range(lax.axis_size(axis))])


def tiles_kernel(tiles_ref, peak_ref, wide_ref):
    ny = lax.axis_size("gy")
    nz = lax.axis_size("gz")
    gy = lax.axis_index("gy")
    gz = lax.axis_index("gz")
    py = lax.rem(gy + ny - 1, ny)
    pz = lax.rem(gz + nz - 1, nz)
    near = lanes((8, 128)) % 16 < 8
    peak_ref[...] = jnp.broadcast_to(jnp.max(tiles_ref[...]), peak_ref.shape)
    for half, row in enumerate((py, gy)):
        low = tiles_ref[row * nz + pz]
        high = tiles_ref[row * nz + gz]
        wide_ref[:, half * 128 : (half + 1) * 128] = jnp.where(near, low, lane_roll(high, 8))


def filter_kernel(wide_ref, below_ref, orbitals_ref, u0_ref, u1_ref, u2_ref, own_ref, w_ref):
    first_half = lanes((8, 128)) % 16 < 8

    def packed(even, odd):
        return jnp.where(first_half, lane_roll(even, -68)[:, :128], lane_roll(odd, -60)[:, :128])

    planes = {}
    for plane in range(3, 13):
        row = below_ref[plane : plane + 1] if plane < 8 else wide_ref[plane - 8 : plane - 7]
        planes[plane] = jnp.broadcast_to(row, (8, 256)) + (3.0 - SHIFT)
        w_ref[plane - 3] = planes[plane]
    for q in range(4):
        own_ref[:, q * 128 : (q + 1) * 128] = packed(planes[4 + 2 * q], planes[5 + 2 * q])

    def around(value):
        return (
            lane_roll(value, 1) + lane_roll(value, -1) + lane_roll(value, 16) + lane_roll(value, -16)
        )

    def filter_rows(step, carry):
        rows = pl.ds(pl.multiple_of(step * 8, 8), 8)
        start = {p: orbitals_ref[rows, p * 256 : (p + 1) * 256] for p in range(2, 14)}
        once = {}
        for p in range(3, 13):
            total = around(start[p]) + (start[p - 1] + start[p + 1])
            once[p] = w_ref[p - 3] * start[p] - 0.5 * total
        twice = {}
        for p in range(4, 12):
            total = around(once[p]) + (once[p - 1] + once[p + 1])
            twice[p] = w_ref[p - 3] * once[p] - 0.5 * total
        for q in range(4):
            at = slice(q * 128, (q + 1) * 128)
            u0_ref[rows, at] = packed(start[4 + 2 * q], start[5 + 2 * q])
            u1_ref[rows, at] = packed(once[4 + 2 * q], once[5 + 2 * q])
            u2_ref[rows, at] = packed(twice[4 + 2 * q], twice[5 + 2 * q])
        return carry

    lax.fori_loop(0, ROWS // 8, filter_rows, 0)


def store_traces(ft, value, *refs):
    traces = dot3(split(ft), split(value))
    for slot in range(3):
        refs[slot][...] = traces[slot * FLAT : (slot + 1) * FLAT]
    at = place()
    for slot, flip in ((3, 4), (4, 2), (5, 1)):
        refs[3][at ^ flip] = traces[slot * FLAT : (slot + 1) * FLAT]


def basis_kernel(peaks_ref, u0_ref, u1_ref, u2_ref, own_ref, vectors_ref,
                 df_ref, ft_ref, scal_ref, x_ref, y_ref, z_ref, cube_ref, bt_ref):
    top = 6.0 + jnp.max(peaks_ref[...])
    centre = (top + cutoff) / 2.0
    half_width = (top - cutoff) / 2.0
    scal_ref[0] = centre
    scal_ref[1] = half_width
    moved = SHIFT - centre
    start = u0_ref[...]
    square = u2_ref[...] + (2.0 * moved) * u1_ref[...] + (moved * moved) * start
    restricted = square * (2.0 / (half_width * half_width)) - start
    halves = split(restricted)
    intersection = exact(restricted, restricted, (((1,), (1,)), ((), ())))
    sigma = jnp.sqrt(jnp.sum(intersection * intersection))
    identity = (
        lax.broadcasted_iota(jnp.int32, (ROWS, ROWS), 0) == lanes((ROWS, ROWS))
    ).astype(jnp.float32)
    current = intersection / sigma
    factor = 1.5 * identity - 0.5 * current
    current = exact(current, factor)
    root = factor
    for step in range(NEWTON - 1):
        factor = 1.5 * identity - 0.5 * exact(root, current)
        if step < NEWTON - 2:
            current = exact(current, factor)
        root = exact(factor, root)
    root = root / jnp.sqrt(sigma)
    basis = dot3(split(root), halves)

    own = own_ref[:1] + SHIFT
    cell = lanes((ROWS, WIDTH))
    z = cell % 8
    y = cell // 16 % 8
    x = cell // 128 * 2 + cell // 8 % 2
    odd = x % 2 == 1

    def gate(ok, value):
        return jnp.where(ok, value, 0.0)

    total = gate(z > 0, lane_roll(basis, 1)) + gate(z < 7, lane_roll(basis, -1))
    total = total + gate(y > 0, lane_roll(basis, 16)) + gate(y < 7, lane_roll(basis, -16))
    total = total + jnp.where(odd, lane_roll(basis, 8), lane_roll(basis, -8))
    total = total + gate(
        (x > 0) & (x < 7), jnp.where(odd, lane_roll(basis, -120), lane_roll(basis, 120))
    )
    applied = own * basis - 0.5 * total
    diagonal = dot3(split(basis), split(applied), (((1,), (1,)), ((), ())))

    bt_ref[...] = jnp.concatenate([basis, jnp.zeros((128 - ROWS, WIDTH), jnp.float32)], axis=0).T
    lower = (
        jnp.concatenate([bt_ref[yy * 16 : yy * 16 + 8] for yy in range(8)], axis=0),
        jnp.concatenate([bt_ref[q * 128 : q * 128 + 16] for q in range(4)], axis=0),
        bt_ref[pl.ds(0, FLAT, stride=8)],
    )
    upper = (
        jnp.concatenate([bt_ref[392 + yy * 16 : 400 + yy * 16] for yy in range(8)], axis=0),
        jnp.concatenate([bt_ref[q * 128 + 112 : q * 128 + 128] for q in range(4)], axis=0),
        bt_ref[pl.ds(7, FLAT, stride=8)],
    )
    bits = parities()
    pieces = [jnp.where(bit == 0, u, l) for bit, u, l in zip(bits, upper, lower)]
    pieces += [jnp.where(bit == 0, l, u) for bit, u, l in zip(bits, upper, lower)]
    faces_t = jnp.concatenate(pieces, axis=0)
    ft = faces_t[:, :ROWS]
    ft_ref[...] = ft
    df_ref[:, :BODY] = -0.5 * faces_t.T[:ROWS]
    df_ref[:, BODY : BODY + ROWS] = diagonal
    df_ref[:, BODY + ROWS :] = jnp.zeros((ROWS, WIDTH - BODY - ROWS), jnp.float32)
    store_traces(ft, vectors_ref[...], x_ref, y_ref, z_ref, cube_ref)


def step_kernel(first, last, scal_ref, df_ref, ft_ref, now_ref, prior_ref, x_ref, y_ref, z_ref,
                cube_ref, out_ref, *sent):
    now = now_ref[...]
    at = place()
    halos = [x_ref[...], y_ref[...], z_ref[...]]
    halos += [cube_ref[at ^ flip] for flip in (4, 2, 1)]
    stacked = jnp.concatenate(
        halos + [now, jnp.zeros((WIDTH - BODY - ROWS, COLS), jnp.float32)], axis=0
    )
    result = dot3(split(df_ref[...]), split(stacked))
    centre, half_width = scal_ref[0], scal_ref[1]
    following = (result - centre * now) / half_width
    if not first:
        following = 2.0 * following - prior_ref[...]
    out_ref[...] = following
    if not last:
        store_traces(ft_ref[...], following, *sent)


def vmem():
    return pl.BlockSpec(memory_space=pltpu.VMEM)


def smem():
    return pl.BlockSpec(memory_space=pltpu.SMEM)


def of(*shape):
    return jax.ShapeDtypeStruct(shape, jnp.float32)


def per_device(orbitals, potential, coefficients):
    f32 = jnp.float32
    nx = lax.axis_size("gx")
    plane = lax.axis_size("gy") * lax.axis_size("gz")
    spread = jnp.pad(potential, ((0, 0), (0, 0), (0, 8))).reshape(8, 128)
    near = lanes((8, 128)) % 16 < 8
    block = jnp.where(near, spread, jnp.max(potential))
    tiles = lax.all_to_all(jnp.broadcast_to(block, (plane, 8, 128)), ("gy", "gz"), 0, 0)
    peak, wide = pl.pallas_call(
        tiles_kernel,
        out_shape=(of(nx, 1, 128), of(8, 256)),
        in_specs=[vmem()],
        out_specs=(vmem(), vmem()),
        compiler_params=pltpu.CompilerParams(vmem_limit_bytes=GRANT),
        name="tiles",
    )(tiles)
    peaks = lax.all_to_all(peak, "gx", 0, 0)
    below = shifted(wide, "gx", 1)
    powers = pl.pallas_call(
        filter_kernel,
        out_shape=(of(ROWS, WIDTH), of(ROWS, WIDTH), of(ROWS, WIDTH), of(8, WIDTH)),
        in_specs=[vmem(), vmem(), vmem()],
        out_specs=(vmem(),) * 4,
        scratch_shapes=[pltpu.VMEM((10, 8, 256), f32)],
        compiler_params=pltpu.CompilerParams(vmem_limit_bytes=GRANT),
        name="powers",
    )(wide, below, orbitals.reshape(ROWS, -1))
    start = coefficients.reshape(ROWS, COLS)
    sent_shapes = (of(FLAT, COLS),) * 3 + (of(CUBE, FLAT, COLS),)
    df, ft, scal, *sent = pl.pallas_call(
        basis_kernel,
        out_shape=(of(ROWS, WIDTH), of(BODY, ROWS), of(2)) + sent_shapes,
        in_specs=[vmem()] * 6,
        out_specs=(vmem(), vmem(), smem()) + (vmem(),) * 4,
        scratch_shapes=[pltpu.VMEM((WIDTH, 128), f32)],
        compiler_params=pltpu.CompilerParams(vmem_limit_bytes=GRANT),
        name="basis",
    )(peaks, *powers, start)

    groups = cubes()
    prior, now = start, start
    for step in range(DG_STEPS):
        halos = [swapped(trace, axis) for trace, axis in zip(sent, AXES)]
        halos.append(lax.all_to_all(sent[3], AXES, 0, 0, axis_index_groups=groups))
        last = step == DG_STEPS - 1
        shapes = (of(ROWS, COLS),) + (() if last else sent_shapes)

        def body(*refs, step=step, last=last):
            step_kernel(step == 0, last, *refs)

        following, *sent = pl.pallas_call(
            body,
            out_shape=shapes,
            in_specs=[smem()] + [vmem()] * 8,
            out_specs=tuple(vmem() for _ in shapes),
            compiler_params=pltpu.CompilerParams(vmem_limit_bytes=GRANT),
            name=f"step{step}",
        )(scal, df, ft, now, prior, *halos)
        prior, now = now, following
    return now.reshape(coefficients.shape)


def solution(mesh):
    placed = (P("gx", "gy", "gz", None, None), P("gx", "gy", "gz"), P("gx", "gy", "gz", None, None))
    return jax.shard_map(
        per_device,
        mesh=mesh,
        in_specs=placed,
        out_specs=P("gx", "gy", "gz", None, None),
        check_vma=False,
    )
```

time: 163 us -> 138 us (0.85)
  starting transfers between devices: 88.7 us -> 69.7 us
  blocking collectives: 16.5 us -> 24.3 us
  local copies, waits for them, and re-layouts: 7.08 us -> 2.26 us
  waiting for transfers between devices: 27.5 us -> 23.6 us
  Pallas kernels: 17.8 us -> 15 us
    ppermute x19 -> x1, starting transfers between devices: 59.4 us -> 3.14 us  [shifted(): lax.ppermute(shard, axis, [(i, (i + by) % count) for i in range(count)])]
    ppermute x0 -> x9, starting transfers between devices: none -> 19.8 us  [swapped(): lax.ppermute(shard, axis, [(i, i ^ 1) for i in range(lax.axis_size(axis))])]
    all_to_all x1 -> x4, starting transfers between devices: 29.3 us -> 46.8 us  [the longest x3 26.9 us: per_device(): halos.append(lax.all_to_all(sent[3], AXES, 0, 0, axis_index_groups=groups))]
    ppermute x0 -> x9, waiting for transfers between devices: none -> 10.8 us  [swapped(): lax.ppermute(shard, axis, [(i, i ^ 1) for i in range(lax.axis_size(axis))])]
    ppermute x19 -> x1, waiting for transfers between devices: 13.1 us -> 2.75 us  [shifted(): lax.ppermute(shard, axis, [(i, (i + by) % count) for i in range(count)])]
    all_to_all x1, blocking collectives: 16.5 us -> 24.3 us  [per_device(): lax.all_to_all(jnp.broadcast_to(block, (plane, 8, 128)), ('gy', 'gz'), 0, 0)]
    all_to_all x1 -> x4, waiting for transfers between devices: 14.4 us -> 10.1 us  [the longest x1 10.1 us: per_device(): peaks = lax.all_to_all(peak, 'gx', 0, 0)]
    squeeze x3 -> x0, local copies, waits for them, and re-layouts: 3.08 us -> none  [per_device(): halos.append(shifted(traces[2 * at], axis, -1))]
  transfers between devices with their start and end apart: 20 -> 14, of which waited for: 8 -> 5; matrix products, arithmetic and copies ran while one was open for 1% -> 0% of each run, Pallas kernels for 0% -> 3%
where the time goes in v2:
time: 138 us; the launch traced here: 137 us
  starting transfers between devices  69.7 us (51%)
  blocking collectives  24.3 us (18%)
  waiting for transfers between devices  23.6 us (17%)
  Pallas kernels  15 us (11%)
  local copies, waits for them, and re-layouts  2.26 us (2%)
  other arithmetic  2.06 us (1%)
    all_to_all x3, starting transfers between devices, per_device(): halos.append(lax.all_to_all(sent[3], AXES, 0, 0, axis_index_groups=groups))  26.9 us
    all_to_all x1, blocking collectives, per_device(): lax.all_to_all(jnp.broadcast_to(block, (plane, 8, 128)), ('gy', 'gz'), 0, 0)  24.3 us
    all_to_all x1, starting transfers between devices, per_device(): peaks = lax.all_to_all(peak, 'gx', 0, 0)  19.9 us
    ppermute x9, starting transfers between devices, swapped(): lax.ppermute(shard, axis, [(i, i ^ 1) for i in range(lax.axis_size(axis))])  19.8 us
    ppermute x9, waiting for transfers between devices, swapped(): lax.ppermute(shard, axis, [(i, i ^ 1) for i in range(lax.axis_size(axis))])  10.8 us
    all_to_all x1, waiting for transfers between devices, per_device(): peaks = lax.all_to_all(peak, 'gx', 0, 0)  10.1 us
    pallas_call x3, Pallas kernels, per_device(): pl.pallas_call(body, out_shape=shapes, in_specs=[smem()] + [vmem()] * 8,...  5.57 us
    pallas_call x1, Pallas kernels, per_device(): pl.pallas_call(basis_kernel, out_shape=(of(ROWS, WIDTH), of(BODY, ROWS),...  4.92 us
  transfers between devices with their start and end apart: 14, of which 5 were waited for; matrix products, arithmetic and copies ran while one was open for 0% of the time, Pallas kernels for 3%

profile of v2, /device:TPU:1, one launch (start us, length us, event | category | flops | bytes accessed | tf_op | source)
XLA Modules:
  0.0 137.2 jit_solution(16049340783182597482)
XLA Ops:
  2.9 24.3 %all_to_all.25.tiles_ref = f32[32,8,128]{2,1,0:T(8,128)S(1)} all-to-all(f32[32,8,128]{2,1,0:T(8,128)S(1)} %broadcast_in_dim.8), channel_id=1, replica_groups=mesh['gx'=32,'gy'=4,'gz'=8] {'gy','gz'}, dimensions={0} | all-to-all | bytes 262144 | tf_op jit(solution)/shard_map/all_to_all | solution.py:264
  28.0 19.9 %all-to-all-start.1 = ((f32[32,1,128]{2,1,0:T(1,128)}), f32[32,1,128]{2,1,0:T(1,128)S(1)}, u32[]{:S(2)}, u32[]{:S(2)}) async-start(f32[32,1,128]{2,1,0:T(1,128)} %get-tuple-element.28), calls=%async_computation.1 | async-start | bytes 32768 | tf_op jit(solution)/shard_map/all_to_all | solution.py:273
  47.9 3.1 %collective-permute-start = (f32[8,256]{1,0:T(8,128)S(1)}, f32[8,256]{1,0:T(8,128)S(1)}, u32[]{:S(2)}, u32[]{:S(2)}) collective-permute-start(f32[8,256]{1,0:T(8,128)S(1)} %get-tuple-element.29.wide_ref), channel_id=1, source_target_pairs={{0,32},{32,64},{64,96},{96,128},{128,160},{160,192},{192,224},{224... | collective-permute-start | bytes 24584 | tf_op jit(solution)/shard_map/ppermute | solution.py:25
  51.1 2.8 %collective-permute-done.below_ref = f32[8,256]{1,0:T(8,128)S(1)} collective-permute-done((f32[8,256]{1,0:T(8,128)S(1)}, f32[8,256]{1,0:T(8,128)S(1)}, u32[]{:S(2)}, u32[]{:S(2)}) %collective-permute-start) | collective-permute-done | bytes 8224 | tf_op jit(solution)/shard_map/ppermute | solution.py:25
  55.2 3.8 %powers.1 = (f32[96,512]{1,0:T(8,128)S(1)}, f32[96,512]{1,0:T(8,128)S(1)}, f32[96,512]{1,0:T(8,128)S(1)}, f32[8,512]{1,0:T(8,128)S(1)}) custom-call(f32[8,256]{1,0:T(8,128)S(1)} %get-tuple-element.29.wide_ref, f32[8,256]{1,0:T(8,128)S(1)} %collective-permute-done.below_ref, f32[96,4096]{1,0:T(8,128)S(1)} %bitcast.3), custom_call_target="tpu_custom_call" | custom-call | tf_op jit(solution)/shard_map/powers/pallas_call | solution.py:275
  59.1 10.1 %all-to-all-done.1.peaks_ref = f32[32,1,128]{2,1,0:T(1,128)S(1)} async-done(((f32[32,1,128]{2,1,0:T(1,128)}), f32[32,1,128]{2,1,0:T(1,128)S(1)}, u32[]{:S(2)}, u32[]{:S(2)}) %all-to-all-start.1) | async-done | bytes 16416 | tf_op jit(solution)/shard_map/all_to_all | solution.py:273
  69.1 4.9 %basis.1 = (f32[96,512]{1,0:T(8,128)S(1)}, f32[384,96]{1,0:T(8,128)S(1)}, f32[2]{0:T(128)S(1)}, f32[64,256]{1,0:T(8,128)S(1)}, f32[64,256]{1,0:T(8,128)S(1)}, /*...) custom-call(f32[32,1,128]{2,1,0:T(1,128)S(1)} %all-to-all-done.1.peaks_ref, f32[96,512]{1,0:T(8,128)S(1)} %get-tuple-element.30.u0_ref, ...), custom_call_target="tpu_custom_call" | custom-call | tf_op jit(solution)/shard_map/basis/pallas_call | solution.py:286
  74.1 9.9 %all-to-all-start.2 = ((f32[8,64,256]{2,1,0:T(8,128)}), f32[8,64,256]{2,1,0:T(8,128)S(1)}, u32[]{:S(2)}, u32[]{:S(2)}) async-start(f32[8,64,256]{2,1,0:T(8,128)} %get-tuple-element.40), calls=%async_computation.2 | async-start | bytes 1048576 | tf_op jit(solution)/shard_map/all_to_all | solution.py:300
  84.0 1.9 %collective-permute-start.1 = (f32[64,256]{1,0:T(8,128)S(1)}, f32[64,256]{1,0:T(8,128)S(1)}, u32[]{:S(2)}, u32[]{:S(2)}) collective-permute-start(f32[64,256]{1,0:T(8,128)S(1)} %get-tuple-element.37), channel_id=1, source_target_pairs={{0,32},{32,0},{64,96},{96,64},{128,160},{160,128},{192,224},{224,1... | collective-permute-start | bytes 196616 | tf_op jit(solution)/shard_map/ppermute | solution.py:88
  85.9 2.8 %collective-permute-start.2 = (f32[64,256]{1,0:T(8,128)S(1)}, f32[64,256]{1,0:T(8,128)S(1)}, u32[]{:S(2)}, u32[]{:S(2)}) collective-permute-start(f32[64,256]{1,0:T(8,128)S(1)} %get-tuple-element.38), channel_id=1, source_target_pairs={{0,8},{8,0},{16,24},{24,16},{1,9},{9,1},{17,25},{25,17},{2,10},{10... | collective-permute-start | bytes 196616 | tf_op jit(solution)/shard_map/ppermute | solution.py:88
  88.7 1.9 %collective-permute-start.3 = (f32[64,256]{1,0:T(8,128)S(1)}, f32[64,256]{1,0:T(8,128)S(1)}, u32[]{:S(2)}, u32[]{:S(2)}) collective-permute-start(f32[64,256]{1,0:T(8,128)S(1)} %get-tuple-element.39), channel_id=1, source_target_pairs={{0,1},{1,0},{2,3},{3,2},{4,5},{5,4},{6,7},{7,6},{8,9},{9,8},{10,11... | collective-permute-start | bytes 196616 | tf_op jit(solution)/shard_map/ppermute | solution.py:88
  90.7 3.6 %collective-permute-done.3.refs_7_ = f32[64,256]{1,0:T(8,128)S(1)} collective-permute-done((f32[64,256]{1,0:T(8,128)S(1)}, f32[64,256]{1,0:T(8,128)S(1)}, u32[]{:S(2)}, u32[]{:S(2)}) %collective-permute-start.3) | collective-permute-done | bytes 65568 | tf_op jit(solution)/shard_map/ppermute | solution.py:88
  94.2 2.1 %step0.1 = (f32[96,256]{1,0:T(8,128)S(1)}, f32[64,256]{1,0:T(8,128)S(1)}, f32[64,256]{1,0:T(8,128)S(1)}, f32[64,256]{1,0:T(8,128)S(1)}, f32[8,64,256]{2,1,0:T(8,128)}) custom-call(f32[2]{0:T(128)S(1)} %get-tuple-element.34.refs_0_, f32[96,512]{1,0:T(8,128)S(1)} %get-tuple-element.35.refs_1_, f32[384,96]{1,0:T(8,128)S(1)} %get-tuple-element.36.refs_2_, ...), custom_call_target="tpu_custom_call" | custom-call | tf_op jit(solution)/shard_map/step0/pallas_call | solution.py:307
  96.3 8.5 %all-to-all-start.3 = ((f32[8,64,256]{2,1,0:T(8,128)}), f32[8,64,256]{2,1,0:T(8,128)S(1)}, u32[]{:S(2)}, u32[]{:S(2)}) async-start(f32[8,64,256]{2,1,0:T(8,128)} %get-tuple-element.45), calls=%async_computation.3 | async-start | bytes 1048576 | tf_op jit(solution)/shard_map/all_to_all | solution.py:300
  104.8 1.9 %collective-permute-start.4 = (f32[64,256]{1,0:T(8,128)S(1)}, f32[64,256]{1,0:T(8,128)S(1)}, u32[]{:S(2)}, u32[]{:S(2)}) collective-permute-start(f32[64,256]{1,0:T(8,128)S(1)} %get-tuple-element.42), channel_id=1, source_target_pairs={{0,32},{32,0},{64,96},{96,64},{128,160},{160,128},{192,224},{224,1... | collective-permute-start | bytes 196616 | tf_op jit(solution)/shard_map/ppermute | solution.py:88
  106.7 2.7 %collective-permute-start.5 = (f32[64,256]{1,0:T(8,128)S(1)}, f32[64,256]{1,0:T(8,128)S(1)}, u32[]{:S(2)}, u32[]{:S(2)}) collective-permute-start(f32[64,256]{1,0:T(8,128)S(1)} %get-tuple-element.43), channel_id=1, source_target_pairs={{0,8},{8,0},{16,24},{24,16},{1,9},{9,1},{17,25},{25,17},{2,10},{10... | collective-permute-start | bytes 196616 | tf_op jit(solution)/shard_map/ppermute | solution.py:88
  109.5 1.9 %collective-permute-start.6 = (f32[64,256]{1,0:T(8,128)S(1)}, f32[64,256]{1,0:T(8,128)S(1)}, u32[]{:S(2)}, u32[]{:S(2)}) collective-permute-start(f32[64,256]{1,0:T(8,128)S(1)} %get-tuple-element.44), channel_id=1, source_target_pairs={{0,1},{1,0},{2,3},{3,2},{4,5},{5,4},{6,7},{7,6},{8,9},{9,8},{10,11... | collective-permute-start | bytes 196616 | tf_op jit(solution)/shard_map/ppermute | solution.py:88
  111.4 3.6 %collective-permute-done.6.refs_7_ = f32[64,256]{1,0:T(8,128)S(1)} collective-permute-done((f32[64,256]{1,0:T(8,128)S(1)}, f32[64,256]{1,0:T(8,128)S(1)}, u32[]{:S(2)}, u32[]{:S(2)}) %collective-permute-start.6) | collective-permute-done | bytes 65568 | tf_op jit(solution)/shard_map/ppermute | solution.py:88
  115.0 2.1 %step1.1 = (f32[96,256]{1,0:T(8,128)S(1)}, f32[64,256]{1,0:T(8,128)S(1)}, f32[64,256]{1,0:T(8,128)S(1)}, f32[64,256]{1,0:T(8,128)S(1)}, f32[8,64,256]{2,1,0:T(8,128)}) custom-call(f32[2]{0:T(128)S(1)} %get-tuple-element.34.refs_0_, f32[96,512]{1,0:T(8,128)S(1)} %get-tuple-element.35.refs_1_, f32[384,96]{1,0:T(8,128)S(1)} %get-tuple-element.36.refs_2_, ...), custom_call_target="tpu_custom_call" | custom-call | tf_op jit(solution)/shard_map/step1/pallas_call | solution.py:307
  117.0 8.5 %all-to-all-start.4 = ((f32[8,64,256]{2,1,0:T(8,128)}), f32[8,64,256]{2,1,0:T(8,128)S(1)}, u32[]{:S(2)}, u32[]{:S(2)}) async-start(f32[8,64,256]{2,1,0:T(8,128)} %get-tuple-element.50), calls=%async_computation.4 | async-start | bytes 1048576 | tf_op jit(solution)/shard_map/all_to_all | solution.py:300
  125.5 1.9 %collective-permute-start.7 = (f32[64,256]{1,0:T(8,128)S(1)}, f32[64,256]{1,0:T(8,128)S(1)}, u32[]{:S(2)}, u32[]{:S(2)}) collective-permute-start(f32[64,256]{1,0:T(8,128)S(1)} %get-tuple-element.47), channel_id=1, source_target_pairs={{0,32},{32,0},{64,96},{96,64},{128,160},{160,128},{192,224},{224,1... | collective-permute-start | bytes 196616 | tf_op jit(solution)/shard_map/ppermute | solution.py:88
  127.5 2.7 %collective-permute-start.8 = (f32[64,256]{1,0:T(8,128)S(1)}, f32[64,256]{1,0:T(8,128)S(1)}, u32[]{:S(2)}, u32[]{:S(2)}) collective-permute-start(f32[64,256]{1,0:T(8,128)S(1)} %get-tuple-element.48), channel_id=1, source_target_pairs={{0,8},{8,0},{16,24},{24,16},{1,9},{9,1},{17,25},{25,17},{2,10},{10... | collective-permute-start | bytes 196616 | tf_op jit(solution)/shard_map/ppermute | solution.py:88
  130.2 1.9 %collective-permute-start.9 = (f32[64,256]{1,0:T(8,128)S(1)}, f32[64,256]{1,0:T(8,128)S(1)}, u32[]{:S(2)}, u32[]{:S(2)}) collective-permute-start(f32[64,256]{1,0:T(8,128)S(1)} %get-tuple-element.49), channel_id=1, source_target_pairs={{0,1},{1,0},{2,3},{3,2},{4,5},{5,4},{6,7},{7,6},{8,9},{9,8},{10,11... | collective-permute-start | bytes 196616 | tf_op jit(solution)/shard_map/ppermute | solution.py:88
  132.2 3.6 %collective-permute-done.9.refs_7_ = f32[64,256]{1,0:T(8,128)S(1)} collective-permute-done((f32[64,256]{1,0:T(8,128)S(1)}, f32[64,256]{1,0:T(8,128)S(1)}, u32[]{:S(2)}, u32[]{:S(2)}) %collective-permute-start.9) | collective-permute-done | bytes 65568 | tf_op jit(solution)/shard_map/ppermute | solution.py:88
  (22 shorter events, 6.5 us)
Async XLA Ops:
  0.0 69.1 %copy-start.1 = (f32[1,1,1,96,256]{4,3,2,1,0:T(8,128)S(1)}, f32[1,1,1,96,256]{4,3,2,1,0:T(8,128)}, u32[]{:S(2)}) copy-start(f32[1,1,1,96,256]{4,3,2,1,0:T(8,128)} %param.5) | copy-start | bytes 294916
  28.0 41.1 %all-to-all-start.1 = ((f32[32,1,128]{2,1,0:T(1,128)}), f32[32,1,128]{2,1,0:T(1,128)S(1)}, u32[]{:S(2)}, u32[]{:S(2)}) async-start(f32[32,1,128]{2,1,0:T(1,128)} %get-tuple-element.28), calls=%async_computation.1 | async-start | bytes 32768 | tf_op jit(solution)/shard_map/all_to_all | solution.py:273
  47.9 5.9 %collective-permute-start = (f32[8,256]{1,0:T(8,128)S(1)}, f32[8,256]{1,0:T(8,128)S(1)}, u32[]{:S(2)}, u32[]{:S(2)}) collective-permute-start(f32[8,256]{1,0:T(8,128)S(1)} %get-tuple-element.29.wide_ref), channel_id=1, source_target_pairs={{0,32},{32,64},{64,96},{96,128},{128,160},{160,192},{192,224},{224... | collective-permute-start | bytes 24584 | tf_op jit(solution)/shard_map/ppermute | solution.py:25
  53.8 1.4 %copy-start = (f32[1,1,1,96,4096]{4,3,2,1,0:T(8,128)S(1)}, f32[1,1,1,96,4096]{4,3,2,1,0:T(8,128)}, u32[]{:S(2)}) copy-start(f32[1,1,1,96,4096]{4,3,2,1,0:T(8,128)} %param.3) | copy-start | bytes 4718596
  74.1 20.2 %all-to-all-start.2 = ((f32[8,64,256]{2,1,0:T(8,128)}), f32[8,64,256]{2,1,0:T(8,128)S(1)}, u32[]{:S(2)}, u32[]{:S(2)}) async-start(f32[8,64,256]{2,1,0:T(8,128)} %get-tuple-element.40), calls=%async_computation.2 | async-start | bytes 1048576 | tf_op jit(solution)/shard_map/all_to_all | solution.py:300
  84.0 6.7 %collective-permute-start.1 = (f32[64,256]{1,0:T(8,128)S(1)}, f32[64,256]{1,0:T(8,128)S(1)}, u32[]{:S(2)}, u32[]{:S(2)}) collective-permute-start(f32[64,256]{1,0:T(8,128)S(1)} %get-tuple-element.37), channel_id=1, source_target_pairs={{0,32},{32,0},{64,96},{96,64},{128,160},{160,128},{192,224},{224,1... | collective-permute-start | bytes 196616 | tf_op jit(solution)/shard_map/ppermute | solution.py:88
  85.9 4.8 %collective-permute-start.2 = (f32[64,256]{1,0:T(8,128)S(1)}, f32[64,256]{1,0:T(8,128)S(1)}, u32[]{:S(2)}, u32[]{:S(2)}) collective-permute-start(f32[64,256]{1,0:T(8,128)S(1)} %get-tuple-element.38), channel_id=1, source_target_pairs={{0,8},{8,0},{16,24},{24,16},{1,9},{9,1},{17,25},{25,17},{2,10},{10... | collective-permute-start | bytes 196616 | tf_op jit(solution)/shard_map/ppermute | solution.py:88
  88.7 5.5 %collective-permute-start.3 = (f32[64,256]{1,0:T(8,128)S(1)}, f32[64,256]{1,0:T(8,128)S(1)}, u32[]{:S(2)}, u32[]{:S(2)}) collective-permute-start(f32[64,256]{1,0:T(8,128)S(1)} %get-tuple-element.39), channel_id=1, source_target_pairs={{0,1},{1,0},{2,3},{3,2},{4,5},{5,4},{6,7},{7,6},{8,9},{9,8},{10,11... | collective-permute-start | bytes 196616 | tf_op jit(solution)/shard_map/ppermute | solution.py:88
  96.3 18.7 %all-to-all-start.3 = ((f32[8,64,256]{2,1,0:T(8,128)}), f32[8,64,256]{2,1,0:T(8,128)S(1)}, u32[]{:S(2)}, u32[]{:S(2)}) async-start(f32[8,64,256]{2,1,0:T(8,128)} %get-tuple-element.45), calls=%async_computation.3 | async-start | bytes 1048576 | tf_op jit(solution)/shard_map/all_to_all | solution.py:300
  104.8 6.6 %collective-permute-start.4 = (f32[64,256]{1,0:T(8,128)S(1)}, f32[64,256]{1,0:T(8,128)S(1)}, u32[]{:S(2)}, u32[]{:S(2)}) collective-permute-start(f32[64,256]{1,0:T(8,128)S(1)} %get-tuple-element.42), channel_id=1, source_target_pairs={{0,32},{32,0},{64,96},{96,64},{128,160},{160,128},{192,224},{224,1... | collective-permute-start | bytes 196616 | tf_op jit(solution)/shard_map/ppermute | solution.py:88
  106.7 4.7 %collective-permute-start.5 = (f32[64,256]{1,0:T(8,128)S(1)}, f32[64,256]{1,0:T(8,128)S(1)}, u32[]{:S(2)}, u32[]{:S(2)}) collective-permute-start(f32[64,256]{1,0:T(8,128)S(1)} %get-tuple-element.43), channel_id=1, source_target_pairs={{0,8},{8,0},{16,24},{24,16},{1,9},{9,1},{17,25},{25,17},{2,10},{10... | collective-permute-start | bytes 196616 | tf_op jit(solution)/shard_map/ppermute | solution.py:88
  109.5 5.5 %collective-permute-start.6 = (f32[64,256]{1,0:T(8,128)S(1)}, f32[64,256]{1,0:T(8,128)S(1)}, u32[]{:S(2)}, u32[]{:S(2)}) collective-permute-start(f32[64,256]{1,0:T(8,128)S(1)} %get-tuple-element.44), channel_id=1, source_target_pairs={{0,1},{1,0},{2,3},{3,2},{4,5},{5,4},{6,7},{7,6},{8,9},{9,8},{10,11... | collective-permute-start | bytes 196616 | tf_op jit(solution)/shard_map/ppermute | solution.py:88
  117.0 18.7 %all-to-all-start.4 = ((f32[8,64,256]{2,1,0:T(8,128)}), f32[8,64,256]{2,1,0:T(8,128)S(1)}, u32[]{:S(2)}, u32[]{:S(2)}) async-start(f32[8,64,256]{2,1,0:T(8,128)} %get-tuple-element.50), calls=%async_computation.4 | async-start | bytes 1048576 | tf_op jit(solution)/shard_map/all_to_all | solution.py:300
  125.5 6.6 %collective-permute-start.7 = (f32[64,256]{1,0:T(8,128)S(1)}, f32[64,256]{1,0:T(8,128)S(1)}, u32[]{:S(2)}, u32[]{:S(2)}) collective-permute-start(f32[64,256]{1,0:T(8,128)S(1)} %get-tuple-element.47), channel_id=1, source_target_pairs={{0,32},{32,0},{64,96},{96,64},{128,160},{160,128},{192,224},{224,1... | collective-permute-start | bytes 196616 | tf_op jit(solution)/shard_map/ppermute | solution.py:88
  127.5 4.7 %collective-permute-start.8 = (f32[64,256]{1,0:T(8,128)S(1)}, f32[64,256]{1,0:T(8,128)S(1)}, u32[]{:S(2)}, u32[]{:S(2)}) collective-permute-start(f32[64,256]{1,0:T(8,128)S(1)} %get-tuple-element.48), channel_id=1, source_target_pairs={{0,8},{8,0},{16,24},{24,16},{1,9},{9,1},{17,25},{25,17},{2,10},{10... | collective-permute-start | bytes 196616 | tf_op jit(solution)/shard_map/ppermute | solution.py:88
  130.2 5.5 %collective-permute-start.9 = (f32[64,256]{1,0:T(8,128)S(1)}, f32[64,256]{1,0:T(8,128)S(1)}, u32[]{:S(2)}, u32[]{:S(2)}) collective-permute-start(f32[64,256]{1,0:T(8,128)S(1)} %get-tuple-element.49), channel_id=1, source_target_pairs={{0,1},{1,0},{2,3},{3,2},{4,5},{5,4},{6,7},{7,6},{8,9},{9,8},{10,11... | collective-permute-start | bytes 196616 | tf_op jit(solution)/shard_map/ppermute | solution.py:88

commit v3 on v2

--- a/solution.py
+++ b/solution.py
@@ -13,7 +13,7 @@
 FLAT = EDGE * EDGE
 COLS = 256
 FACES = 6
-CUBE = 8
+RING = 4
 GRANT = 16 << 20
 BODY = FACES * FLAT
 WIDTH = 512
@@ -55,37 +55,43 @@
     return lax.broadcasted_iota(jnp.int32, shape, len(shape) - 1)
 
 
+SWAPS = (("gz", 0), ("gx", 0), ("gy", 1), ("gy", 0))
+SLOTS = SWAPS + (("gx", 1), ("gz", 1))
 AXES = ("gx", "gy", "gz")
 
 
-def parities():
-    return [lax.rem(lax.axis_index(axis), 2) for axis in AXES]
+def upper_side(axis, odd):
+    return lax.rem(lax.axis_index(axis), 2) == odd
+
+
+def swapped(shard, axis, odd):
+    count = lax.axis_size(axis)
+    pairs = [((2 * i + odd) % count, (2 * i + 1 + odd) % count) for i in range(count // 2)]
+    return lax.ppermute(shard, axis, pairs + [(b, a) for a, b in pairs])
 
 
 def place():
-    a, b, c = parities()
-    return CUBE - 1 - (a * 4 + b * 2 + c)
-
-
-def cubes():
-    sizes = [lax.axis_size(axis) for axis in AXES]
-    groups = []
-    for i in range(sizes[0] // 2):
-        for j in range(sizes[1] // 2):
-            for k in range(sizes[2] // 2):
-                group = []
-                for spot in range(CUBE):
-                    at = [
-                        (2 * base + 1 + (spot >> (2 - axis) & 1)) % sizes[axis]
-                        for axis, base in enumerate((i, j, k))
-                    ]
-                    group.append((at[0] * sizes[1] + at[1]) * sizes[2] + at[2])
-                groups.append(group)
-    return groups
-
-
-def swapped(shard, axis):
-    return lax.ppermute(shard, axis, [(i, i ^ 1) for i in range(lax.axis_size(axis))])
+    return (1 - lax.rem(lax.axis_index("gx"), 2)) * 2 + 1 - lax.rem(lax.axis_index("gz"), 2)
+
+
+def rings():
+    nx, nz = lax.axis_size("gx"), lax.axis_size("gz")
+    return [
+        [(2 * i + 1 + a) % nx * nz + (2 * k + 1 + c) % nz for a in range(2) for c in range(2)]
+        for i in range(nx // 2)
+        for k in range(nz // 2)
+    ]
+
+
+def tile_kernel(potential_ref, out_ref):
+    lane = lanes((8, 128))
+    tile = jnp.full((8, 128), jnp.max(potential_ref[...]))
+    for y in range(8):
+        row = jnp.concatenate([potential_ref[:, y, :], jnp.zeros((8, 120), jnp.float32)], axis=1)
+        if y:
+            row = lane_roll(row, 16 * y)
+        tile = jnp.where((lane >= 16 * y) & (lane < 16 * y + 8), row, tile)
+    out_ref[...] = jnp.broadcast_to(tile, out_ref.shape)
 
 
 def tiles_kernel(tiles_ref, peak_ref, wide_ref):
@@ -103,7 +109,14 @@
         wide_ref[:, half * 128 : (half + 1) * 128] = jnp.where(near, low, lane_roll(high, 8))
 
 
-def filter_kernel(wide_ref, below_ref, orbitals_ref, u0_ref, u1_ref, u2_ref, own_ref, w_ref):
+def filter_kernel(wide_ref, below_ref, orbitals_ref, u0_ref, u1_ref, u2_ref, own_ref, w_ref,
+                  held_ref, sems):
+    def fetch(step):
+        rows = pl.ds(pl.multiple_of(step * 8, 8), 8)
+        return pltpu.make_async_copy(orbitals_ref.at[rows], held_ref.at[step], sems.at[step])
+
+    for step in range(ROWS // 8):
+        fetch(step).start()
     first_half = lanes((8, 128)) % 16 < 8
 
     def packed(even, odd):
@@ -124,7 +137,8 @@
 
     def filter_rows(step, carry):
         rows = pl.ds(pl.multiple_of(step * 8, 8), 8)
-        start = {p: orbitals_ref[rows, p * 256 : (p + 1) * 256] for p in range(2, 14)}
+        fetch(step).wait()
+        start = {p: held_ref[step, :, p * 256 : (p + 1) * 256] for p in range(2, 14)}
         once = {}
         for p in range(3, 13):
             total = around(start[p]) + (start[p - 1] + start[p + 1])
@@ -145,15 +159,16 @@
 
 def store_traces(ft, value, *refs):
     traces = dot3(split(ft), split(value))
-    for slot in range(3):
+    for slot in range(4):
         refs[slot][...] = traces[slot * FLAT : (slot + 1) * FLAT]
     at = place()
-    for slot, flip in ((3, 4), (4, 2), (5, 1)):
-        refs[3][at ^ flip] = traces[slot * FLAT : (slot + 1) * FLAT]
+    for slot, flip in ((4, 2), (5, 1)):
+        refs[4][at ^ flip] = traces[slot * FLAT : (slot + 1) * FLAT]
 
 
 def basis_kernel(peaks_ref, u0_ref, u1_ref, u2_ref, own_ref, vectors_ref,
-                 df_ref, ft_ref, scal_ref, x_ref, y_ref, z_ref, cube_ref, bt_ref):
+                 df_ref, ft_ref, scal_ref, *refs):
+    sent, bt_ref = refs[:-1], refs[-1]
     top = 6.0 + jnp.max(peaks_ref[...])
     centre = (top + cutoff) / 2.0
     half_width = (top - cutoff) / 2.0
@@ -211,24 +226,24 @@
         jnp.concatenate([bt_ref[q * 128 + 112 : q * 128 + 128] for q in range(4)], axis=0),
         bt_ref[pl.ds(7, FLAT, stride=8)],
     )
-    bits = parities()
-    pieces = [jnp.where(bit == 0, u, l) for bit, u, l in zip(bits, upper, lower)]
-    pieces += [jnp.where(bit == 0, l, u) for bit, u, l in zip(bits, upper, lower)]
+    pieces = [
+        jnp.where(upper_side(axis, odd), upper[AXES.index(axis)], lower[AXES.index(axis)])
+        for axis, odd in SLOTS
+    ]
     faces_t = jnp.concatenate(pieces, axis=0)
     ft = faces_t[:, :ROWS]
     ft_ref[...] = ft
     df_ref[:, :BODY] = -0.5 * faces_t.T[:ROWS]
     df_ref[:, BODY : BODY + ROWS] = diagonal
     df_ref[:, BODY + ROWS :] = jnp.zeros((ROWS, WIDTH - BODY - ROWS), jnp.float32)
-    store_traces(ft, vectors_ref[...], x_ref, y_ref, z_ref, cube_ref)
-
-
-def step_kernel(first, last, scal_ref, df_ref, ft_ref, now_ref, prior_ref, x_ref, y_ref, z_ref,
-                cube_ref, out_ref, *sent):
+    store_traces(ft, vectors_ref[...], *sent)
+
+
+def step_kernel(first, last, scal_ref, df_ref, ft_ref, now_ref, prior_ref, *refs):
+    swap_refs, ring_ref, out_ref, sent = refs[:4], refs[4], refs[5], refs[6:]
     now = now_ref[...]
     at = place()
-    halos = [x_ref[...], y_ref[...], z_ref[...]]
-    halos += [cube_ref[at ^ flip] for flip in (4, 2, 1)]
+    halos = [ref[...] for ref in swap_refs] + [ring_ref[at ^ 2], ring_ref[at ^ 1]]
     stacked = jnp.concatenate(
         halos + [now, jnp.zeros((WIDTH - BODY - ROWS, COLS), jnp.float32)], axis=0
     )
@@ -258,10 +273,15 @@
     f32 = jnp.float32
     nx = lax.axis_size("gx")
     plane = lax.axis_size("gy") * lax.axis_size("gz")
-    spread = jnp.pad(potential, ((0, 0), (0, 0), (0, 8))).reshape(8, 128)
-    near = lanes((8, 128)) % 16 < 8
-    block = jnp.where(near, spread, jnp.max(potential))
-    tiles = lax.all_to_all(jnp.broadcast_to(block, (plane, 8, 128)), ("gy", "gz"), 0, 0)
+    tile = pl.pallas_call(
+        tile_kernel,
+        out_shape=of(plane, 8, 128),
+        in_specs=[vmem()],
+        out_specs=vmem(),
+        compiler_params=pltpu.CompilerParams(vmem_limit_bytes=GRANT),
+        name="tile",
+    )(potential)
+    tiles = lax.all_to_all(tile, ("gy", "gz"), 0, 0)
     peak, wide = pl.pallas_call(
         tiles_kernel,
         out_shape=(of(nx, 1, 128), of(8, 256)),
@@ -275,29 +295,33 @@
     powers = pl.pallas_call(
         filter_kernel,
         out_shape=(of(ROWS, WIDTH), of(ROWS, WIDTH), of(ROWS, WIDTH), of(8, WIDTH)),
-        in_specs=[vmem(), vmem(), vmem()],
+        in_specs=[vmem(), vmem(), pl.BlockSpec(memory_space=pltpu.HBM)],
         out_specs=(vmem(),) * 4,
-        scratch_shapes=[pltpu.VMEM((10, 8, 256), f32)],
+        scratch_shapes=[
+            pltpu.VMEM((10, 8, 256), f32),
+            pltpu.VMEM((ROWS // 8, 8, 4096), f32),
+            pltpu.SemaphoreType.DMA((ROWS // 8,)),
+        ],
         compiler_params=pltpu.CompilerParams(vmem_limit_bytes=GRANT),
         name="powers",
     )(wide, below, orbitals.reshape(ROWS, -1))
     start = coefficients.reshape(ROWS, COLS)
-    sent_shapes = (of(FLAT, COLS),) * 3 + (of(CUBE, FLAT, COLS),)
+    sent_shapes = (of(FLAT, COLS),) * 4 + (of(RING, FLAT, COLS),)
     df, ft, scal, *sent = pl.pallas_call(
         basis_kernel,
         out_shape=(of(ROWS, WIDTH), of(BODY, ROWS), of(2)) + sent_shapes,
         in_specs=[vmem()] * 6,
-        out_specs=(vmem(), vmem(), smem()) + (vmem(),) * 4,
+        out_specs=(vmem(), vmem(), smem()) + (vmem(),) * 5,
         scratch_shapes=[pltpu.VMEM((WIDTH, 128), f32)],
         compiler_params=pltpu.CompilerParams(vmem_limit_bytes=GRANT),
         name="basis",
     )(peaks, *powers, start)
 
-    groups = cubes()
+    groups = rings()
     prior, now = start, start
     for step in range(DG_STEPS):
-        halos = [swapped(trace, axis) for trace, axis in zip(sent, AXES)]
-        halos.append(lax.all_to_all(sent[3], AXES, 0, 0, axis_index_groups=groups))
+        halos = [swapped(trace, *pairing) for trace, pairing in zip(sent, SWAPS)]
+        halos.append(lax.all_to_all(sent[4], ("gx", "gz"), 0, 0, axis_index_groups=groups))
         last = step == DG_STEPS - 1
         shapes = (of(ROWS, COLS),) + (() if last else sent_shapes)
 
@@ -307,7 +331,7 @@
         following, *sent = pl.pallas_call(
             body,
             out_shape=shapes,
-            in_specs=[smem()] + [vmem()] * 8,
+            in_specs=[smem()] + [vmem()] * 9,
             out_specs=tuple(vmem() for _ in shapes),
             compiler_params=pltpu.CompilerParams(vmem_limit_bytes=GRANT),
             name=f"step{step}",

time: 138 us -> 137 us (level)
  waiting for transfers between devices: 23.6 us -> 14.3 us
  starting transfers between devices: 69.7 us -> 78 us
  Pallas kernels: 15 us -> 17.1 us
  other arithmetic: 2.06 us -> 0 us
    ppermute x9 -> x12, starting transfers between devices: 19.8 us -> 29.6 us  [swapped(): return lax.ppermute(shard, axis, pairs + [(b, a) for a, b in pairs])]
    ppermute x9 -> x12, waiting for transfers between devices: 10.8 us -> 3.6 us  [swapped(): return lax.ppermute(shard, axis, pairs + [(b, a) for a, b in pairs])]
    all_to_all x1, waiting for transfers between devices: 10.1 us -> 7.95 us  [per_device(): peaks = lax.all_to_all(peak, 'gx', 0, 0)]
    pallas_call x1, Pallas kernels: 3.82 us -> 5.95 us  [per_device(): pl.pallas_call(filter_kernel, out_shape=(of(ROWS, WIDTH), of(ROWS, WIDTH)...]
    all_to_all x3, starting transfers between devices: 26.9 us -> 25.4 us  [per_device(): lax.all_to_all(sent[4], ('gx', 'gz'), 0, 0, axis_index_groups=groups)]
    reduce_max x1 -> x0, other arithmetic: 1.41 us -> none  [per_device(): block = jnp.where(near, spread, jnp.max(potential))]
    pallas_call x3 -> x4, Pallas kernels: 5.57 us -> 5.52 us  [the longest x3 5.39 us: per_device(): pl.pallas_call(body, out_shape=shapes, in_specs=[smem()] + [vmem()] * 9,...]
  transfers between devices with their start and end apart: 14 -> 17, of which waited for: 5 -> 7; matrix products, arithmetic and copies ran while one was open for 0% -> 0% of each run, Pallas kernels for 3% -> 4%
where the time goes in v3:
time: 137 us; the launch traced here: 136 us
  starting transfers between devices  78 us (57%)
  blocking collectives  24.3 us (18%)
  Pallas kernels  17.1 us (12%)
  waiting for transfers between devices  14.3 us (10%)
  local copies, waits for them, and re-layouts  2.17 us (2%)
    ppermute x12, starting transfers between devices, swapped(): return lax.ppermute(shard, axis, pairs + [(b, a) for a, b in pairs])  29.6 us
    all_to_all x3, starting transfers between devices, per_device(): lax.all_to_all(sent[4], ('gx', 'gz'), 0, 0, axis_index_groups=groups)  25.4 us
    all_to_all x1, blocking collectives, per_device(): tiles = lax.all_to_all(tile, ('gy', 'gz'), 0, 0)  24.3 us
    all_to_all x1, starting transfers between devices, per_device(): peaks = lax.all_to_all(peak, 'gx', 0, 0)  19.9 us
    all_to_all x1, waiting for transfers between devices, per_device(): peaks = lax.all_to_all(peak, 'gx', 0, 0)  7.95 us
    pallas_call x1, Pallas kernels, per_device(): pl.pallas_call(filter_kernel, out_shape=(of(ROWS, WIDTH), of(ROWS, WIDTH)...  5.95 us
    pallas_call x3, Pallas kernels, per_device(): pl.pallas_call(body, out_shape=shapes, in_specs=[smem()] + [vmem()] * 9,...  5.39 us
    pallas_call x1, Pallas kernels, per_device(): pl.pallas_call(basis_kernel, out_shape=(of(ROWS, WIDTH), of(BODY, ROWS),...  4.88 us
  transfers between devices with their start and end apart: 17, of which 7 were waited for; matrix products, arithmetic and copies ran while one was open for 0% of the time, Pallas kernels for 4%

profile of v3, /device:TPU:1, one launch (start us, length us, event | category | flops | bytes accessed | tf_op | source)
XLA Modules:
  0.0 136.2 jit_solution(4817401450019448986)
XLA Ops:
  0.9 24.3 %all_to_all.25.tiles_ref = f32[32,8,128]{2,1,0:T(8,128)S(1)} all-to-all(f32[32,8,128]{2,1,0:T(8,128)S(1)} %tile.1), channel_id=1, replica_groups=mesh['gx'=32,'gy'=4,'gz'=8] {'gy','gz'}, dimensions={0} | all-to-all | bytes 262144 | tf_op jit(solution)/shard_map/all_to_all | solution.py:284
  26.0 19.9 %all-to-all-start.1 = ((f32[32,1,128]{2,1,0:T(1,128)}), f32[32,1,128]{2,1,0:T(1,128)S(1)}, u32[]{:S(2)}, u32[]{:S(2)}) async-start(f32[32,1,128]{2,1,0:T(1,128)} %get-tuple-element.31), calls=%async_computation.1 | async-start | bytes 32768 | tf_op jit(solution)/shard_map/all_to_all | solution.py:293
  45.9 3.1 %collective-permute-start = (f32[8,256]{1,0:T(8,128)S(1)}, f32[8,256]{1,0:T(8,128)S(1)}, u32[]{:S(2)}, u32[]{:S(2)}) collective-permute-start(f32[8,256]{1,0:T(8,128)S(1)} %get-tuple-element.32.wide_ref), channel_id=1, source_target_pairs={{0,32},{32,64},{64,96},{96,128},{128,160},{160,192},{192,224},{224... | collective-permute-start | bytes 24584 | tf_op jit(solution)/shard_map/ppermute | solution.py:25
  49.0 2.8 %collective-permute-done.below_ref = f32[8,256]{1,0:T(8,128)S(1)} collective-permute-done((f32[8,256]{1,0:T(8,128)S(1)}, f32[8,256]{1,0:T(8,128)S(1)}, u32[]{:S(2)}, u32[]{:S(2)}) %collective-permute-start) | collective-permute-done | bytes 8224 | tf_op jit(solution)/shard_map/ppermute | solution.py:25
  53.2 5.9 %powers.1 = (f32[96,512]{1,0:T(8,128)S(1)}, f32[96,512]{1,0:T(8,128)S(1)}, f32[96,512]{1,0:T(8,128)S(1)}, f32[8,512]{1,0:T(8,128)S(1)}) custom-call(f32[8,256]{1,0:T(8,128)S(1)} %get-tuple-element.32.wide_ref, f32[8,256]{1,0:T(8,128)S(1)} %collective-permute-done.below_ref, f32[96,4096]{1,0:T(8,128)S(1)} %bitcast.3), custom_call_target="tpu_custom_call" | custom-call | tf_op jit(solution)/shard_map/powers/pallas_call | solution.py:295
  59.2 7.9 %all-to-all-done.1.peaks_ref = f32[32,1,128]{2,1,0:T(1,128)S(1)} async-done(((f32[32,1,128]{2,1,0:T(1,128)}), f32[32,1,128]{2,1,0:T(1,128)S(1)}, u32[]{:S(2)}, u32[]{:S(2)}) %all-to-all-start.1) | async-done | bytes 16416 | tf_op jit(solution)/shard_map/all_to_all | solution.py:293
  67.1 4.9 %basis.1 = (f32[96,512]{1,0:T(8,128)S(1)}, f32[384,96]{1,0:T(8,128)S(1)}, f32[2]{0:T(128)S(1)}, f32[64,256]{1,0:T(8,128)S(1)}, f32[64,256]{1,0:T(8,128)S(1)}, /*...) custom-call(f32[32,1,128]{2,1,0:T(1,128)S(1)} %all-to-all-done.1.peaks_ref, ...), custom_call_target="tpu_custom_call" | custom-call | tf_op jit(solution)/shard_map/basis/pallas_call | solution.py:310
  72.0 8.5 %all-to-all-start.2 = ((f32[4,64,256]{2,1,0:T(8,128)}), f32[4,64,256]{2,1,0:T(8,128)S(1)}, u32[]{:S(2)}, u32[]{:S(2)}) async-start(f32[4,64,256]{2,1,0:T(8,128)} %get-tuple-element.44), calls=%async_computation.2 | async-start | bytes 524288 | tf_op jit(solution)/shard_map/all_to_all | solution.py:324
  80.5 1.9 %collective-permute-start.1 = (f32[64,256]{1,0:T(8,128)S(1)}, f32[64,256]{1,0:T(8,128)S(1)}, u32[]{:S(2)}, u32[]{:S(2)}) collective-permute-start(f32[64,256]{1,0:T(8,128)S(1)} %get-tuple-element.40), channel_id=1, source_target_pairs={{0,1},{2,3},{4,5},{6,7},{1,0},{3,2},{5,4},{7,6},{8,9},{10,11},{12,... | collective-permute-start | bytes 196616 | tf_op jit(solution)/shard_map/ppermute | solution.py:70
  82.4 1.9 %collective-permute-start.2 = (f32[64,256]{1,0:T(8,128)S(1)}, f32[64,256]{1,0:T(8,128)S(1)}, u32[]{:S(2)}, u32[]{:S(2)}) collective-permute-start(f32[64,256]{1,0:T(8,128)S(1)} %get-tuple-element.41), channel_id=1, source_target_pairs={{0,32},{64,96},{128,160},{192,224},{256,288},{320,352},{384,416},{... | collective-permute-start | bytes 196616 | tf_op jit(solution)/shard_map/ppermute | solution.py:70
  84.3 5.1 %collective-permute-start.3 = (f32[64,256]{1,0:T(8,128)S(1)}, f32[64,256]{1,0:T(8,128)S(1)}, u32[]{:S(2)}, u32[]{:S(2)}) collective-permute-start(f32[64,256]{1,0:T(8,128)S(1)} %get-tuple-element.42), channel_id=1, source_target_pairs={{8,16},{24,0},{16,8},{0,24},{9,17},{25,1},{17,9},{1,25},{10,18},{2... | collective-permute-start | bytes 196616 | tf_op jit(solution)/shard_map/ppermute | solution.py:70
  89.4 1.9 %collective-permute-start.4 = (f32[64,256]{1,0:T(8,128)S(1)}, f32[64,256]{1,0:T(8,128)S(1)}, u32[]{:S(2)}, u32[]{:S(2)}) collective-permute-start(f32[64,256]{1,0:T(8,128)S(1)} %get-tuple-element.43), channel_id=1, source_target_pairs={{0,8},{16,24},{8,0},{24,16},{1,9},{17,25},{9,1},{25,17},{2,10},{18... | collective-permute-start | bytes 196616 | tf_op jit(solution)/shard_map/ppermute | solution.py:70
  92.6 2.0 %step0.1 = (f32[96,256]{1,0:T(8,128)S(1)}, f32[64,256]{1,0:T(8,128)S(1)}, f32[64,256]{1,0:T(8,128)S(1)}, f32[64,256]{1,0:T(8,128)S(1)}, f32[64,256]{1,0:T(8,128)S(1)}, /*index=5*/f32[4,64,256]{2,1,0:T(8,128)}) custom-call(f32[2]{0:T(128)S(1)} %get-tuple-element.37.refs_0_, f32[96,512]{1,0:T(8,128)S(1)} %get-tuple-element.38.refs_1_, ...), custom_call_target="tpu_custom_call" | custom-call | tf_op jit(solution)/shard_map/step0/pallas_call | solution.py:331
  94.5 8.5 %all-to-all-start.3 = ((f32[4,64,256]{2,1,0:T(8,128)}), f32[4,64,256]{2,1,0:T(8,128)S(1)}, u32[]{:S(2)}, u32[]{:S(2)}) async-start(f32[4,64,256]{2,1,0:T(8,128)} %get-tuple-element.50), calls=%async_computation.3 | async-start | bytes 524288 | tf_op jit(solution)/shard_map/all_to_all | solution.py:324
  103.0 1.9 %collective-permute-start.5 = (f32[64,256]{1,0:T(8,128)S(1)}, f32[64,256]{1,0:T(8,128)S(1)}, u32[]{:S(2)}, u32[]{:S(2)}) collective-permute-start(f32[64,256]{1,0:T(8,128)S(1)} %get-tuple-element.46), channel_id=1, source_target_pairs={{0,1},{2,3},{4,5},{6,7},{1,0},{3,2},{5,4},{7,6},{8,9},{10,11},{12,... | collective-permute-start | bytes 196616 | tf_op jit(solution)/shard_map/ppermute | solution.py:70
  104.9 1.9 %collective-permute-start.6 = (f32[64,256]{1,0:T(8,128)S(1)}, f32[64,256]{1,0:T(8,128)S(1)}, u32[]{:S(2)}, u32[]{:S(2)}) collective-permute-start(f32[64,256]{1,0:T(8,128)S(1)} %get-tuple-element.47), channel_id=1, source_target_pairs={{0,32},{64,96},{128,160},{192,224},{256,288},{320,352},{384,416},{... | collective-permute-start | bytes 196616 | tf_op jit(solution)/shard_map/ppermute | solution.py:70
  106.8 3.6 %collective-permute-start.7 = (f32[64,256]{1,0:T(8,128)S(1)}, f32[64,256]{1,0:T(8,128)S(1)}, u32[]{:S(2)}, u32[]{:S(2)}) collective-permute-start(f32[64,256]{1,0:T(8,128)S(1)} %get-tuple-element.48), channel_id=1, source_target_pairs={{8,16},{24,0},{16,8},{0,24},{9,17},{25,1},{17,9},{1,25},{10,18},{2... | collective-permute-start | bytes 196616 | tf_op jit(solution)/shard_map/ppermute | solution.py:70
  110.5 1.9 %collective-permute-start.8 = (f32[64,256]{1,0:T(8,128)S(1)}, f32[64,256]{1,0:T(8,128)S(1)}, u32[]{:S(2)}, u32[]{:S(2)}) collective-permute-start(f32[64,256]{1,0:T(8,128)S(1)} %get-tuple-element.49), channel_id=1, source_target_pairs={{0,8},{16,24},{8,0},{24,16},{1,9},{17,25},{9,1},{25,17},{2,10},{18... | collective-permute-start | bytes 196616 | tf_op jit(solution)/shard_map/ppermute | solution.py:70
  113.6 2.0 %step1.1 = (f32[96,256]{1,0:T(8,128)S(1)}, f32[64,256]{1,0:T(8,128)S(1)}, f32[64,256]{1,0:T(8,128)S(1)}, f32[64,256]{1,0:T(8,128)S(1)}, f32[64,256]{1,0:T(8,128)S(1)}, /*index=5*/f32[4,64,256]{2,1,0:T(8,128)}) custom-call(f32[2]{0:T(128)S(1)} %get-tuple-element.37.refs_0_, f32[96,512]{1,0:T(8,128)S(1)} %get-tuple-element.38.refs_1_, ...), custom_call_target="tpu_custom_call" | custom-call | tf_op jit(solution)/shard_map/step1/pallas_call | solution.py:331
  115.6 8.5 %all-to-all-start.4 = ((f32[4,64,256]{2,1,0:T(8,128)}), f32[4,64,256]{2,1,0:T(8,128)S(1)}, u32[]{:S(2)}, u32[]{:S(2)}) async-start(f32[4,64,256]{2,1,0:T(8,128)} %get-tuple-element.56), calls=%async_computation.4 | async-start | bytes 524288 | tf_op jit(solution)/shard_map/all_to_all | solution.py:324
  124.1 1.9 %collective-permute-start.9 = (f32[64,256]{1,0:T(8,128)S(1)}, f32[64,256]{1,0:T(8,128)S(1)}, u32[]{:S(2)}, u32[]{:S(2)}) collective-permute-start(f32[64,256]{1,0:T(8,128)S(1)} %get-tuple-element.52), channel_id=1, source_target_pairs={{0,1},{2,3},{4,5},{6,7},{1,0},{3,2},{5,4},{7,6},{8,9},{10,11},{12,... | collective-permute-start | bytes 196616 | tf_op jit(solution)/shard_map/ppermute | solution.py:70
  126.0 1.9 %collective-permute-start.10 = (f32[64,256]{1,0:T(8,128)S(1)}, f32[64,256]{1,0:T(8,128)S(1)}, u32[]{:S(2)}, u32[]{:S(2)}) collective-permute-start(f32[64,256]{1,0:T(8,128)S(1)} %get-tuple-element.53), channel_id=1, source_target_pairs={{0,32},{64,96},{128,160},{192,224},{256,288},{320,352},{384,416},{... | collective-permute-start | bytes 196616 | tf_op jit(solution)/shard_map/ppermute | solution.py:70
  127.9 3.6 %collective-permute-start.11 = (f32[64,256]{1,0:T(8,128)S(1)}, f32[64,256]{1,0:T(8,128)S(1)}, u32[]{:S(2)}, u32[]{:S(2)}) collective-permute-start(f32[64,256]{1,0:T(8,128)S(1)} %get-tuple-element.54), channel_id=1, source_target_pairs={{8,16},{24,0},{16,8},{0,24},{9,17},{25,1},{17,9},{1,25},{10,18},{2... | collective-permute-start | bytes 196616 | tf_op jit(solution)/shard_map/ppermute | solution.py:70
  131.5 1.9 %collective-permute-start.12 = (f32[64,256]{1,0:T(8,128)S(1)}, f32[64,256]{1,0:T(8,128)S(1)}, u32[]{:S(2)}, u32[]{:S(2)}) collective-permute-start(f32[64,256]{1,0:T(8,128)S(1)} %get-tuple-element.55), channel_id=1, source_target_pairs={{0,8},{16,24},{8,0},{24,16},{1,9},{17,25},{9,1},{25,17},{2,10},{18... | collective-permute-start | bytes 196616 | tf_op jit(solution)/shard_map/ppermute | solution.py:70
  (24 shorter events, 8.1 us)
Async XLA Ops:
  0.0 0.8 copy-start.2
  0.8 66.3 %copy-start.1 = (f32[1,1,1,96,256]{4,3,2,1,0:T(8,128)S(1)}, f32[1,1,1,96,256]{4,3,2,1,0:T(8,128)}, u32[]{:S(2)}) copy-start(f32[1,1,1,96,256]{4,3,2,1,0:T(8,128)} %param.5) | copy-start | bytes 294916
  26.0 41.1 %all-to-all-start.1 = ((f32[32,1,128]{2,1,0:T(1,128)}), f32[32,1,128]{2,1,0:T(1,128)S(1)}, u32[]{:S(2)}, u32[]{:S(2)}) async-start(f32[32,1,128]{2,1,0:T(1,128)} %get-tuple-element.31), calls=%async_computation.1 | async-start | bytes 32768 | tf_op jit(solution)/shard_map/all_to_all | solution.py:293
  45.9 5.9 %collective-permute-start = (f32[8,256]{1,0:T(8,128)S(1)}, f32[8,256]{1,0:T(8,128)S(1)}, u32[]{:S(2)}, u32[]{:S(2)}) collective-permute-start(f32[8,256]{1,0:T(8,128)S(1)} %get-tuple-element.32.wide_ref), channel_id=1, source_target_pairs={{0,32},{32,64},{64,96},{96,128},{128,160},{160,192},{192,224},{224... | collective-permute-start | bytes 24584 | tf_op jit(solution)/shard_map/ppermute | solution.py:25
  51.8 1.4 %copy-start = (f32[1,1,1,96,4096]{4,3,2,1,0:T(8,128)S(1)}, f32[1,1,1,96,4096]{4,3,2,1,0:T(8,128)}, u32[]{:S(2)}) copy-start(f32[1,1,1,96,4096]{4,3,2,1,0:T(8,128)} %param.3) | copy-start | bytes 4718596
  72.0 20.6 %all-to-all-start.2 = ((f32[4,64,256]{2,1,0:T(8,128)}), f32[4,64,256]{2,1,0:T(8,128)S(1)}, u32[]{:S(2)}, u32[]{:S(2)}) async-start(f32[4,64,256]{2,1,0:T(8,128)} %get-tuple-element.44), calls=%async_computation.2 | async-start | bytes 524288 | tf_op jit(solution)/shard_map/all_to_all | solution.py:324
  80.5 10.9 %collective-permute-start.1 = (f32[64,256]{1,0:T(8,128)S(1)}, f32[64,256]{1,0:T(8,128)S(1)}, u32[]{:S(2)}, u32[]{:S(2)}) collective-permute-start(f32[64,256]{1,0:T(8,128)S(1)} %get-tuple-element.40), channel_id=1, source_target_pairs={{0,1},{2,3},{4,5},{6,7},{1,0},{3,2},{5,4},{7,6},{8,9},{10,11},{12,... | collective-permute-start | bytes 196616 | tf_op jit(solution)/shard_map/ppermute | solution.py:70
  82.4 9.0 %collective-permute-start.2 = (f32[64,256]{1,0:T(8,128)S(1)}, f32[64,256]{1,0:T(8,128)S(1)}, u32[]{:S(2)}, u32[]{:S(2)}) collective-permute-start(f32[64,256]{1,0:T(8,128)S(1)} %get-tuple-element.41), channel_id=1, source_target_pairs={{0,32},{64,96},{128,160},{192,224},{256,288},{320,352},{384,416},{... | collective-permute-start | bytes 196616 | tf_op jit(solution)/shard_map/ppermute | solution.py:70
  84.3 7.0 %collective-permute-start.3 = (f32[64,256]{1,0:T(8,128)S(1)}, f32[64,256]{1,0:T(8,128)S(1)}, u32[]{:S(2)}, u32[]{:S(2)}) collective-permute-start(f32[64,256]{1,0:T(8,128)S(1)} %get-tuple-element.42), channel_id=1, source_target_pairs={{8,16},{24,0},{16,8},{0,24},{9,17},{25,1},{17,9},{1,25},{10,18},{2... | collective-permute-start | bytes 196616 | tf_op jit(solution)/shard_map/ppermute | solution.py:70
  89.4 3.1 %collective-permute-start.4 = (f32[64,256]{1,0:T(8,128)S(1)}, f32[64,256]{1,0:T(8,128)S(1)}, u32[]{:S(2)}, u32[]{:S(2)}) collective-permute-start(f32[64,256]{1,0:T(8,128)S(1)} %get-tuple-element.43), channel_id=1, source_target_pairs={{0,8},{16,24},{8,0},{24,16},{1,9},{17,25},{9,1},{25,17},{2,10},{18... | collective-permute-start | bytes 196616 | tf_op jit(solution)/shard_map/ppermute | solution.py:70
  94.5 19.1 %all-to-all-start.3 = ((f32[4,64,256]{2,1,0:T(8,128)}), f32[4,64,256]{2,1,0:T(8,128)S(1)}, u32[]{:S(2)}, u32[]{:S(2)}) async-start(f32[4,64,256]{2,1,0:T(8,128)} %get-tuple-element.50), calls=%async_computation.3 | async-start | bytes 524288 | tf_op jit(solution)/shard_map/all_to_all | solution.py:324
  103.0 9.4 %collective-permute-start.5 = (f32[64,256]{1,0:T(8,128)S(1)}, f32[64,256]{1,0:T(8,128)S(1)}, u32[]{:S(2)}, u32[]{:S(2)}) collective-permute-start(f32[64,256]{1,0:T(8,128)S(1)} %get-tuple-element.46), channel_id=1, source_target_pairs={{0,1},{2,3},{4,5},{6,7},{1,0},{3,2},{5,4},{7,6},{8,9},{10,11},{12,... | collective-permute-start | bytes 196616 | tf_op jit(solution)/shard_map/ppermute | solution.py:70
  104.9 7.5 %collective-permute-start.6 = (f32[64,256]{1,0:T(8,128)S(1)}, f32[64,256]{1,0:T(8,128)S(1)}, u32[]{:S(2)}, u32[]{:S(2)}) collective-permute-start(f32[64,256]{1,0:T(8,128)S(1)} %get-tuple-element.47), channel_id=1, source_target_pairs={{0,32},{64,96},{128,160},{192,224},{256,288},{320,352},{384,416},{... | collective-permute-start | bytes 196616 | tf_op jit(solution)/shard_map/ppermute | solution.py:70
  106.8 6.4 %collective-permute-start.7 = (f32[64,256]{1,0:T(8,128)S(1)}, f32[64,256]{1,0:T(8,128)S(1)}, u32[]{:S(2)}, u32[]{:S(2)}) collective-permute-start(f32[64,256]{1,0:T(8,128)S(1)} %get-tuple-element.48), channel_id=1, source_target_pairs={{8,16},{24,0},{16,8},{0,24},{9,17},{25,1},{17,9},{1,25},{10,18},{2... | collective-permute-start | bytes 196616 | tf_op jit(solution)/shard_map/ppermute | solution.py:70
  110.5 3.1 %collective-permute-start.8 = (f32[64,256]{1,0:T(8,128)S(1)}, f32[64,256]{1,0:T(8,128)S(1)}, u32[]{:S(2)}, u32[]{:S(2)}) collective-permute-start(f32[64,256]{1,0:T(8,128)S(1)} %get-tuple-element.49), channel_id=1, source_target_pairs={{0,8},{16,24},{8,0},{24,16},{1,9},{17,25},{9,1},{25,17},{2,10},{18... | collective-permute-start | bytes 196616 | tf_op jit(solution)/shard_map/ppermute | solution.py:70
  115.6 19.1 %all-to-all-start.4 = ((f32[4,64,256]{2,1,0:T(8,128)}), f32[4,64,256]{2,1,0:T(8,128)S(1)}, u32[]{:S(2)}, u32[]{:S(2)}) async-start(f32[4,64,256]{2,1,0:T(8,128)} %get-tuple-element.56), calls=%async_computation.4 | async-start | bytes 524288 | tf_op jit(solution)/shard_map/all_to_all | solution.py:324
  124.1 9.4 %collective-permute-start.9 = (f32[64,256]{1,0:T(8,128)S(1)}, f32[64,256]{1,0:T(8,128)S(1)}, u32[]{:S(2)}, u32[]{:S(2)}) collective-permute-start(f32[64,256]{1,0:T(8,128)S(1)} %get-tuple-element.52), channel_id=1, source_target_pairs={{0,1},{2,3},{4,5},{6,7},{1,0},{3,2},{5,4},{7,6},{8,9},{10,11},{12,... | collective-permute-start | bytes 196616 | tf_op jit(solution)/shard_map/ppermute | solution.py:70
  126.0 7.5 %collective-permute-start.10 = (f32[64,256]{1,0:T(8,128)S(1)}, f32[64,256]{1,0:T(8,128)S(1)}, u32[]{:S(2)}, u32[]{:S(2)}) collective-permute-start(f32[64,256]{1,0:T(8,128)S(1)} %get-tuple-element.53), channel_id=1, source_target_pairs={{0,32},{64,96},{128,160},{192,224},{256,288},{320,352},{384,416},{... | collective-permute-start | bytes 196616 | tf_op jit(solution)/shard_map/ppermute | solution.py:70
  127.9 6.5 %collective-permute-start.11 = (f32[64,256]{1,0:T(8,128)S(1)}, f32[64,256]{1,0:T(8,128)S(1)}, u32[]{:S(2)}, u32[]{:S(2)}) collective-permute-start(f32[64,256]{1,0:T(8,128)S(1)} %get-tuple-element.54), channel_id=1, source_target_pairs={{8,16},{24,0},{16,8},{0,24},{9,17},{25,1},{17,9},{1,25},{10,18},{2... | collective-permute-start | bytes 196616 | tf_op jit(solution)/shard_map/ppermute | solution.py:70
  131.5 3.1 %collective-permute-start.12 = (f32[64,256]{1,0:T(8,128)S(1)}, f32[64,256]{1,0:T(8,128)S(1)}, u32[]{:S(2)}, u32[]{:S(2)}) collective-permute-start(f32[64,256]{1,0:T(8,128)S(1)} %get-tuple-element.55), channel_id=1, source_target_pairs={{0,8},{16,24},{8,0},{24,16},{1,9},{17,25},{9,1},{25,17},{2,10},{18... | collective-permute-start | bytes 196616 | tf_op jit(solution)/shard_map/ppermute | solution.py:70

commit v4 on v3

--- a/solution.py
+++ b/solution.py
@@ -13,7 +13,7 @@
 FLAT = EDGE * EDGE
 COLS = 256
 FACES = 6
-RING = 4
+CUBE = 8
 GRANT = 16 << 20
 BODY = FACES * FLAT
 WIDTH = 512
@@ -34,11 +34,13 @@
 def dot3(left, right, dims=(((1,), (0,)), ((), ()))):
     lh, ll = left
     rh, rl = right
+    rows = lh.shape[0]
 
     def one(a, b):
         return lax.dot_general(a, b, dims, preferred_element_type=jnp.float32)
 
-    return one(lh, rh) + (one(lh, rl) + one(ll, rh))
+    both = one(jnp.concatenate([lh, ll], axis=0), rh)
+    return both[:rows] + (both[rows:] + one(lh, rl))
 
 
 def exact(left, right, dims=(((1,), (0,)), ((), ()))):
@@ -47,6 +49,10 @@
     )
 
 
+def product(left, right):
+    return dot3(split(left), split(right))
+
+
 def lane_roll(value, by):
     return pltpu.roll(value, by % value.shape[-1], axis=value.ndim - 1)
 
@@ -55,9 +61,10 @@
     return lax.broadcasted_iota(jnp.int32, shape, len(shape) - 1)
 
 
-SWAPS = (("gz", 0), ("gx", 0), ("gy", 1), ("gy", 0))
-SLOTS = SWAPS + (("gx", 1), ("gz", 1))
+SWAPS = (("gz", 1), ("gx", 1), ("gy", 1))
 AXES = ("gx", "gy", "gz")
+SLOTS = SWAPS + tuple((axis, 0) for axis in AXES)
+FLIPS = (4, 2, 1)
 
 
 def upper_side(axis, odd):
@@ -71,14 +78,20 @@
 
 
 def place():
-    return (1 - lax.rem(lax.axis_index("gx"), 2)) * 2 + 1 - lax.rem(lax.axis_index("gz"), 2)
-
-
-def rings():
-    nx, nz = lax.axis_size("gx"), lax.axis_size("gz")
+    return sum(flip * lax.rem(lax.axis_index(axis), 2) for flip, axis in zip(FLIPS, AXES))
+
+
+def cubes():
+    nx, ny, nz = (lax.axis_size(axis) for axis in AXES)
     return [
-        [(2 * i + 1 + a) % nx * nz + (2 * k + 1 + c) % nz for a in range(2) for c in range(2)]
+        [
+            ((2 * i + a) * ny + 2 * j + b) * nz + 2 * k + c
+            for a in range(2)
+            for b in range(2)
+            for c in range(2)
+        ]
         for i in range(nx // 2)
+        for j in range(ny // 2)
         for k in range(nz // 2)
     ]
 
@@ -109,14 +122,7 @@
         wide_ref[:, half * 128 : (half + 1) * 128] = jnp.where(near, low, lane_roll(high, 8))
 
 
-def filter_kernel(wide_ref, below_ref, orbitals_ref, u0_ref, u1_ref, u2_ref, own_ref, w_ref,
-                  held_ref, sems):
-    def fetch(step):
-        rows = pl.ds(pl.multiple_of(step * 8, 8), 8)
-        return pltpu.make_async_copy(orbitals_ref.at[rows], held_ref.at[step], sems.at[step])
-
-    for step in range(ROWS // 8):
-        fetch(step).start()
+def filter_kernel(wide_ref, below_ref, orbitals_ref, u0_ref, u1_ref, u2_ref, own_ref, w_ref):
     first_half = lanes((8, 128)) % 16 < 8
 
     def packed(even, odd):
@@ -137,8 +143,7 @@
 
     def filter_rows(step, carry):
         rows = pl.ds(pl.multiple_of(step * 8, 8), 8)
-        fetch(step).wait()
-        start = {p: held_ref[step, :, p * 256 : (p + 1) * 256] for p in range(2, 14)}
+        start = {p: orbitals_ref[rows, p * 256 : (p + 1) * 256] for p in range(2, 14)}
         once = {}
         for p in range(3, 13):
             total = around(start[p]) + (start[p - 1] + start[p + 1])
@@ -158,12 +163,17 @@
 
 
 def store_traces(ft, value, *refs):
-    traces = dot3(split(ft), split(value))
-    for slot in range(4):
-        refs[slot][...] = traces[slot * FLAT : (slot + 1) * FLAT]
-    at = place()
-    for slot, flip in ((4, 2), (5, 1)):
-        refs[4][at ^ flip] = traces[slot * FLAT : (slot + 1) * FLAT]
+    right = split(value)
+    half = BODY // 2
+    for part in range(2):
+        traces = dot3(split(ft[part * half : (part + 1) * half]), right)
+        at = place()
+        for slot in range(3):
+            block = traces[slot * FLAT : (slot + 1) * FLAT]
+            if part == 0:
+                refs[slot][...] = block
+            else:
+                refs[3][at ^ FLIPS[slot]] = block
 
 
 def basis_kernel(peaks_ref, u0_ref, u1_ref, u2_ref, own_ref, vectors_ref,
@@ -179,20 +189,20 @@
     square = u2_ref[...] + (2.0 * moved) * u1_ref[...] + (moved * moved) * start
     restricted = square * (2.0 / (half_width * half_width)) - start
     halves = split(restricted)
-    intersection = exact(restricted, restricted, (((1,), (1,)), ((), ())))
+    intersection = dot3(halves, halves, (((1,), (1,)), ((), ())))
     sigma = jnp.sqrt(jnp.sum(intersection * intersection))
     identity = (
         lax.broadcasted_iota(jnp.int32, (ROWS, ROWS), 0) == lanes((ROWS, ROWS))
     ).astype(jnp.float32)
     current = intersection / sigma
     factor = 1.5 * identity - 0.5 * current
-    current = exact(current, factor)
+    current = product(current, factor)
     root = factor
     for step in range(NEWTON - 1):
-        factor = 1.5 * identity - 0.5 * exact(root, current)
+        factor = 1.5 * identity - 0.5 * product(root, current)
         if step < NEWTON - 2:
-            current = exact(current, factor)
-        root = exact(factor, root)
+            current = product(current, factor)
+        root = product(factor, root)
     root = root / jnp.sqrt(sigma)
     basis = dot3(split(root), halves)
 
@@ -240,14 +250,15 @@
 
 
 def step_kernel(first, last, scal_ref, df_ref, ft_ref, now_ref, prior_ref, *refs):
-    swap_refs, ring_ref, out_ref, sent = refs[:4], refs[4], refs[5], refs[6:]
+    swap_refs, cube_ref, out_ref, sent = refs[:3], refs[3], refs[4], refs[5:]
     now = now_ref[...]
     at = place()
-    halos = [ref[...] for ref in swap_refs] + [ring_ref[at ^ 2], ring_ref[at ^ 1]]
-    stacked = jnp.concatenate(
-        halos + [now, jnp.zeros((WIDTH - BODY - ROWS, COLS), jnp.float32)], axis=0
-    )
-    result = dot3(split(df_ref[...]), split(stacked))
+    halos = [ref[...] for ref in swap_refs] + [cube_ref[at ^ flip] for flip in FLIPS]
+    first_half = halos[:4]
+    second_half = halos[4:] + [now, jnp.zeros((WIDTH - BODY - ROWS, COLS), jnp.float32)]
+    result = dot3(
+        split(df_ref[:, : WIDTH // 2]), split(jnp.concatenate(first_half, axis=0))
+    ) + dot3(split(df_ref[:, WIDTH // 2 :]), split(jnp.concatenate(second_half, axis=0)))
     centre, half_width = scal_ref[0], scal_ref[1]
     following = (result - centre * now) / half_width
     if not first:
@@ -295,33 +306,29 @@
     powers = pl.pallas_call(
         filter_kernel,
         out_shape=(of(ROWS, WIDTH), of(ROWS, WIDTH), of(ROWS, WIDTH), of(8, WIDTH)),
-        in_specs=[vmem(), vmem(), pl.BlockSpec(memory_space=pltpu.HBM)],
+        in_specs=[vmem(), vmem(), vmem()],
         out_specs=(vmem(),) * 4,
-        scratch_shapes=[
-            pltpu.VMEM((10, 8, 256), f32),
-            pltpu.VMEM((ROWS // 8, 8, 4096), f32),
-            pltpu.SemaphoreType.DMA((ROWS // 8,)),
-        ],
+        scratch_shapes=[pltpu.VMEM((10, 8, 256), f32)],
         compiler_params=pltpu.CompilerParams(vmem_limit_bytes=GRANT),
         name="powers",
     )(wide, below, orbitals.reshape(ROWS, -1))
     start = coefficients.reshape(ROWS, COLS)
-    sent_shapes = (of(FLAT, COLS),) * 4 + (of(RING, FLAT, COLS),)
+    sent_shapes = (of(FLAT, COLS),) * 3 + (of(CUBE, FLAT, COLS),)
     df, ft, scal, *sent = pl.pallas_call(
         basis_kernel,
         out_shape=(of(ROWS, WIDTH), of(BODY, ROWS), of(2)) + sent_shapes,
         in_specs=[vmem()] * 6,
-        out_specs=(vmem(), vmem(), smem()) + (vmem(),) * 5,
+        out_specs=(vmem(), vmem(), smem()) + (vmem(),) * 4,
         scratch_shapes=[pltpu.VMEM((WIDTH, 128), f32)],
         compiler_params=pltpu.CompilerParams(vmem_limit_bytes=GRANT),
         name="basis",
     )(peaks, *powers, start)
 
-    groups = rings()
+    groups = cubes()
     prior, now = start, start
     for step in range(DG_STEPS):
         halos = [swapped(trace, *pairing) for trace, pairing in zip(sent, SWAPS)]
-        halos.append(lax.all_to_all(sent[4], ("gx", "gz"), 0, 0, axis_index_groups=groups))
+        halos.append(lax.all_to_all(sent[3], AXES, 0, 0, axis_index_groups=groups))
         last = step == DG_STEPS - 1
         shapes = (of(ROWS, COLS),) + (() if last else sent_shapes)
 
@@ -331,7 +338,7 @@
         following, *sent = pl.pallas_call(
             body,
             out_shape=shapes,
-            in_specs=[smem()] + [vmem()] * 9,
+            in_specs=[smem()] + [vmem()] * 8,
             out_specs=tuple(vmem() for _ in shapes),
             compiler_params=pltpu.CompilerParams(vmem_limit_bytes=GRANT),
             name=f"step{step}",

time: 137 us -> 132 us (0.964)
  starting transfers between devices: 78 us -> 68.6 us
  waiting for transfers between devices: 14.3 us -> 21.6 us
  Pallas kernels: 17.1 us -> 14.4 us
    all_to_all x3, starting transfers between devices: 25.4 us -> 13.9 us  [per_device(): halos.append(lax.all_to_all(sent[3], AXES, 0, 0, axis_index_groups=groups))]
    ppermute x12 -> x9, waiting for transfers between devices: 3.6 us -> 8.76 us  [swapped(): return lax.ppermute(shard, axis, pairs + [(b, a) for a, b in pairs])]
    all_to_all x1, waiting for transfers between devices: 7.95 us -> 10.1 us  [per_device(): peaks = lax.all_to_all(peak, 'gx', 0, 0)]
    pallas_call x1, Pallas kernels: 5.95 us -> 3.82 us  [per_device(): pl.pallas_call(filter_kernel, out_shape=(of(ROWS, WIDTH), of(ROWS, WIDTH)...]
    ppermute x12 -> x9, starting transfers between devices: 29.6 us -> 31.7 us  [swapped(): return lax.ppermute(shard, axis, pairs + [(b, a) for a, b in pairs])]
  transfers between devices with their start and end apart: 17 -> 14, of which waited for: 7 -> 6; matrix products, arithmetic and copies ran while one was open for 0% -> 0% of each run, Pallas kernels for 4% -> 3%
where the time goes in v4:
time: 132 us; the launch traced here: 131 us
  starting transfers between devices  68.6 us (52%)
  blocking collectives  24.3 us (18%)
  waiting for transfers between devices  21.6 us (16%)
  Pallas kernels  14.4 us (11%)
  local copies, waits for them, and re-layouts  2.17 us (2%)
    ppermute x9, starting transfers between devices, swapped(): return lax.ppermute(shard, axis, pairs + [(b, a) for a, b in pairs])  31.7 us
    all_to_all x1, blocking collectives, per_device(): tiles = lax.all_to_all(tile, ('gy', 'gz'), 0, 0)  24.3 us
    all_to_all x1, starting transfers between devices, per_device(): peaks = lax.all_to_all(peak, 'gx', 0, 0)  19.9 us
    all_to_all x3, starting transfers between devices, per_device(): halos.append(lax.all_to_all(sent[3], AXES, 0, 0, axis_index_groups=groups))  13.9 us
    all_to_all x1, waiting for transfers between devices, per_device(): peaks = lax.all_to_all(peak, 'gx', 0, 0)  10.1 us
    ppermute x9, waiting for transfers between devices, swapped(): return lax.ppermute(shard, axis, pairs + [(b, a) for a, b in pairs])  8.76 us
    pallas_call x3, Pallas kernels, per_device(): pl.pallas_call(body, out_shape=shapes, in_specs=[smem()] + [vmem()] * 8,...  5.51 us
    pallas_call x1, Pallas kernels, per_device(): pl.pallas_call(basis_kernel, out_shape=(of(ROWS, WIDTH), of(BODY, ROWS),...  4.21 us
  transfers between devices with their start and end apart: 14, of which 6 were waited for; matrix products, arithmetic and copies ran while one was open for 0% of the time, Pallas kernels for 3%

profile of v4, /device:TPU:1, one launch (start us, length us, event | category | flops | bytes accessed | tf_op | source)
XLA Modules:
  0.0 131.3 jit_solution(13268194356598105517)
XLA Ops:
  0.9 24.3 %all_to_all.25.tiles_ref = f32[32,8,128]{2,1,0:T(8,128)S(1)} all-to-all(f32[32,8,128]{2,1,0:T(8,128)S(1)} %tile.1), channel_id=1, replica_groups=mesh['gx'=32,'gy'=4,'gz'=8] {'gy','gz'}, dimensions={0} | all-to-all | bytes 262144 | tf_op jit(solution)/shard_map/all_to_all | solution.py:295
  26.0 19.9 %all-to-all-start.1 = ((f32[32,1,128]{2,1,0:T(1,128)}), f32[32,1,128]{2,1,0:T(1,128)S(1)}, u32[]{:S(2)}, u32[]{:S(2)}) async-start(f32[32,1,128]{2,1,0:T(1,128)} %get-tuple-element.28), calls=%async_computation.1 | async-start | bytes 32768 | tf_op jit(solution)/shard_map/all_to_all | solution.py:304
  45.9 3.1 %collective-permute-start = (f32[8,256]{1,0:T(8,128)S(1)}, f32[8,256]{1,0:T(8,128)S(1)}, u32[]{:S(2)}, u32[]{:S(2)}) collective-permute-start(f32[8,256]{1,0:T(8,128)S(1)} %get-tuple-element.29.wide_ref), channel_id=1, source_target_pairs={{0,32},{32,64},{64,96},{96,128},{128,160},{160,192},{192,224},{224... | collective-permute-start | bytes 24584 | tf_op jit(solution)/shard_map/ppermute | solution.py:25
  49.0 2.8 %collective-permute-done.below_ref = f32[8,256]{1,0:T(8,128)S(1)} collective-permute-done((f32[8,256]{1,0:T(8,128)S(1)}, f32[8,256]{1,0:T(8,128)S(1)}, u32[]{:S(2)}, u32[]{:S(2)}) %collective-permute-start) | collective-permute-done | bytes 8224 | tf_op jit(solution)/shard_map/ppermute | solution.py:25
  53.2 3.8 %powers.1 = (f32[96,512]{1,0:T(8,128)S(1)}, f32[96,512]{1,0:T(8,128)S(1)}, f32[96,512]{1,0:T(8,128)S(1)}, f32[8,512]{1,0:T(8,128)S(1)}) custom-call(f32[8,256]{1,0:T(8,128)S(1)} %get-tuple-element.29.wide_ref, f32[8,256]{1,0:T(8,128)S(1)} %collective-permute-done.below_ref, f32[96,4096]{1,0:T(8,128)S(1)} %bitcast.3), custom_call_target="tpu_custom_call" | custom-call | tf_op jit(solution)/shard_map/powers/pallas_call | solution.py:306
  57.0 10.1 %all-to-all-done.1.peaks_ref = f32[32,1,128]{2,1,0:T(1,128)S(1)} async-done(((f32[32,1,128]{2,1,0:T(1,128)}), f32[32,1,128]{2,1,0:T(1,128)S(1)}, u32[]{:S(2)}, u32[]{:S(2)}) %all-to-all-start.1) | async-done | bytes 16416 | tf_op jit(solution)/shard_map/all_to_all | solution.py:304
  67.1 4.2 %basis.1 = (f32[96,512]{1,0:T(8,128)S(1)}, f32[384,96]{1,0:T(8,128)S(1)}, f32[2]{0:T(128)S(1)}, f32[64,256]{1,0:T(8,128)S(1)}, f32[64,256]{1,0:T(8,128)S(1)}, /*...) custom-call(f32[32,1,128]{2,1,0:T(1,128)S(1)} %all-to-all-done.1.peaks_ref, f32[96,512]{1,0:T(8,128)S(1)} %get-tuple-element.30.u0_ref, ...), custom_call_target="tpu_custom_call" | custom-call | tf_op jit(solution)/shard_map/basis/pallas_call | solution.py:317
  71.3 5.8 %all-to-all-start.2 = ((f32[8,64,256]{2,1,0:T(8,128)}), f32[8,64,256]{2,1,0:T(8,128)S(1)}, u32[]{:S(2)}, u32[]{:S(2)}) async-start(f32[8,64,256]{2,1,0:T(8,128)} %get-tuple-element.40), calls=%async_computation.2 | async-start | bytes 1048576 | tf_op jit(solution)/shard_map/all_to_all | solution.py:331
  77.1 3.4 %collective-permute-start.1 = (f32[64,256]{1,0:T(8,128)S(1)}, f32[64,256]{1,0:T(8,128)S(1)}, u32[]{:S(2)}, u32[]{:S(2)}) collective-permute-start(f32[64,256]{1,0:T(8,128)S(1)} %get-tuple-element.37), channel_id=1, source_target_pairs={{1,2},{3,4},{5,6},{7,0},{2,1},{4,3},{6,5},{0,7},{9,10},{11,12},{13... | collective-permute-start | bytes 196616 | tf_op jit(solution)/shard_map/ppermute | solution.py:77
  80.5 2.3 %collective-permute-start.2 = (f32[64,256]{1,0:T(8,128)S(1)}, f32[64,256]{1,0:T(8,128)S(1)}, u32[]{:S(2)}, u32[]{:S(2)}) collective-permute-start(f32[64,256]{1,0:T(8,128)S(1)} %get-tuple-element.38), channel_id=1, source_target_pairs={{32,64},{96,128},{160,192},{224,256},{288,320},{352,384},{416,448}... | collective-permute-start | bytes 196616 | tf_op jit(solution)/shard_map/ppermute | solution.py:77
  82.8 3.6 %collective-permute-start.3 = (f32[64,256]{1,0:T(8,128)S(1)}, f32[64,256]{1,0:T(8,128)S(1)}, u32[]{:S(2)}, u32[]{:S(2)}) collective-permute-start(f32[64,256]{1,0:T(8,128)S(1)} %get-tuple-element.39), channel_id=1, source_target_pairs={{8,16},{24,0},{16,8},{0,24},{9,17},{25,1},{17,9},{1,25},{10,18},{2... | collective-permute-start | bytes 196616 | tf_op jit(solution)/shard_map/ppermute | solution.py:77
  86.8 2.4 %collective-permute-done.3.refs_7_ = f32[64,256]{1,0:T(8,128)S(1)} collective-permute-done((f32[64,256]{1,0:T(8,128)S(1)}, f32[64,256]{1,0:T(8,128)S(1)}, u32[]{:S(2)}, u32[]{:S(2)}) %collective-permute-start.3) | collective-permute-done | bytes 65568 | tf_op jit(solution)/shard_map/ppermute | solution.py:77
  89.1 2.0 %step0.1 = (f32[96,256]{1,0:T(8,128)S(1)}, f32[64,256]{1,0:T(8,128)S(1)}, f32[64,256]{1,0:T(8,128)S(1)}, f32[64,256]{1,0:T(8,128)S(1)}, f32[8,64,256]{2,1,0:T(8,128)}) custom-call(f32[2]{0:T(128)S(1)} %get-tuple-element.34.refs_0_, f32[96,512]{1,0:T(8,128)S(1)} %get-tuple-element.35.refs_1_, f32[384,96]{1,0:T(8,128)S(1)} %get-tuple-element.36.refs_2_, ...), custom_call_target="tpu_custom_call" | custom-call | tf_op jit(solution)/shard_map/step0/pallas_call | solution.py:338
  91.2 4.1 %all-to-all-start.3 = ((f32[8,64,256]{2,1,0:T(8,128)}), f32[8,64,256]{2,1,0:T(8,128)S(1)}, u32[]{:S(2)}, u32[]{:S(2)}) async-start(f32[8,64,256]{2,1,0:T(8,128)} %get-tuple-element.45), calls=%async_computation.3 | async-start | bytes 1048576 | tf_op jit(solution)/shard_map/all_to_all | solution.py:331
  95.2 5.6 %collective-permute-start.4 = (f32[64,256]{1,0:T(8,128)S(1)}, f32[64,256]{1,0:T(8,128)S(1)}, u32[]{:S(2)}, u32[]{:S(2)}) collective-permute-start(f32[64,256]{1,0:T(8,128)S(1)} %get-tuple-element.42), channel_id=1, source_target_pairs={{1,2},{3,4},{5,6},{7,0},{2,1},{4,3},{6,5},{0,7},{9,10},{11,12},{13... | collective-permute-start | bytes 196616 | tf_op jit(solution)/shard_map/ppermute | solution.py:77
  100.9 4.4 %collective-permute-start.5 = (f32[64,256]{1,0:T(8,128)S(1)}, f32[64,256]{1,0:T(8,128)S(1)}, u32[]{:S(2)}, u32[]{:S(2)}) collective-permute-start(f32[64,256]{1,0:T(8,128)S(1)} %get-tuple-element.43), channel_id=1, source_target_pairs={{32,64},{96,128},{160,192},{224,256},{288,320},{352,384},{416,448}... | collective-permute-start | bytes 196616 | tf_op jit(solution)/shard_map/ppermute | solution.py:77
  105.3 3.1 %collective-permute-start.6 = (f32[64,256]{1,0:T(8,128)S(1)}, f32[64,256]{1,0:T(8,128)S(1)}, u32[]{:S(2)}, u32[]{:S(2)}) collective-permute-start(f32[64,256]{1,0:T(8,128)S(1)} %get-tuple-element.44), channel_id=1, source_target_pairs={{8,16},{24,0},{16,8},{0,24},{9,17},{25,1},{17,9},{1,25},{10,18},{2... | collective-permute-start | bytes 196616 | tf_op jit(solution)/shard_map/ppermute | solution.py:77
  108.4 3.2 %collective-permute-done.6.refs_7_ = f32[64,256]{1,0:T(8,128)S(1)} collective-permute-done((f32[64,256]{1,0:T(8,128)S(1)}, f32[64,256]{1,0:T(8,128)S(1)}, u32[]{:S(2)}, u32[]{:S(2)}) %collective-permute-start.6) | collective-permute-done | bytes 65568 | tf_op jit(solution)/shard_map/ppermute | solution.py:77
  111.6 2.0 %step1.1 = (f32[96,256]{1,0:T(8,128)S(1)}, f32[64,256]{1,0:T(8,128)S(1)}, f32[64,256]{1,0:T(8,128)S(1)}, f32[64,256]{1,0:T(8,128)S(1)}, f32[8,64,256]{2,1,0:T(8,128)}) custom-call(f32[2]{0:T(128)S(1)} %get-tuple-element.34.refs_0_, f32[96,512]{1,0:T(8,128)S(1)} %get-tuple-element.35.refs_1_, f32[384,96]{1,0:T(8,128)S(1)} %get-tuple-element.36.refs_2_, ...), custom_call_target="tpu_custom_call" | custom-call | tf_op jit(solution)/shard_map/step1/pallas_call | solution.py:338
  113.6 4.1 %all-to-all-start.4 = ((f32[8,64,256]{2,1,0:T(8,128)}), f32[8,64,256]{2,1,0:T(8,128)S(1)}, u32[]{:S(2)}, u32[]{:S(2)}) async-start(f32[8,64,256]{2,1,0:T(8,128)} %get-tuple-element.50), calls=%async_computation.4 | async-start | bytes 1048576 | tf_op jit(solution)/shard_map/all_to_all | solution.py:331
  117.7 2.4 %collective-permute-start.7 = (f32[64,256]{1,0:T(8,128)S(1)}, f32[64,256]{1,0:T(8,128)S(1)}, u32[]{:S(2)}, u32[]{:S(2)}) collective-permute-start(f32[64,256]{1,0:T(8,128)S(1)} %get-tuple-element.47), channel_id=1, source_target_pairs={{1,2},{3,4},{5,6},{7,0},{2,1},{4,3},{6,5},{0,7},{9,10},{11,12},{13... | collective-permute-start | bytes 196616 | tf_op jit(solution)/shard_map/ppermute | solution.py:77
  120.1 3.1 %collective-permute-start.8 = (f32[64,256]{1,0:T(8,128)S(1)}, f32[64,256]{1,0:T(8,128)S(1)}, u32[]{:S(2)}, u32[]{:S(2)}) collective-permute-start(f32[64,256]{1,0:T(8,128)S(1)} %get-tuple-element.48), channel_id=1, source_target_pairs={{32,64},{96,128},{160,192},{224,256},{288,320},{352,384},{416,448}... | collective-permute-start | bytes 196616 | tf_op jit(solution)/shard_map/ppermute | solution.py:77
  123.1 3.8 %collective-permute-start.9 = (f32[64,256]{1,0:T(8,128)S(1)}, f32[64,256]{1,0:T(8,128)S(1)}, u32[]{:S(2)}, u32[]{:S(2)}) collective-permute-start(f32[64,256]{1,0:T(8,128)S(1)} %get-tuple-element.49), channel_id=1, source_target_pairs={{8,16},{24,0},{16,8},{0,24},{9,17},{25,1},{17,9},{1,25},{10,18},{2... | collective-permute-start | bytes 196616 | tf_op jit(solution)/shard_map/ppermute | solution.py:77
  127.0 2.8 %collective-permute-done.9.refs_7_ = f32[64,256]{1,0:T(8,128)S(1)} collective-permute-done((f32[64,256]{1,0:T(8,128)S(1)}, f32[64,256]{1,0:T(8,128)S(1)}, u32[]{:S(2)}, u32[]{:S(2)}) %collective-permute-start.9) | collective-permute-done | bytes 65568 | tf_op jit(solution)/shard_map/ppermute | solution.py:77
  (18 shorter events, 4.9 us)
Async XLA Ops:
  0.0 0.8 copy-start.2
  0.8 66.3 %copy-start.1 = (f32[1,1,1,96,256]{4,3,2,1,0:T(8,128)S(1)}, f32[1,1,1,96,256]{4,3,2,1,0:T(8,128)}, u32[]{:S(2)}) copy-start(f32[1,1,1,96,256]{4,3,2,1,0:T(8,128)} %param.5) | copy-start | bytes 294916
  26.0 41.1 %all-to-all-start.1 = ((f32[32,1,128]{2,1,0:T(1,128)}), f32[32,1,128]{2,1,0:T(1,128)S(1)}, u32[]{:S(2)}, u32[]{:S(2)}) async-start(f32[32,1,128]{2,1,0:T(1,128)} %get-tuple-element.28), calls=%async_computation.1 | async-start | bytes 32768 | tf_op jit(solution)/shard_map/all_to_all | solution.py:304
  45.9 5.9 %collective-permute-start = (f32[8,256]{1,0:T(8,128)S(1)}, f32[8,256]{1,0:T(8,128)S(1)}, u32[]{:S(2)}, u32[]{:S(2)}) collective-permute-start(f32[8,256]{1,0:T(8,128)S(1)} %get-tuple-element.29.wide_ref), channel_id=1, source_target_pairs={{0,32},{32,64},{64,96},{96,128},{128,160},{160,192},{192,224},{224... | collective-permute-start | bytes 24584 | tf_op jit(solution)/shard_map/ppermute | solution.py:25
  51.8 1.4 %copy-start = (f32[1,1,1,96,4096]{4,3,2,1,0:T(8,128)S(1)}, f32[1,1,1,96,4096]{4,3,2,1,0:T(8,128)}, u32[]{:S(2)}) copy-start(f32[1,1,1,96,4096]{4,3,2,1,0:T(8,128)} %param.3) | copy-start | bytes 4718596
  71.3 17.8 %all-to-all-start.2 = ((f32[8,64,256]{2,1,0:T(8,128)}), f32[8,64,256]{2,1,0:T(8,128)S(1)}, u32[]{:S(2)}, u32[]{:S(2)}) async-start(f32[8,64,256]{2,1,0:T(8,128)} %get-tuple-element.40), calls=%async_computation.2 | async-start | bytes 1048576 | tf_op jit(solution)/shard_map/all_to_all | solution.py:331
  77.1 9.3 %collective-permute-start.1 = (f32[64,256]{1,0:T(8,128)S(1)}, f32[64,256]{1,0:T(8,128)S(1)}, u32[]{:S(2)}, u32[]{:S(2)}) collective-permute-start(f32[64,256]{1,0:T(8,128)S(1)} %get-tuple-element.37), channel_id=1, source_target_pairs={{1,2},{3,4},{5,6},{7,0},{2,1},{4,3},{6,5},{0,7},{9,10},{11,12},{13... | collective-permute-start | bytes 196616 | tf_op jit(solution)/shard_map/ppermute | solution.py:77
  80.5 6.2 %collective-permute-start.2 = (f32[64,256]{1,0:T(8,128)S(1)}, f32[64,256]{1,0:T(8,128)S(1)}, u32[]{:S(2)}, u32[]{:S(2)}) collective-permute-start(f32[64,256]{1,0:T(8,128)S(1)} %get-tuple-element.38), channel_id=1, source_target_pairs={{32,64},{96,128},{160,192},{224,256},{288,320},{352,384},{416,448}... | collective-permute-start | bytes 196616 | tf_op jit(solution)/shard_map/ppermute | solution.py:77
  82.8 6.3 %collective-permute-start.3 = (f32[64,256]{1,0:T(8,128)S(1)}, f32[64,256]{1,0:T(8,128)S(1)}, u32[]{:S(2)}, u32[]{:S(2)}) collective-permute-start(f32[64,256]{1,0:T(8,128)S(1)} %get-tuple-element.39), channel_id=1, source_target_pairs={{8,16},{24,0},{16,8},{0,24},{9,17},{25,1},{17,9},{1,25},{10,18},{2... | collective-permute-start | bytes 196616 | tf_op jit(solution)/shard_map/ppermute | solution.py:77
  91.2 20.4 %all-to-all-start.3 = ((f32[8,64,256]{2,1,0:T(8,128)}), f32[8,64,256]{2,1,0:T(8,128)S(1)}, u32[]{:S(2)}, u32[]{:S(2)}) async-start(f32[8,64,256]{2,1,0:T(8,128)} %get-tuple-element.45), calls=%async_computation.3 | async-start | bytes 1048576 | tf_op jit(solution)/shard_map/all_to_all | solution.py:331
  95.2 13.2 %collective-permute-start.4 = (f32[64,256]{1,0:T(8,128)S(1)}, f32[64,256]{1,0:T(8,128)S(1)}, u32[]{:S(2)}, u32[]{:S(2)}) collective-permute-start(f32[64,256]{1,0:T(8,128)S(1)} %get-tuple-element.42), channel_id=1, source_target_pairs={{1,2},{3,4},{5,6},{7,0},{2,1},{4,3},{6,5},{0,7},{9,10},{11,12},{13... | collective-permute-start | bytes 196616 | tf_op jit(solution)/shard_map/ppermute | solution.py:77
  100.9 7.5 %collective-permute-start.5 = (f32[64,256]{1,0:T(8,128)S(1)}, f32[64,256]{1,0:T(8,128)S(1)}, u32[]{:S(2)}, u32[]{:S(2)}) collective-permute-start(f32[64,256]{1,0:T(8,128)S(1)} %get-tuple-element.43), channel_id=1, source_target_pairs={{32,64},{96,128},{160,192},{224,256},{288,320},{352,384},{416,448}... | collective-permute-start | bytes 196616 | tf_op jit(solution)/shard_map/ppermute | solution.py:77
  105.3 6.3 %collective-permute-start.6 = (f32[64,256]{1,0:T(8,128)S(1)}, f32[64,256]{1,0:T(8,128)S(1)}, u32[]{:S(2)}, u32[]{:S(2)}) collective-permute-start(f32[64,256]{1,0:T(8,128)S(1)} %get-tuple-element.44), channel_id=1, source_target_pairs={{8,16},{24,0},{16,8},{0,24},{9,17},{25,1},{17,9},{1,25},{10,18},{2... | collective-permute-start | bytes 196616 | tf_op jit(solution)/shard_map/ppermute | solution.py:77
  113.6 16.2 %all-to-all-start.4 = ((f32[8,64,256]{2,1,0:T(8,128)}), f32[8,64,256]{2,1,0:T(8,128)S(1)}, u32[]{:S(2)}, u32[]{:S(2)}) async-start(f32[8,64,256]{2,1,0:T(8,128)} %get-tuple-element.50), calls=%async_computation.4 | async-start | bytes 1048576 | tf_op jit(solution)/shard_map/all_to_all | solution.py:331
  117.7 9.3 %collective-permute-start.7 = (f32[64,256]{1,0:T(8,128)S(1)}, f32[64,256]{1,0:T(8,128)S(1)}, u32[]{:S(2)}, u32[]{:S(2)}) collective-permute-start(f32[64,256]{1,0:T(8,128)S(1)} %get-tuple-element.47), channel_id=1, source_target_pairs={{1,2},{3,4},{5,6},{7,0},{2,1},{4,3},{6,5},{0,7},{9,10},{11,12},{13... | collective-permute-start | bytes 196616 | tf_op jit(solution)/shard_map/ppermute | solution.py:77
  120.1 6.9 %collective-permute-start.8 = (f32[64,256]{1,0:T(8,128)S(1)}, f32[64,256]{1,0:T(8,128)S(1)}, u32[]{:S(2)}, u32[]{:S(2)}) collective-permute-start(f32[64,256]{1,0:T(8,128)S(1)} %get-tuple-element.48), channel_id=1, source_target_pairs={{32,64},{96,128},{160,192},{224,256},{288,320},{352,384},{416,448}... | collective-permute-start | bytes 196616 | tf_op jit(solution)/shard_map/ppermute | solution.py:77
  123.1 6.7 %collective-permute-start.9 = (f32[64,256]{1,0:T(8,128)S(1)}, f32[64,256]{1,0:T(8,128)S(1)}, u32[]{:S(2)}, u32[]{:S(2)}) collective-permute-start(f32[64,256]{1,0:T(8,128)S(1)} %get-tuple-element.49), channel_id=1, source_target_pairs={{8,16},{24,0},{16,8},{0,24},{9,17},{25,1},{17,9},{1,25},{10,18},{2... | collective-permute-start | bytes 196616 | tf_op jit(solution)/shard_map/ppermute | solution.py:77

commit v5 on v4

v5 whole, which is shorter than its diff:
```python
import jax
import jax.numpy as jnp
from jax import lax
from jax.experimental import pallas as pl
from jax.experimental.pallas import tpu as pltpu
from jax.sharding import PartitionSpec as P

NEWTON = 6
DG_STEPS = 3
ROWS = 96
EDGE = 8
FLAT = EDGE * EDGE
COLS = 256
FACES = 6
CUBE = 8
GRANT = 16 << 20
BODY = FACES * FLAT
WIDTH = 512
cutoff = 1.0


def shifted(shard, axis, by):
    count = lax.axis_size(axis)
    return lax.ppermute(shard, axis, [(i, (i + by) % count) for i in range(count)])


def split(value):
    high = value.astype(jnp.bfloat16)
    low = (value - high.astype(jnp.float32)).astype(jnp.bfloat16)
    return high, low


def dot3(left, right, dims=(((1,), (0,)), ((), ()))):
    lh, ll = left
    rh, rl = right
    rows = lh.shape[0]

    def one(a, b):
        return lax.dot_general(a, b, dims, preferred_element_type=jnp.float32)

    both = one(jnp.concatenate([lh, ll], axis=0), rh)
    return both[:rows] + (both[rows:] + one(lh, rl))


def exact(left, right, dims=(((1,), (0,)), ((), ()))):
    return lax.dot_general(
        left, right, dims, precision=lax.Precision.HIGHEST, preferred_element_type=jnp.float32
    )


def product(left, right):
    return dot3(split(left), split(right))


def lane_roll(value, by):
    return pltpu.roll(value, by % value.shape[-1], axis=value.ndim - 1)


def lanes(shape):
    return lax.broadcasted_iota(jnp.int32, shape, len(shape) - 1)


SWAPS = (("gz", 1), ("gx", 1), ("gy", 0))
CUBE_PAIRS = (("gx", 0), ("gy", 1), ("gz", 0))
SLOTS = SWAPS + CUBE_PAIRS
AXES = ("gx", "gy", "gz")
FLIPS = (4, 2, 1)


def upper_side(axis, odd):
    return lax.rem(lax.axis_index(axis), 2) == odd


def swapped(shard, axis, odd):
    count = lax.axis_size(axis)
    pairs = [((2 * i + odd) % count, (2 * i + 1 + odd) % count) for i in range(count // 2)]
    return lax.ppermute(shard, axis, pairs + [(b, a) for a, b in pairs])


def place():
    return sum(
        flip * lax.rem(lax.axis_index(axis) + odd, 2) for flip, (axis, odd) in zip(FLIPS, CUBE_PAIRS)
    )


def cubes():
    sizes = [lax.axis_size(axis) for axis in AXES]
    groups = []
    for base in ((i, j, k) for i in range(sizes[0] // 2) for j in range(sizes[1] // 2) for k in range(sizes[2] // 2)):
        group = []
        for spot in range(CUBE):
            x, y, z = [
                (2 * base[n] + CUBE_PAIRS[n][1] + (spot // FLIPS[n]) % 2) % sizes[n] for n in range(3)
            ]
            group.append((x * sizes[1] + y) * sizes[2] + z)
        groups.append(group)
    return groups


def tile_kernel(potential_ref, tile_ref, peak_ref):
    lane = lanes((8, 128))
    potential = potential_ref[...]
    tile = jnp.zeros((8, 128), jnp.float32)
    for y in range(8):
        row = jnp.concatenate([potential_ref[:, y, :], jnp.zeros((8, 120), jnp.float32)], axis=1)
        if y:
            row = lane_roll(row, 16 * y)
        tile = jnp.where((lane >= 16 * y) & (lane < 16 * y + 8), row, tile)
    tile_ref[...] = tile
    peak_ref[...] = jnp.broadcast_to(jnp.max(potential), peak_ref.shape)


def block_kernel(tile_ref, below_ref, peaks_ref, out_ref):
    shape = (8, 128)
    near = lanes(shape) % 16 < 8
    row = lax.broadcasted_iota(jnp.int32, shape, 0)
    block = jnp.where(row == 5, jnp.max(peaks_ref[...]), tile_ref[...])
    block = jnp.where(near, block, lane_roll(below_ref[...], 8))
    out_ref[...] = jnp.broadcast_to(block, out_ref.shape)


def send_traces(ft, value, sent, held_ref, sems):
    right = split(value)
    half = BODY // 2
    traces = dot3(split(ft[half:]), right)
    at = place()
    copies = []
    for n, flip in enumerate(FLIPS):
        held_ref[n] = traces[n * FLAT : (n + 1) * FLAT]
        copies.append(pltpu.make_async_copy(held_ref.at[n], sent[3].at[at ^ flip], sems.at[n]))
        copies[-1].start()
    traces = dot3(split(ft[:half]), right)
    for slot in range(3):
        sent[slot][...] = traces[slot * FLAT : (slot + 1) * FLAT]
    for copy in copies:
        copy.wait()


def basis_kernel(tiles_ref, orbitals_ref, vectors_ref, df_ref, ft_ref, scal_ref, *refs):
    sent, (w_ref, restricted_ref, bt_ref, held_ref, sems) = refs[:-5], refs[-5:]
    gy = lax.axis_index("gy")
    gz = lax.axis_index("gz")
    ny = lax.axis_size("gy")
    nz = lax.axis_size("gz")
    py = lax.rem(gy + ny - 1, ny)
    pz = lax.rem(gz + nz - 1, nz)
    near = lanes((8, 128)) % 16 < 8
    tallest = jnp.max(jnp.max(tiles_ref[...], axis=0)[5:6])
    top = 6.0 + tallest
    centre = (top + cutoff) / 2.0
    half_width = (top - cutoff) / 2.0
    scal_ref[0] = centre
    scal_ref[1] = half_width
    own_x, prior_x = [], []
    for row in (py, gy):
        low = tiles_ref[row * nz + pz]
        high = tiles_ref[row * nz + gz]
        own_x.append(jnp.where(near, low, lane_roll(high, 8)))
        prior_x.append(jnp.where(near, lane_roll(low, -8), high))
    own_x = jnp.concatenate(own_x, axis=1)
    prior_x = jnp.concatenate(prior_x, axis=1)
    planes = {}
    for plane in range(3, 13):
        source, row = (prior_x, plane) if plane < 8 else (own_x, plane - 8)
        planes[plane] = jnp.broadcast_to(source[row : row + 1], (8, 256))
        w_ref[plane - 3] = planes[plane] + (3.0 - centre)
    first_half = lanes((8, 128)) % 16 < 8

    def packed(even, odd):
        return jnp.where(first_half, lane_roll(even, -68)[:, :128], lane_roll(odd, -60)[:, :128])

    inverse = 1.0 / half_width

    def around(value):
        return (
            lane_roll(value, 1) + lane_roll(value, -1) + lane_roll(value, 16) + lane_roll(value, -16)
        )

    def filter_rows(step, carry):
        rows = pl.ds(pl.multiple_of(step * 8, 8), 8)
        start = {p: orbitals_ref[rows, p * 256 : (p + 1) * 256] for p in range(2, 14)}
        once = {}
        for p in range(3, 13):
            total = around(start[p]) + (start[p - 1] + start[p + 1])
            once[p] = (w_ref[p - 3] * start[p] - 0.5 * total) * inverse
        twice = {}
        for p in range(4, 12):
            total = around(once[p]) + (once[p - 1] + once[p + 1])
            twice[p] = (w_ref[p - 3] * once[p] - 0.5 * total) * (2.0 * inverse) - start[p]
        for q in range(4):
            restricted_ref[rows, q * 128 : (q + 1) * 128] = packed(twice[4 + 2 * q], twice[5 + 2 * q])
        return carry

    lax.fori_loop(0, ROWS // 8, filter_rows, 0)
    restricted = restricted_ref[...]
    halves = split(restricted)
    intersection = dot3(halves, halves, (((1,), (1,)), ((), ())))
    sigma = jnp.sqrt(jnp.sum(intersection * intersection))
    identity = (
        lax.broadcasted_iota(jnp.int32, (ROWS, ROWS), 0) == lanes((ROWS, ROWS))
    ).astype(jnp.float32)
    current = intersection / sigma
    factor = 1.5 * identity - 0.5 * current
    current = product(current, factor)
    root = factor
    for step in range(NEWTON - 1):
        factor = 1.5 * identity - 0.5 * product(root, current)
        if step < NEWTON - 2:
            current = product(current, factor)
        root = product(factor, root)
    root = root / jnp.sqrt(sigma)
    basis = dot3(split(root), halves)

    own = jnp.concatenate([packed(planes[4 + 2 * q], planes[5 + 2 * q]) for q in range(4)], axis=1)
    own = own[:1] + 3.0
    cell = lanes((ROWS, WIDTH))
    z = cell % 8
    y = cell // 16 % 8
    x = cell // 128 * 2 + cell // 8 % 2
    odd = x % 2 == 1

    def gate(ok, value):
        return jnp.where(ok, value, 0.0)

    total = gate(z > 0, lane_roll(basis, 1)) + gate(z < 7, lane_roll(basis, -1))
    total = total + gate(y > 0, lane_roll(basis, 16)) + gate(y < 7, lane_roll(basis, -16))
    total = total + jnp.where(odd, lane_roll(basis, 8), lane_roll(basis, -8))
    total = total + gate(
        (x > 0) & (x < 7), jnp.where(odd, lane_roll(basis, -120), lane_roll(basis, 120))
    )
    applied = own * basis - 0.5 * total
    diagonal = dot3(split(basis), split(applied), (((1,), (1,)), ((), ())))

    bt_ref[...] = jnp.concatenate([basis, jnp.zeros((128 - ROWS, WIDTH), jnp.float32)], axis=0).T
    lower = (
        jnp.concatenate([bt_ref[yy * 16 : yy * 16 + 8] for yy in range(8)], axis=0),
        jnp.concatenate([bt_ref[q * 128 : q * 128 + 16] for q in range(4)], axis=0),
        bt_ref[pl.ds(0, FLAT, stride=8)],
    )
    upper = (
        jnp.concatenate([bt_ref[392 + yy * 16 : 400 + yy * 16] for yy in range(8)], axis=0),
        jnp.concatenate([bt_ref[q * 128 + 112 : q * 128 + 128] for q in range(4)], axis=0),
        bt_ref[pl.ds(7, FLAT, stride=8)],
    )
    pieces = [
        jnp.where(upper_side(axis, odd), upper[AXES.index(axis)], lower[AXES.index(axis)])
        for axis, odd in SLOTS
    ]
    faces_t = jnp.concatenate(pieces, axis=0)
    ft = faces_t[:, :ROWS]
    ft_ref[...] = ft
    df_ref[:, :BODY] = -0.5 * faces_t.T[:ROWS]
    df_ref[:, BODY : BODY + ROWS] = diagonal
    df_ref[:, BODY + ROWS :] = jnp.zeros((ROWS, WIDTH - BODY - ROWS), jnp.float32)
    send_traces(ft, vectors_ref[...], sent, held_ref, sems)


def step_kernel(first, last, scal_ref, df_ref, ft_ref, now_ref, prior_ref, *refs):
    swap_refs, cube_ref, out_ref, rest = refs[:3], refs[3], refs[4], refs[5:]
    now = now_ref[...]
    at = place()
    halos = [ref[...] for ref in swap_refs] + [cube_ref[at ^ flip] for flip in FLIPS]
    first_half = halos[:4]
    second_half = halos[4:] + [now, jnp.zeros((WIDTH - BODY - ROWS, COLS), jnp.float32)]
    result = dot3(
        split(df_ref[:, : WIDTH // 2]), split(jnp.concatenate(first_half, axis=0))
    ) + dot3(split(df_ref[:, WIDTH // 2 :]), split(jnp.concatenate(second_half, axis=0)))
    centre, half_width = scal_ref[0], scal_ref[1]
    following = (result - centre * now) / half_width
    if not first:
        following = 2.0 * following - prior_ref[...]
    out_ref[...] = following
    if not last:
        send_traces(ft_ref[...], following, rest[:4], rest[4], rest[5])


def vmem():
    return pl.BlockSpec(memory_space=pltpu.VMEM)


def smem():
    return pl.BlockSpec(memory_space=pltpu.SMEM)


def of(*shape):
    return jax.ShapeDtypeStruct(shape, jnp.float32)


def call(kernel, name, out_shape, in_specs, out_specs, scratch=()):
    return pl.pallas_call(
        kernel,
        out_shape=out_shape,
        in_specs=in_specs,
        out_specs=out_specs,
        scratch_shapes=list(scratch),
        compiler_params=pltpu.CompilerParams(vmem_limit_bytes=GRANT),
        name=name,
    )


def per_device(orbitals, potential, coefficients):
    f32 = jnp.float32
    nx = lax.axis_size("gx")
    plane = lax.axis_size("gy") * lax.axis_size("gz")
    tile, peak = call(
        tile_kernel, "tile", (of(8, 128), of(nx, 1, 128)), [vmem()], (vmem(), vmem())
    )(potential)
    below = shifted(tile, "gx", 1)
    peaks = lax.all_to_all(peak, "gx", 0, 0)
    block = call(block_kernel, "block", of(plane, 8, 128), [vmem()] * 3, vmem())(tile, below, peaks)
    tiles = lax.all_to_all(block, ("gy", "gz"), 0, 0)
    start = coefficients.reshape(ROWS, COLS)
    sent_shapes = (of(FLAT, COLS),) * 3 + (of(CUBE, FLAT, COLS),)
    sent_specs = (vmem(),) * 3 + (pl.BlockSpec(memory_space=pltpu.HBM),)
    staging = [pltpu.VMEM((3, FLAT, COLS), f32), pltpu.SemaphoreType.DMA((3,))]
    df, ft, scal, *sent = call(
        basis_kernel,
        "basis",
        (of(ROWS, WIDTH), of(BODY, ROWS), of(2)) + sent_shapes,
        [vmem()] * 3,
        (vmem(), vmem(), smem()) + sent_specs,
        [pltpu.VMEM((10, 8, 256), f32), pltpu.VMEM((ROWS, WIDTH), f32), pltpu.VMEM((WIDTH, 128), f32)]
        + staging,
    )(tiles, orbitals.reshape(ROWS, -1), start)

    groups = cubes()
    prior, now = start, start
    for step in range(DG_STEPS):
        halos = [swapped(trace, *pairing) for trace, pairing in zip(sent, SWAPS)]
        halos.append(lax.all_to_all(sent[3], AXES, 0, 0, axis_index_groups=groups))
        last = step == DG_STEPS - 1

        def body(*refs, step=step, last=last):
            step_kernel(step == 0, last, *refs)

        following, *sent = call(
            body,
            f"step{step}",
            (of(ROWS, COLS),) + (() if last else sent_shapes),
            [smem()] + [vmem()] * 8,
            (vmem(),) + (() if last else sent_specs),
            () if last else staging,
        )(scal, df, ft, now, prior, *halos)
        prior, now = now, following
    return now.reshape(coefficients.shape)


def solution(mesh):
    placed = (P("gx", "gy", "gz", None, None), P("gx", "gy", "gz"), P("gx", "gy", "gz", None, None))
    return jax.shard_map(
        per_device,
        mesh=mesh,
        in_specs=placed,
        out_specs=P("gx", "gy", "gz", None, None),
        check_vma=False,
    )
```

time: 132 us -> 133 us (level)
  starting transfers between devices: 68.6 us -> 77.1 us
  blocking collectives: 24.3 us -> 16.5 us
    all_to_all x1, starting transfers between devices: 19.9 us -> 29.3 us  [per_device(): peaks = lax.all_to_all(peak, 'gx', 0, 0)]
    all_to_all x1, blocking collectives: 24.3 us -> 16.5 us  [per_device(): tiles = lax.all_to_all(block, ('gy', 'gz'), 0, 0)]
    ppermute x9, waiting for transfers between devices: 8.76 us -> 2.62 us  [swapped(): return lax.ppermute(shard, axis, pairs + [(b, a) for a, b in pairs])]
    all_to_all x1, waiting for transfers between devices: 10.1 us -> 15.4 us  [per_device(): peaks = lax.all_to_all(peak, 'gx', 0, 0)]
    all_to_all x3, starting transfers between devices: 13.9 us -> 10.5 us  [per_device(): halos.append(lax.all_to_all(sent[3], AXES, 0, 0, axis_index_groups=groups))]
    ppermute x9, starting transfers between devices: 31.7 us -> 34.2 us  [swapped(): return lax.ppermute(shard, axis, pairs + [(b, a) for a, b in pairs])]
    unnamed x6 -> x8, local copies, waits for them, and re-layouts: 2.17 us -> 3.06 us
    pallas_call x7 -> x6, Pallas kernels: 14.4 us -> 14.4 us  [the longest x1 8.56 us: per_device(): call(basis_kernel, 'basis', (of(ROWS, WIDTH), of(BODY, ROWS), of(2)) + se...]
  transfers between devices with their start and end apart: 14 -> 14, of which waited for: 6 -> 9; matrix products, arithmetic and copies ran while one was open for 0% -> 0% of each run, Pallas kernels for 3% -> 0%
where the time goes in v5:
time: 133 us; the launch traced here: 132 us
  starting transfers between devices  77.1 us (58%)
  waiting for transfers between devices  20.7 us (16%)
  blocking collectives  16.5 us (12%)
  Pallas kernels  14.4 us (11%)
  local copies, waits for them, and re-layouts  3.06 us (2%)
    ppermute x9, starting transfers between devices, swapped(): return lax.ppermute(shard, axis, pairs + [(b, a) for a, b in pairs])  34.2 us
    all_to_all x1, starting transfers between devices, per_device(): peaks = lax.all_to_all(peak, 'gx', 0, 0)  29.3 us
    all_to_all x1, blocking collectives, per_device(): tiles = lax.all_to_all(block, ('gy', 'gz'), 0, 0)  16.5 us
    all_to_all x1, waiting for transfers between devices, per_device(): peaks = lax.all_to_all(peak, 'gx', 0, 0)  15.4 us
    all_to_all x3, starting transfers between devices, per_device(): halos.append(lax.all_to_all(sent[3], AXES, 0, 0, axis_index_groups=groups))  10.5 us
    pallas_call x1, Pallas kernels, per_device(): call(basis_kernel, 'basis', (of(ROWS, WIDTH), of(BODY, ROWS), of(2)) + se...  8.56 us
    pallas_call x3, Pallas kernels, per_device(): call(body, f'step{step}', (of(ROWS, COLS),) + (() if last else sent_shape...  4.93 us
    ppermute x1, starting transfers between devices, shifted(): lax.ppermute(shard, axis, [(i, (i + by) % count) for i in range(count)])  3.14 us
  transfers between devices with their start and end apart: 14, of which 9 were waited for; matrix products, arithmetic and copies ran while one was open for 0% of the time, Pallas kernels for 0%

profile of v5, /device:TPU:1, one launch (start us, length us, event | category | flops | bytes accessed | tf_op | source)
XLA Modules:
  0.0 131.9 jit_solution(15394525473668509340)
XLA Ops:
  1.5 29.3 %all-to-all-start = ((f32[32,1,128]{2,1,0:T(1,128)}), f32[32,1,128]{2,1,0:T(1,128)S(1)}, u32[]{:S(2)}, u32[]{:S(2)}) async-start(f32[32,1,128]{2,1,0:T(1,128)} %get-tuple-element.25), calls=%async_computation | async-start | bytes 32768 | tf_op jit(solution)/shard_map/all_to_all | solution.py:309
  30.8 3.1 %collective-permute-start = (f32[8,128]{1,0:T(8,128)S(1)}, f32[8,128]{1,0:T(8,128)S(1)}, u32[]{:S(2)}, u32[]{:S(2)}) collective-permute-start(f32[8,128]{1,0:T(8,128)S(1)} %get-tuple-element.24.tile_ref), channel_id=1, source_target_pairs={{0,32},{32,64},{64,96},{96,128},{128,160},{160,192},{192,224},{224... | collective-permute-start | bytes 12296 | tf_op jit(solution)/shard_map/ppermute | solution.py:24
  33.9 2.7 %collective-permute-done.below_ref = f32[8,128]{1,0:T(8,128)S(1)} collective-permute-done((f32[8,128]{1,0:T(8,128)S(1)}, f32[8,128]{1,0:T(8,128)S(1)}, u32[]{:S(2)}, u32[]{:S(2)}) %collective-permute-start) | collective-permute-done | bytes 4128 | tf_op jit(solution)/shard_map/ppermute | solution.py:24
  36.6 15.4 %all-to-all-done.peaks_ref = f32[32,1,128]{2,1,0:T(1,128)S(1)} async-done(((f32[32,1,128]{2,1,0:T(1,128)}), f32[32,1,128]{2,1,0:T(1,128)S(1)}, u32[]{:S(2)}, u32[]{:S(2)}) %all-to-all-start) | async-done | bytes 16416 | tf_op jit(solution)/shard_map/all_to_all | solution.py:309
  52.1 16.5 %all_to_all.25.tiles_ref = f32[32,8,128]{2,1,0:T(8,128)S(1)} all-to-all(f32[32,8,128]{2,1,0:T(8,128)S(1)} %block.1), channel_id=1, replica_groups=mesh['gx'=32,'gy'=4,'gz'=8] {'gy','gz'}, dimensions={0} | all-to-all | bytes 262144 | tf_op jit(solution)/shard_map/all_to_all | solution.py:311
  68.7 0.9 copy-done
  69.5 1.4 %copy-done.2 = f32[1,1,1,96,4096]{4,3,2,1,0:T(8,128)S(1)} copy-done((f32[1,1,1,96,4096]{4,3,2,1,0:T(8,128)S(1)}, f32[1,1,1,96,4096]{4,3,2,1,0:T(8,128)}, u32[]{:S(2)}) %copy-start.2) | copy-done | bytes 1572888
  71.0 8.6 %basis.1 = (f32[96,512]{1,0:T(8,128)S(1)}, f32[384,96]{1,0:T(8,128)S(1)}, f32[2]{0:T(128)S(1)}, f32[64,256]{1,0:T(8,128)S(1)}, f32[64,256]{1,0:T(8,128)S(1)}, /*...) custom-call(f32[32,8,128]{2,1,0:T(8,128)S(1)} %all_to_all.25.tiles_ref, f32[96,4096]{1,0:T(8,128)S(1)} %bitcast.7, ...), custom_call_target="tpu_custom_call" | custom-call | tf_op jit(solution)/shard_map/basis/pallas_call | solution.py:316
  79.5 3.5 %all-to-all-start.2 = ((f32[8,64,256]{2,1,0:T(8,128)}), f32[8,64,256]{2,1,0:T(8,128)S(1)}, u32[]{:S(2)}, u32[]{:S(2)}) async-start(f32[8,64,256]{2,1,0:T(8,128)} %get-tuple-element.32), calls=%async_computation.2 | async-start | bytes 1048576 | tf_op jit(solution)/shard_map/all_to_all | solution.py:330
  83.0 4.0 %collective-permute-start.1 = (f32[64,256]{1,0:T(8,128)S(1)}, f32[64,256]{1,0:T(8,128)S(1)}, u32[]{:S(2)}, u32[]{:S(2)}) collective-permute-start(f32[64,256]{1,0:T(8,128)S(1)} %get-tuple-element.29), channel_id=1, source_target_pairs={{1,2},{3,4},{5,6},{7,0},{2,1},{4,3},{6,5},{0,7},{9,10},{11,12},{13... | collective-permute-start | bytes 196616 | tf_op jit(solution)/shard_map/ppermute | solution.py:77
  87.0 2.7 %collective-permute-start.2 = (f32[64,256]{1,0:T(8,128)S(1)}, f32[64,256]{1,0:T(8,128)S(1)}, u32[]{:S(2)}, u32[]{:S(2)}) collective-permute-start(f32[64,256]{1,0:T(8,128)S(1)} %get-tuple-element.30), channel_id=1, source_target_pairs={{32,64},{96,128},{160,192},{224,256},{288,320},{352,384},{416,448}... | collective-permute-start | bytes 196616 | tf_op jit(solution)/shard_map/ppermute | solution.py:77
  89.7 3.4 %collective-permute-start.3 = (f32[64,256]{1,0:T(8,128)S(1)}, f32[64,256]{1,0:T(8,128)S(1)}, u32[]{:S(2)}, u32[]{:S(2)}) collective-permute-start(f32[64,256]{1,0:T(8,128)S(1)} %get-tuple-element.31), channel_id=1, source_target_pairs={{0,8},{16,24},{8,0},{24,16},{1,9},{17,25},{9,1},{25,17},{2,10},{18... | collective-permute-start | bytes 196616 | tf_op jit(solution)/shard_map/ppermute | solution.py:77
  93.9 1.7 %step0.1 = (f32[96,256]{1,0:T(8,128)S(1)}, f32[64,256]{1,0:T(8,128)S(1)}, f32[64,256]{1,0:T(8,128)S(1)}, f32[64,256]{1,0:T(8,128)S(1)}, f32[8,64,256]{2,1,0:T(8,128)}) custom-call(f32[2]{0:T(128)S(1)} %get-tuple-element.26.refs_0_, f32[96,512]{1,0:T(8,128)S(1)} %get-tuple-element.27.refs_1_, f32[384,96]{1,0:T(8,128)S(1)} %get-tuple-element.28.refs_2_, ...), custom_call_target="tpu_custom_call" | custom-call | tf_op jit(solution)/shard_map/step0/pallas_call | solution.py:336
  95.7 3.5 %all-to-all-start.3 = ((f32[8,64,256]{2,1,0:T(8,128)}), f32[8,64,256]{2,1,0:T(8,128)S(1)}, u32[]{:S(2)}, u32[]{:S(2)}) async-start(f32[8,64,256]{2,1,0:T(8,128)} %get-tuple-element.37), calls=%async_computation.3 | async-start | bytes 1048576 | tf_op jit(solution)/shard_map/all_to_all | solution.py:330
  99.2 6.8 %collective-permute-start.4 = (f32[64,256]{1,0:T(8,128)S(1)}, f32[64,256]{1,0:T(8,128)S(1)}, u32[]{:S(2)}, u32[]{:S(2)}) collective-permute-start(f32[64,256]{1,0:T(8,128)S(1)} %get-tuple-element.34), channel_id=1, source_target_pairs={{1,2},{3,4},{5,6},{7,0},{2,1},{4,3},{6,5},{0,7},{9,10},{11,12},{13... | collective-permute-start | bytes 196616 | tf_op jit(solution)/shard_map/ppermute | solution.py:77
  106.1 3.4 %collective-permute-start.5 = (f32[64,256]{1,0:T(8,128)S(1)}, f32[64,256]{1,0:T(8,128)S(1)}, u32[]{:S(2)}, u32[]{:S(2)}) collective-permute-start(f32[64,256]{1,0:T(8,128)S(1)} %get-tuple-element.35), channel_id=1, source_target_pairs={{32,64},{96,128},{160,192},{224,256},{288,320},{352,384},{416,448}... | collective-permute-start | bytes 196616 | tf_op jit(solution)/shard_map/ppermute | solution.py:77
  109.5 2.6 %collective-permute-start.6 = (f32[64,256]{1,0:T(8,128)S(1)}, f32[64,256]{1,0:T(8,128)S(1)}, u32[]{:S(2)}, u32[]{:S(2)}) collective-permute-start(f32[64,256]{1,0:T(8,128)S(1)} %get-tuple-element.36), channel_id=1, source_target_pairs={{0,8},{16,24},{8,0},{24,16},{1,9},{17,25},{9,1},{25,17},{2,10},{18... | collective-permute-start | bytes 196616 | tf_op jit(solution)/shard_map/ppermute | solution.py:77
  113.0 1.7 %step1.1 = (f32[96,256]{1,0:T(8,128)S(1)}, f32[64,256]{1,0:T(8,128)S(1)}, f32[64,256]{1,0:T(8,128)S(1)}, f32[64,256]{1,0:T(8,128)S(1)}, f32[8,64,256]{2,1,0:T(8,128)}) custom-call(f32[2]{0:T(128)S(1)} %get-tuple-element.26.refs_0_, f32[96,512]{1,0:T(8,128)S(1)} %get-tuple-element.27.refs_1_, f32[384,96]{1,0:T(8,128)S(1)} %get-tuple-element.28.refs_2_, ...), custom_call_target="tpu_custom_call" | custom-call | tf_op jit(solution)/shard_map/step1/pallas_call | solution.py:336
  114.8 3.5 %all-to-all-start.4 = ((f32[8,64,256]{2,1,0:T(8,128)}), f32[8,64,256]{2,1,0:T(8,128)S(1)}, u32[]{:S(2)}, u32[]{:S(2)}) async-start(f32[8,64,256]{2,1,0:T(8,128)} %get-tuple-element.42), calls=%async_computation.4 | async-start | bytes 1048576 | tf_op jit(solution)/shard_map/all_to_all | solution.py:330
  118.3 4.1 %collective-permute-start.7 = (f32[64,256]{1,0:T(8,128)S(1)}, f32[64,256]{1,0:T(8,128)S(1)}, u32[]{:S(2)}, u32[]{:S(2)}) collective-permute-start(f32[64,256]{1,0:T(8,128)S(1)} %get-tuple-element.39), channel_id=1, source_target_pairs={{1,2},{3,4},{5,6},{7,0},{2,1},{4,3},{6,5},{0,7},{9,10},{11,12},{13... | collective-permute-start | bytes 196616 | tf_op jit(solution)/shard_map/ppermute | solution.py:77
  122.4 3.7 %collective-permute-start.8 = (f32[64,256]{1,0:T(8,128)S(1)}, f32[64,256]{1,0:T(8,128)S(1)}, u32[]{:S(2)}, u32[]{:S(2)}) collective-permute-start(f32[64,256]{1,0:T(8,128)S(1)} %get-tuple-element.40), channel_id=1, source_target_pairs={{32,64},{96,128},{160,192},{224,256},{288,320},{352,384},{416,448}... | collective-permute-start | bytes 196616 | tf_op jit(solution)/shard_map/ppermute | solution.py:77
  126.2 3.4 %collective-permute-start.9 = (f32[64,256]{1,0:T(8,128)S(1)}, f32[64,256]{1,0:T(8,128)S(1)}, u32[]{:S(2)}, u32[]{:S(2)}) collective-permute-start(f32[64,256]{1,0:T(8,128)S(1)} %get-tuple-element.41), channel_id=1, source_target_pairs={{0,8},{16,24},{8,0},{24,16},{1,9},{17,25},{9,1},{25,17},{2,10},{18... | collective-permute-start | bytes 196616 | tf_op jit(solution)/shard_map/ppermute | solution.py:77
  129.6 0.9 collective-permute-done.9.refs_7_
  130.4 1.4 %step2.1 = f32[96,256]{1,0:T(8,128)} custom-call(f32[2]{0:T(128)S(1)} %get-tuple-element.26.refs_0_, f32[96,512]{1,0:T(8,128)S(1)} %get-tuple-element.27.refs_1_, f32[384,96]{1,0:T(8,128)S(1)} %get-tuple-element.28.refs_2_, f32[96,256]{1,0:T(8,128)S(1)} %get-tuple-element.38.refs_3_, f32[96,256]{1,0:T(8,128)S(1)} %get-tuple-element.33.refs_3_.refs_4_, ...), custom_call_target="tpu_custom_call" | custom-call | tf_op jit(solution)/shard_map/step2/pallas_call | solution.py:336
  (19 shorter events, 3.4 us)
Async XLA Ops:
  0.0 0.8 copy-start.3
  1.5 50.5 %all-to-all-start = ((f32[32,1,128]{2,1,0:T(1,128)}), f32[32,1,128]{2,1,0:T(1,128)S(1)}, u32[]{:S(2)}, u32[]{:S(2)}) async-start(f32[32,1,128]{2,1,0:T(1,128)} %get-tuple-element.25), calls=%async_computation | async-start | bytes 32768 | tf_op jit(solution)/shard_map/all_to_all | solution.py:309
  30.8 5.9 %collective-permute-start = (f32[8,128]{1,0:T(8,128)S(1)}, f32[8,128]{1,0:T(8,128)S(1)}, u32[]{:S(2)}, u32[]{:S(2)}) collective-permute-start(f32[8,128]{1,0:T(8,128)S(1)} %get-tuple-element.24.tile_ref), channel_id=1, source_target_pairs={{0,32},{32,64},{64,96},{96,128},{128,160},{160,192},{192,224},{224... | collective-permute-start | bytes 12296 | tf_op jit(solution)/shard_map/ppermute | solution.py:24
  52.1 41.8 %copy-start.1 = (f32[1,1,1,96,256]{4,3,2,1,0:T(8,128)S(1)}, f32[1,1,1,96,256]{4,3,2,1,0:T(8,128)}, u32[]{:S(2)}) copy-start(f32[1,1,1,96,256]{4,3,2,1,0:T(8,128)} %param.5) | copy-start | bytes 294916
  68.6 0.9 copy-start
  69.5 1.4 %copy-start.2 = (f32[1,1,1,96,4096]{4,3,2,1,0:T(8,128)S(1)}, f32[1,1,1,96,4096]{4,3,2,1,0:T(8,128)}, u32[]{:S(2)}) copy-start(f32[1,1,1,96,4096]{4,3,2,1,0:T(8,128)} %param.3) | copy-start | bytes 4718596
  79.5 14.4 %all-to-all-start.2 = ((f32[8,64,256]{2,1,0:T(8,128)}), f32[8,64,256]{2,1,0:T(8,128)S(1)}, u32[]{:S(2)}, u32[]{:S(2)}) async-start(f32[8,64,256]{2,1,0:T(8,128)} %get-tuple-element.32), calls=%async_computation.2 | async-start | bytes 1048576 | tf_op jit(solution)/shard_map/all_to_all | solution.py:330
  83.0 10.1 %collective-permute-start.1 = (f32[64,256]{1,0:T(8,128)S(1)}, f32[64,256]{1,0:T(8,128)S(1)}, u32[]{:S(2)}, u32[]{:S(2)}) collective-permute-start(f32[64,256]{1,0:T(8,128)S(1)} %get-tuple-element.29), channel_id=1, source_target_pairs={{1,2},{3,4},{5,6},{7,0},{2,1},{4,3},{6,5},{0,7},{9,10},{11,12},{13... | collective-permute-start | bytes 196616 | tf_op jit(solution)/shard_map/ppermute | solution.py:77
  87.0 6.5 %collective-permute-start.2 = (f32[64,256]{1,0:T(8,128)S(1)}, f32[64,256]{1,0:T(8,128)S(1)}, u32[]{:S(2)}, u32[]{:S(2)}) collective-permute-start(f32[64,256]{1,0:T(8,128)S(1)} %get-tuple-element.30), channel_id=1, source_target_pairs={{32,64},{96,128},{160,192},{224,256},{288,320},{352,384},{416,448}... | collective-permute-start | bytes 196616 | tf_op jit(solution)/shard_map/ppermute | solution.py:77
  89.7 4.3 %collective-permute-start.3 = (f32[64,256]{1,0:T(8,128)S(1)}, f32[64,256]{1,0:T(8,128)S(1)}, u32[]{:S(2)}, u32[]{:S(2)}) collective-permute-start(f32[64,256]{1,0:T(8,128)S(1)} %get-tuple-element.31), channel_id=1, source_target_pairs={{0,8},{16,24},{8,0},{24,16},{1,9},{17,25},{9,1},{25,17},{2,10},{18... | collective-permute-start | bytes 196616 | tf_op jit(solution)/shard_map/ppermute | solution.py:77
  95.7 17.3 %all-to-all-start.3 = ((f32[8,64,256]{2,1,0:T(8,128)}), f32[8,64,256]{2,1,0:T(8,128)S(1)}, u32[]{:S(2)}, u32[]{:S(2)}) async-start(f32[8,64,256]{2,1,0:T(8,128)} %get-tuple-element.37), calls=%async_computation.3 | async-start | bytes 1048576 | tf_op jit(solution)/shard_map/all_to_all | solution.py:330
  99.2 13.1 %collective-permute-start.4 = (f32[64,256]{1,0:T(8,128)S(1)}, f32[64,256]{1,0:T(8,128)S(1)}, u32[]{:S(2)}, u32[]{:S(2)}) collective-permute-start(f32[64,256]{1,0:T(8,128)S(1)} %get-tuple-element.34), channel_id=1, source_target_pairs={{1,2},{3,4},{5,6},{7,0},{2,1},{4,3},{6,5},{0,7},{9,10},{11,12},{13... | collective-permute-start | bytes 196616 | tf_op jit(solution)/shard_map/ppermute | solution.py:77
  106.1 6.5 %collective-permute-start.5 = (f32[64,256]{1,0:T(8,128)S(1)}, f32[64,256]{1,0:T(8,128)S(1)}, u32[]{:S(2)}, u32[]{:S(2)}) collective-permute-start(f32[64,256]{1,0:T(8,128)S(1)} %get-tuple-element.35), channel_id=1, source_target_pairs={{32,64},{96,128},{160,192},{224,256},{288,320},{352,384},{416,448}... | collective-permute-start | bytes 196616 | tf_op jit(solution)/shard_map/ppermute | solution.py:77
  109.5 3.5 %collective-permute-start.6 = (f32[64,256]{1,0:T(8,128)S(1)}, f32[64,256]{1,0:T(8,128)S(1)}, u32[]{:S(2)}, u32[]{:S(2)}) collective-permute-start(f32[64,256]{1,0:T(8,128)S(1)} %get-tuple-element.36), channel_id=1, source_target_pairs={{0,8},{16,24},{8,0},{24,16},{1,9},{17,25},{9,1},{25,17},{2,10},{18... | collective-permute-start | bytes 196616 | tf_op jit(solution)/shard_map/ppermute | solution.py:77
  114.8 15.7 %all-to-all-start.4 = ((f32[8,64,256]{2,1,0:T(8,128)}), f32[8,64,256]{2,1,0:T(8,128)S(1)}, u32[]{:S(2)}, u32[]{:S(2)}) async-start(f32[8,64,256]{2,1,0:T(8,128)} %get-tuple-element.42), calls=%async_computation.4 | async-start | bytes 1048576 | tf_op jit(solution)/shard_map/all_to_all | solution.py:330
  118.3 11.3 %collective-permute-start.7 = (f32[64,256]{1,0:T(8,128)S(1)}, f32[64,256]{1,0:T(8,128)S(1)}, u32[]{:S(2)}, u32[]{:S(2)}) collective-permute-start(f32[64,256]{1,0:T(8,128)S(1)} %get-tuple-element.39), channel_id=1, source_target_pairs={{1,2},{3,4},{5,6},{7,0},{2,1},{4,3},{6,5},{0,7},{9,10},{11,12},{13... | collective-permute-start | bytes 196616 | tf_op jit(solution)/shard_map/ppermute | solution.py:77
  122.4 7.1 %collective-permute-start.8 = (f32[64,256]{1,0:T(8,128)S(1)}, f32[64,256]{1,0:T(8,128)S(1)}, u32[]{:S(2)}, u32[]{:S(2)}) collective-permute-start(f32[64,256]{1,0:T(8,128)S(1)} %get-tuple-element.40), channel_id=1, source_target_pairs={{32,64},{96,128},{160,192},{224,256},{288,320},{352,384},{416,448}... | collective-permute-start | bytes 196616 | tf_op jit(solution)/shard_map/ppermute | solution.py:77
  126.2 4.3 %collective-permute-start.9 = (f32[64,256]{1,0:T(8,128)S(1)}, f32[64,256]{1,0:T(8,128)S(1)}, u32[]{:S(2)}, u32[]{:S(2)}) collective-permute-start(f32[64,256]{1,0:T(8,128)S(1)} %get-tuple-element.41), channel_id=1, source_target_pairs={{0,8},{16,24},{8,0},{24,16},{1,9},{17,25},{9,1},{25,17},{2,10},{18... | collective-permute-start | bytes 196616 | tf_op jit(solution)/shard_map/ppermute | solution.py:77

commit v6 on v4

--- a/solution.py
+++ b/solution.py
@@ -61,9 +61,10 @@
     return lax.broadcasted_iota(jnp.int32, shape, len(shape) - 1)
 
 
-SWAPS = (("gz", 1), ("gx", 1), ("gy", 1))
+SWAPS = (("gz", 1), ("gx", 1), ("gy", 0))
+CUBE_PAIRS = (("gx", 0), ("gy", 1), ("gz", 0))
+SLOTS = SWAPS + CUBE_PAIRS
 AXES = ("gx", "gy", "gz")
-SLOTS = SWAPS + tuple((axis, 0) for axis in AXES)
 FLIPS = (4, 2, 1)
 
 
@@ -78,22 +79,23 @@
 
 
 def place():
-    return sum(flip * lax.rem(lax.axis_index(axis), 2) for flip, axis in zip(FLIPS, AXES))
+    return sum(
+        flip * lax.rem(lax.axis_index(axis) + odd, 2) for flip, (axis, odd) in zip(FLIPS, CUBE_PAIRS)
+    )
 
 
 def cubes():
-    nx, ny, nz = (lax.axis_size(axis) for axis in AXES)
-    return [
-        [
-            ((2 * i + a) * ny + 2 * j + b) * nz + 2 * k + c
-            for a in range(2)
-            for b in range(2)
-            for c in range(2)
-        ]
-        for i in range(nx // 2)
-        for j in range(ny // 2)
-        for k in range(nz // 2)
-    ]
+    sizes = [lax.axis_size(axis) for axis in AXES]
+    groups = []
+    for base in ((i, j, k) for i in range(sizes[0] // 2) for j in range(sizes[1] // 2) for k in range(sizes[2] // 2)):
+        group = []
+        for spot in range(CUBE):
+            x, y, z = [
+                (2 * base[n] + CUBE_PAIRS[n][1] + (spot // FLIPS[n]) % 2) % sizes[n] for n in range(3)
+            ]
+            group.append((x * sizes[1] + y) * sizes[2] + z)
+        groups.append(group)
+    return groups
 
 
 def tile_kernel(potential_ref, out_ref):
@@ -162,23 +164,26 @@
     lax.fori_loop(0, ROWS // 8, filter_rows, 0)
 
 
-def store_traces(ft, value, *refs):
+def send_traces(ft, value, sent, held_ref, sems):
     right = split(value)
     half = BODY // 2
-    for part in range(2):
-        traces = dot3(split(ft[part * half : (part + 1) * half]), right)
-        at = place()
-        for slot in range(3):
-            block = traces[slot * FLAT : (slot + 1) * FLAT]
-            if part == 0:
-                refs[slot][...] = block
-            else:
-                refs[3][at ^ FLIPS[slot]] = block
+    traces = dot3(split(ft[half:]), right)
+    at = place()
+    copies = []
+    for n, flip in enumerate(FLIPS):
+        held_ref[n] = traces[n * FLAT : (n + 1) * FLAT]
+        copies.append(pltpu.make_async_copy(held_ref.at[n], sent[3].at[at ^ flip], sems.at[n]))
+        copies[-1].start()
+    traces = dot3(split(ft[:half]), right)
+    for slot in range(3):
+        sent[slot][...] = traces[slot * FLAT : (slot + 1) * FLAT]
+    for copy in copies:
+        copy.wait()
 
 
 def basis_kernel(peaks_ref, u0_ref, u1_ref, u2_ref, own_ref, vectors_ref,
                  df_ref, ft_ref, scal_ref, *refs):
-    sent, bt_ref = refs[:-1], refs[-1]
+    sent, (bt_ref, held_ref, sems) = refs[:-3], refs[-3:]
     top = 6.0 + jnp.max(peaks_ref[...])
     centre = (top + cutoff) / 2.0
     half_width = (top - cutoff) / 2.0
@@ -246,11 +251,11 @@
     df_ref[:, :BODY] = -0.5 * faces_t.T[:ROWS]
     df_ref[:, BODY : BODY + ROWS] = diagonal
     df_ref[:, BODY + ROWS :] = jnp.zeros((ROWS, WIDTH - BODY - ROWS), jnp.float32)
-    store_traces(ft, vectors_ref[...], *sent)
+    send_traces(ft, vectors_ref[...], sent, held_ref, sems)
 
 
 def step_kernel(first, last, scal_ref, df_ref, ft_ref, now_ref, prior_ref, *refs):
-    swap_refs, cube_ref, out_ref, sent = refs[:3], refs[3], refs[4], refs[5:]
+    swap_refs, cube_ref, out_ref, rest = refs[:3], refs[3], refs[4], refs[5:]
     now = now_ref[...]
     at = place()
     halos = [ref[...] for ref in swap_refs] + [cube_ref[at ^ flip] for flip in FLIPS]
@@ -265,7 +270,7 @@
         following = 2.0 * following - prior_ref[...]
     out_ref[...] = following
     if not last:
-        store_traces(ft_ref[...], following, *sent)
+        send_traces(ft_ref[...], following, rest[:4], rest[4], rest[5])
 
 
 def vmem():
@@ -278,50 +283,50 @@
 
 def of(*shape):
     return jax.ShapeDtypeStruct(shape, jnp.float32)
+
+
+def call(kernel, name, out_shape, in_specs, out_specs, scratch=()):
+    return pl.pallas_call(
+        kernel,
+        out_shape=out_shape,
+        in_specs=in_specs,
+        out_specs=out_specs,
+        scratch_shapes=list(scratch),
+        compiler_params=pltpu.CompilerParams(vmem_limit_bytes=GRANT),
+        name=name,
+    )
 
 
 def per_device(orbitals, potential, coefficients):
     f32 = jnp.float32
     nx = lax.axis_size("gx")
     plane = lax.axis_size("gy") * lax.axis_size("gz")
-    tile = pl.pallas_call(
-        tile_kernel,
-        out_shape=of(plane, 8, 128),
-        in_specs=[vmem()],
-        out_specs=vmem(),
-        compiler_params=pltpu.CompilerParams(vmem_limit_bytes=GRANT),
-        name="tile",
-    )(potential)
+    tile = call(tile_kernel, "tile", of(plane, 8, 128), [vmem()], vmem())(potential)
     tiles = lax.all_to_all(tile, ("gy", "gz"), 0, 0)
-    peak, wide = pl.pallas_call(
-        tiles_kernel,
-        out_shape=(of(nx, 1, 128), of(8, 256)),
-        in_specs=[vmem()],
-        out_specs=(vmem(), vmem()),
-        compiler_params=pltpu.CompilerParams(vmem_limit_bytes=GRANT),
-        name="tiles",
+    peak, wide = call(
+        tiles_kernel, "tiles", (of(nx, 1, 128), of(8, 256)), [vmem()], (vmem(), vmem())
     )(tiles)
     peaks = lax.all_to_all(peak, "gx", 0, 0)
     below = shifted(wide, "gx", 1)
-    powers = pl.pallas_call(
+    powers = call(
         filter_kernel,
-        out_shape=(of(ROWS, WIDTH), of(ROWS, WIDTH), of(ROWS, WIDTH), of(8, WIDTH)),
-        in_specs=[vmem(), vmem(), vmem()],
-        out_specs=(vmem(),) * 4,
-        scratch_shapes=[pltpu.VMEM((10, 8, 256), f32)],
-        compiler_params=pltpu.CompilerParams(vmem_limit_bytes=GRANT),
-        name="powers",
+        "powers",
+        (of(ROWS, WIDTH),) * 3 + (of(8, WIDTH),),
+        [vmem()] * 3,
+        (vmem(),) * 4,
+        [pltpu.VMEM((10, 8, 256), f32)],
     )(wide, below, orbitals.reshape(ROWS, -1))
     start = coefficients.reshape(ROWS, COLS)
     sent_shapes = (of(FLAT, COLS),) * 3 + (of(CUBE, FLAT, COLS),)
-    df, ft, scal, *sent = pl.pallas_call(
+    sent_specs = (vmem(),) * 3 + (pl.BlockSpec(memory_space=pltpu.HBM),)
+    staging = [pltpu.VMEM((3, FLAT, COLS), f32), pltpu.SemaphoreType.DMA((3,))]
+    df, ft, scal, *sent = call(
         basis_kernel,
-        out_shape=(of(ROWS, WIDTH), of(BODY, ROWS), of(2)) + sent_shapes,
-        in_specs=[vmem()] * 6,
-        out_specs=(vmem(), vmem(), smem()) + (vmem(),) * 4,
-        scratch_shapes=[pltpu.VMEM((WIDTH, 128), f32)],
-        compiler_params=pltpu.CompilerParams(vmem_limit_bytes=GRANT),
-        name="basis",
+        "basis",
+        (of(ROWS, WIDTH), of(BODY, ROWS), of(2)) + sent_shapes,
+        [vmem()] * 6,
+        (vmem(), vmem(), smem()) + sent_specs,
+        [pltpu.VMEM((WIDTH, 128), f32)] + staging,
     )(peaks, *powers, start)
 
     groups = cubes()
@@ -330,18 +335,17 @@
         halos = [swapped(trace, *pairing) for trace, pairing in zip(sent, SWAPS)]
         halos.append(lax.all_to_all(sent[3], AXES, 0, 0, axis_index_groups=groups))
         last = step == DG_STEPS - 1
-        shapes = (of(ROWS, COLS),) + (() if last else sent_shapes)
 
         def body(*refs, step=step, last=last):
             step_kernel(step == 0, last, *refs)
 
-        following, *sent = pl.pallas_call(
+        following, *sent = call(
             body,
-            out_shape=shapes,
-            in_specs=[smem()] + [vmem()] * 8,
-            out_specs=tuple(vmem() for _ in shapes),
-            compiler_params=pltpu.CompilerParams(vmem_limit_bytes=GRANT),
-            name=f"step{step}",
+            f"step{step}",
+            (of(ROWS, COLS),) + (() if last else sent_shapes),
+            [smem()] + [vmem()] * 8,
+            (vmem(),) + (() if last else sent_specs),
+            () if last else staging,
         )(scal, df, ft, now, prior, *halos)
         prior, now = now, following
     return now.reshape(coefficients.shape)

time: 132 us -> 126 us (0.955)
  waiting for transfers between devices: 21.6 us -> 15.4 us
    ppermute x9, waiting for transfers between devices: 8.76 us -> 2.6 us  [swapped(): return lax.ppermute(shard, axis, pairs + [(b, a) for a, b in pairs])]
    ppermute x9, starting transfers between devices: 31.7 us -> 35.2 us  [swapped(): return lax.ppermute(shard, axis, pairs + [(b, a) for a, b in pairs])]
    all_to_all x3, starting transfers between devices: 13.9 us -> 10.9 us  [per_device(): halos.append(lax.all_to_all(sent[3], AXES, 0, 0, axis_index_groups=groups))]
where the time goes in v6:
time: 126 us; the launch traced here: 125 us
  starting transfers between devices  69.2 us (55%)
  blocking collectives  24.3 us (19%)
  waiting for transfers between devices  15.4 us (12%)
  Pallas kernels  14.2 us (11%)
  local copies, waits for them, and re-layouts  2.17 us (2%)
    ppermute x9, starting transfers between devices, swapped(): return lax.ppermute(shard, axis, pairs + [(b, a) for a, b in pairs])  35.2 us
    all_to_all x1, blocking collectives, per_device(): tiles = lax.all_to_all(tile, ('gy', 'gz'), 0, 0)  24.3 us
    all_to_all x1, starting transfers between devices, per_device(): peaks = lax.all_to_all(peak, 'gx', 0, 0)  19.9 us
    all_to_all x3, starting transfers between devices, per_device(): halos.append(lax.all_to_all(sent[3], AXES, 0, 0, axis_index_groups=groups))  10.9 us
    all_to_all x1, waiting for transfers between devices, per_device(): peaks = lax.all_to_all(peak, 'gx', 0, 0)  10.1 us
    pallas_call x3, Pallas kernels, per_device(): call(body, f'step{step}', (of(ROWS, COLS),) + (() if last else sent_shape...  4.93 us
    pallas_call x1, Pallas kernels, per_device(): call(basis_kernel, 'basis', (of(ROWS, WIDTH), of(BODY, ROWS), of(2)) + se...  4.57 us
    pallas_call x1, Pallas kernels, per_device(): call(filter_kernel, 'powers', (of(ROWS, WIDTH),) * 3 + (of(8, WIDTH),), [...  3.82 us
  transfers between devices with their start and end apart: 14, of which 6 were waited for; matrix products, arithmetic and copies ran while one was open for 0% of the time, Pallas kernels for 3%

profile of v6, /device:TPU:1, one launch (start us, length us, event | category | flops | bytes accessed | tf_op | source)
XLA Modules:
  0.0 125.5 jit_solution(18399301933901746100)
XLA Ops:
  0.9 24.3 %all_to_all.25.tiles_ref = f32[32,8,128]{2,1,0:T(8,128)S(1)} all-to-all(f32[32,8,128]{2,1,0:T(8,128)S(1)} %tile.1), channel_id=1, replica_groups=mesh['gx'=32,'gy'=4,'gz'=8] {'gy','gz'}, dimensions={0} | all-to-all | bytes 262144 | tf_op jit(solution)/shard_map/all_to_all | solution.py:305
  26.0 19.9 %all-to-all-start.1 = ((f32[32,1,128]{2,1,0:T(1,128)}), f32[32,1,128]{2,1,0:T(1,128)S(1)}, u32[]{:S(2)}, u32[]{:S(2)}) async-start(f32[32,1,128]{2,1,0:T(1,128)} %get-tuple-element.28), calls=%async_computation.1 | async-start | bytes 32768 | tf_op jit(solution)/shard_map/all_to_all | solution.py:309
  45.9 3.1 %collective-permute-start = (f32[8,256]{1,0:T(8,128)S(1)}, f32[8,256]{1,0:T(8,128)S(1)}, u32[]{:S(2)}, u32[]{:S(2)}) collective-permute-start(f32[8,256]{1,0:T(8,128)S(1)} %get-tuple-element.29.wide_ref), channel_id=1, source_target_pairs={{0,32},{32,64},{64,96},{96,128},{128,160},{160,192},{192,224},{224... | collective-permute-start | bytes 24584 | tf_op jit(solution)/shard_map/ppermute | solution.py:25
  49.0 2.8 %collective-permute-done.below_ref = f32[8,256]{1,0:T(8,128)S(1)} collective-permute-done((f32[8,256]{1,0:T(8,128)S(1)}, f32[8,256]{1,0:T(8,128)S(1)}, u32[]{:S(2)}, u32[]{:S(2)}) %collective-permute-start) | collective-permute-done | bytes 8224 | tf_op jit(solution)/shard_map/ppermute | solution.py:25
  51.8 1.4 %copy-done = f32[1,1,1,96,4096]{4,3,2,1,0:T(8,128)S(1)} copy-done((f32[1,1,1,96,4096]{4,3,2,1,0:T(8,128)S(1)}, f32[1,1,1,96,4096]{4,3,2,1,0:T(8,128)}, u32[]{:S(2)}) %copy-start) | copy-done | bytes 1572888
  53.2 3.8 %powers.1 = (f32[96,512]{1,0:T(8,128)S(1)}, f32[96,512]{1,0:T(8,128)S(1)}, f32[96,512]{1,0:T(8,128)S(1)}, f32[8,512]{1,0:T(8,128)S(1)}) custom-call(f32[8,256]{1,0:T(8,128)S(1)} %get-tuple-element.29.wide_ref, f32[8,256]{1,0:T(8,128)S(1)} %collective-permute-done.below_ref, f32[96,4096]{1,0:T(8,128)S(1)} %bitcast.3), custom_call_target="tpu_custom_call" | custom-call | tf_op jit(solution)/shard_map/powers/pallas_call | solution.py:311
  57.0 10.1 %all-to-all-done.1.peaks_ref = f32[32,1,128]{2,1,0:T(1,128)S(1)} async-done(((f32[32,1,128]{2,1,0:T(1,128)}), f32[32,1,128]{2,1,0:T(1,128)S(1)}, u32[]{:S(2)}, u32[]{:S(2)}) %all-to-all-start.1) | async-done | bytes 16416 | tf_op jit(solution)/shard_map/all_to_all | solution.py:309
  67.1 4.6 %basis.1 = (f32[96,512]{1,0:T(8,128)S(1)}, f32[384,96]{1,0:T(8,128)S(1)}, f32[2]{0:T(128)S(1)}, f32[64,256]{1,0:T(8,128)S(1)}, f32[64,256]{1,0:T(8,128)S(1)}, /*...) custom-call(f32[32,1,128]{2,1,0:T(1,128)S(1)} %all-to-all-done.1.peaks_ref, f32[96,512]{1,0:T(8,128)S(1)} %get-tuple-element.30.u0_ref, ...), custom_call_target="tpu_custom_call" | custom-call | tf_op jit(solution)/shard_map/basis/pallas_call | solution.py:323
  71.7 3.9 %all-to-all-start.2 = ((f32[8,64,256]{2,1,0:T(8,128)}), f32[8,64,256]{2,1,0:T(8,128)S(1)}, u32[]{:S(2)}, u32[]{:S(2)}) async-start(f32[8,64,256]{2,1,0:T(8,128)} %get-tuple-element.40), calls=%async_computation.2 | async-start | bytes 1048576 | tf_op jit(solution)/shard_map/all_to_all | solution.py:336
  75.6 4.9 %collective-permute-start.1 = (f32[64,256]{1,0:T(8,128)S(1)}, f32[64,256]{1,0:T(8,128)S(1)}, u32[]{:S(2)}, u32[]{:S(2)}) collective-permute-start(f32[64,256]{1,0:T(8,128)S(1)} %get-tuple-element.37), channel_id=1, source_target_pairs={{1,2},{3,4},{5,6},{7,0},{2,1},{4,3},{6,5},{0,7},{9,10},{11,12},{13... | collective-permute-start | bytes 196616 | tf_op jit(solution)/shard_map/ppermute | solution.py:78
  80.5 2.8 %collective-permute-start.2 = (f32[64,256]{1,0:T(8,128)S(1)}, f32[64,256]{1,0:T(8,128)S(1)}, u32[]{:S(2)}, u32[]{:S(2)}) collective-permute-start(f32[64,256]{1,0:T(8,128)S(1)} %get-tuple-element.38), channel_id=1, source_target_pairs={{32,64},{96,128},{160,192},{224,256},{288,320},{352,384},{416,448}... | collective-permute-start | bytes 196616 | tf_op jit(solution)/shard_map/ppermute | solution.py:78
  83.3 3.4 %collective-permute-start.3 = (f32[64,256]{1,0:T(8,128)S(1)}, f32[64,256]{1,0:T(8,128)S(1)}, u32[]{:S(2)}, u32[]{:S(2)}) collective-permute-start(f32[64,256]{1,0:T(8,128)S(1)} %get-tuple-element.39), channel_id=1, source_target_pairs={{0,8},{16,24},{8,0},{24,16},{1,9},{17,25},{9,1},{25,17},{2,10},{18... | collective-permute-start | bytes 196616 | tf_op jit(solution)/shard_map/ppermute | solution.py:78
  87.6 1.7 %step0.1 = (f32[96,256]{1,0:T(8,128)S(1)}, f32[64,256]{1,0:T(8,128)S(1)}, f32[64,256]{1,0:T(8,128)S(1)}, f32[64,256]{1,0:T(8,128)S(1)}, f32[8,64,256]{2,1,0:T(8,128)}) custom-call(f32[2]{0:T(128)S(1)} %get-tuple-element.34.refs_0_, f32[96,512]{1,0:T(8,128)S(1)} %get-tuple-element.35.refs_1_, f32[384,96]{1,0:T(8,128)S(1)} %get-tuple-element.36.refs_2_, ...), custom_call_target="tpu_custom_call" | custom-call | tf_op jit(solution)/shard_map/step0/pallas_call | solution.py:342
  89.3 3.5 %all-to-all-start.3 = ((f32[8,64,256]{2,1,0:T(8,128)}), f32[8,64,256]{2,1,0:T(8,128)S(1)}, u32[]{:S(2)}, u32[]{:S(2)}) async-start(f32[8,64,256]{2,1,0:T(8,128)} %get-tuple-element.45), calls=%async_computation.3 | async-start | bytes 1048576 | tf_op jit(solution)/shard_map/all_to_all | solution.py:336
  92.8 6.3 %collective-permute-start.4 = (f32[64,256]{1,0:T(8,128)S(1)}, f32[64,256]{1,0:T(8,128)S(1)}, u32[]{:S(2)}, u32[]{:S(2)}) collective-permute-start(f32[64,256]{1,0:T(8,128)S(1)} %get-tuple-element.42), channel_id=1, source_target_pairs={{1,2},{3,4},{5,6},{7,0},{2,1},{4,3},{6,5},{0,7},{9,10},{11,12},{13... | collective-permute-start | bytes 196616 | tf_op jit(solution)/shard_map/ppermute | solution.py:78
  99.2 3.4 %collective-permute-start.5 = (f32[64,256]{1,0:T(8,128)S(1)}, f32[64,256]{1,0:T(8,128)S(1)}, u32[]{:S(2)}, u32[]{:S(2)}) collective-permute-start(f32[64,256]{1,0:T(8,128)S(1)} %get-tuple-element.43), channel_id=1, source_target_pairs={{32,64},{96,128},{160,192},{224,256},{288,320},{352,384},{416,448}... | collective-permute-start | bytes 196616 | tf_op jit(solution)/shard_map/ppermute | solution.py:78
  102.6 3.1 %collective-permute-start.6 = (f32[64,256]{1,0:T(8,128)S(1)}, f32[64,256]{1,0:T(8,128)S(1)}, u32[]{:S(2)}, u32[]{:S(2)}) collective-permute-start(f32[64,256]{1,0:T(8,128)S(1)} %get-tuple-element.44), channel_id=1, source_target_pairs={{0,8},{16,24},{8,0},{24,16},{1,9},{17,25},{9,1},{25,17},{2,10},{18... | collective-permute-start | bytes 196616 | tf_op jit(solution)/shard_map/ppermute | solution.py:78
  106.6 1.7 %step1.1 = (f32[96,256]{1,0:T(8,128)S(1)}, f32[64,256]{1,0:T(8,128)S(1)}, f32[64,256]{1,0:T(8,128)S(1)}, f32[64,256]{1,0:T(8,128)S(1)}, f32[8,64,256]{2,1,0:T(8,128)}) custom-call(f32[2]{0:T(128)S(1)} %get-tuple-element.34.refs_0_, f32[96,512]{1,0:T(8,128)S(1)} %get-tuple-element.35.refs_1_, f32[384,96]{1,0:T(8,128)S(1)} %get-tuple-element.36.refs_2_, ...), custom_call_target="tpu_custom_call" | custom-call | tf_op jit(solution)/shard_map/step1/pallas_call | solution.py:342
  108.3 3.5 %all-to-all-start.4 = ((f32[8,64,256]{2,1,0:T(8,128)}), f32[8,64,256]{2,1,0:T(8,128)S(1)}, u32[]{:S(2)}, u32[]{:S(2)}) async-start(f32[8,64,256]{2,1,0:T(8,128)} %get-tuple-element.50), calls=%async_computation.4 | async-start | bytes 1048576 | tf_op jit(solution)/shard_map/all_to_all | solution.py:336
  111.9 4.0 %collective-permute-start.7 = (f32[64,256]{1,0:T(8,128)S(1)}, f32[64,256]{1,0:T(8,128)S(1)}, u32[]{:S(2)}, u32[]{:S(2)}) collective-permute-start(f32[64,256]{1,0:T(8,128)S(1)} %get-tuple-element.47), channel_id=1, source_target_pairs={{1,2},{3,4},{5,6},{7,0},{2,1},{4,3},{6,5},{0,7},{9,10},{11,12},{13... | collective-permute-start | bytes 196616 | tf_op jit(solution)/shard_map/ppermute | solution.py:78
  115.8 3.9 %collective-permute-start.8 = (f32[64,256]{1,0:T(8,128)S(1)}, f32[64,256]{1,0:T(8,128)S(1)}, u32[]{:S(2)}, u32[]{:S(2)}) collective-permute-start(f32[64,256]{1,0:T(8,128)S(1)} %get-tuple-element.48), channel_id=1, source_target_pairs={{32,64},{96,128},{160,192},{224,256},{288,320},{352,384},{416,448}... | collective-permute-start | bytes 196616 | tf_op jit(solution)/shard_map/ppermute | solution.py:78
  119.8 3.4 %collective-permute-start.9 = (f32[64,256]{1,0:T(8,128)S(1)}, f32[64,256]{1,0:T(8,128)S(1)}, u32[]{:S(2)}, u32[]{:S(2)}) collective-permute-start(f32[64,256]{1,0:T(8,128)S(1)} %get-tuple-element.49), channel_id=1, source_target_pairs={{0,8},{16,24},{8,0},{24,16},{1,9},{17,25},{9,1},{25,17},{2,10},{18... | collective-permute-start | bytes 196616 | tf_op jit(solution)/shard_map/ppermute | solution.py:78
  123.2 0.9 collective-permute-done.9.refs_7_
  124.0 1.4 %step2.1 = f32[96,256]{1,0:T(8,128)} custom-call(f32[2]{0:T(128)S(1)} %get-tuple-element.34.refs_0_, f32[96,512]{1,0:T(8,128)S(1)} %get-tuple-element.35.refs_1_, f32[384,96]{1,0:T(8,128)S(1)} %get-tuple-element.36.refs_2_, f32[96,256]{1,0:T(8,128)S(1)} %get-tuple-element.46.refs_3_, f32[96,256]{1,0:T(8,128)S(1)} %get-tuple-element.41.refs_3_.refs_4_, ...), custom_call_target="tpu_custom_call" | custom-call | tf_op jit(solution)/shard_map/step2/pallas_call | solution.py:342
  (18 shorter events, 3.4 us)
Async XLA Ops:
  0.0 0.8 copy-start.2
  0.8 66.3 %copy-start.1 = (f32[1,1,1,96,256]{4,3,2,1,0:T(8,128)S(1)}, f32[1,1,1,96,256]{4,3,2,1,0:T(8,128)}, u32[]{:S(2)}) copy-start(f32[1,1,1,96,256]{4,3,2,1,0:T(8,128)} %param.5) | copy-start | bytes 294916
  26.0 41.1 %all-to-all-start.1 = ((f32[32,1,128]{2,1,0:T(1,128)}), f32[32,1,128]{2,1,0:T(1,128)S(1)}, u32[]{:S(2)}, u32[]{:S(2)}) async-start(f32[32,1,128]{2,1,0:T(1,128)} %get-tuple-element.28), calls=%async_computation.1 | async-start | bytes 32768 | tf_op jit(solution)/shard_map/all_to_all | solution.py:309
  45.9 5.9 %collective-permute-start = (f32[8,256]{1,0:T(8,128)S(1)}, f32[8,256]{1,0:T(8,128)S(1)}, u32[]{:S(2)}, u32[]{:S(2)}) collective-permute-start(f32[8,256]{1,0:T(8,128)S(1)} %get-tuple-element.29.wide_ref), channel_id=1, source_target_pairs={{0,32},{32,64},{64,96},{96,128},{128,160},{160,192},{192,224},{224... | collective-permute-start | bytes 24584 | tf_op jit(solution)/shard_map/ppermute | solution.py:25
  51.8 1.4 %copy-start = (f32[1,1,1,96,4096]{4,3,2,1,0:T(8,128)S(1)}, f32[1,1,1,96,4096]{4,3,2,1,0:T(8,128)}, u32[]{:S(2)}) copy-start(f32[1,1,1,96,4096]{4,3,2,1,0:T(8,128)} %param.3) | copy-start | bytes 4718596
  71.7 15.9 %all-to-all-start.2 = ((f32[8,64,256]{2,1,0:T(8,128)}), f32[8,64,256]{2,1,0:T(8,128)S(1)}, u32[]{:S(2)}, u32[]{:S(2)}) async-start(f32[8,64,256]{2,1,0:T(8,128)} %get-tuple-element.40), calls=%async_computation.2 | async-start | bytes 1048576 | tf_op jit(solution)/shard_map/all_to_all | solution.py:336
  75.6 11.1 %collective-permute-start.1 = (f32[64,256]{1,0:T(8,128)S(1)}, f32[64,256]{1,0:T(8,128)S(1)}, u32[]{:S(2)}, u32[]{:S(2)}) collective-permute-start(f32[64,256]{1,0:T(8,128)S(1)} %get-tuple-element.37), channel_id=1, source_target_pairs={{1,2},{3,4},{5,6},{7,0},{2,1},{4,3},{6,5},{0,7},{9,10},{11,12},{13... | collective-permute-start | bytes 196616 | tf_op jit(solution)/shard_map/ppermute | solution.py:78
  80.5 6.5 %collective-permute-start.2 = (f32[64,256]{1,0:T(8,128)S(1)}, f32[64,256]{1,0:T(8,128)S(1)}, u32[]{:S(2)}, u32[]{:S(2)}) collective-permute-start(f32[64,256]{1,0:T(8,128)S(1)} %get-tuple-element.38), channel_id=1, source_target_pairs={{32,64},{96,128},{160,192},{224,256},{288,320},{352,384},{416,448}... | collective-permute-start | bytes 196616 | tf_op jit(solution)/shard_map/ppermute | solution.py:78
  83.3 4.3 %collective-permute-start.3 = (f32[64,256]{1,0:T(8,128)S(1)}, f32[64,256]{1,0:T(8,128)S(1)}, u32[]{:S(2)}, u32[]{:S(2)}) collective-permute-start(f32[64,256]{1,0:T(8,128)S(1)} %get-tuple-element.39), channel_id=1, source_target_pairs={{0,8},{16,24},{8,0},{24,16},{1,9},{17,25},{9,1},{25,17},{2,10},{18... | collective-permute-start | bytes 196616 | tf_op jit(solution)/shard_map/ppermute | solution.py:78
  89.3 17.3 %all-to-all-start.3 = ((f32[8,64,256]{2,1,0:T(8,128)}), f32[8,64,256]{2,1,0:T(8,128)S(1)}, u32[]{:S(2)}, u32[]{:S(2)}) async-start(f32[8,64,256]{2,1,0:T(8,128)} %get-tuple-element.45), calls=%async_computation.3 | async-start | bytes 1048576 | tf_op jit(solution)/shard_map/all_to_all | solution.py:336
  92.8 12.9 %collective-permute-start.4 = (f32[64,256]{1,0:T(8,128)S(1)}, f32[64,256]{1,0:T(8,128)S(1)}, u32[]{:S(2)}, u32[]{:S(2)}) collective-permute-start(f32[64,256]{1,0:T(8,128)S(1)} %get-tuple-element.42), channel_id=1, source_target_pairs={{1,2},{3,4},{5,6},{7,0},{2,1},{4,3},{6,5},{0,7},{9,10},{11,12},{13... | collective-permute-start | bytes 196616 | tf_op jit(solution)/shard_map/ppermute | solution.py:78
  99.2 6.6 %collective-permute-start.5 = (f32[64,256]{1,0:T(8,128)S(1)}, f32[64,256]{1,0:T(8,128)S(1)}, u32[]{:S(2)}, u32[]{:S(2)}) collective-permute-start(f32[64,256]{1,0:T(8,128)S(1)} %get-tuple-element.43), channel_id=1, source_target_pairs={{32,64},{96,128},{160,192},{224,256},{288,320},{352,384},{416,448}... | collective-permute-start | bytes 196616 | tf_op jit(solution)/shard_map/ppermute | solution.py:78
  102.6 4.0 %collective-permute-start.6 = (f32[64,256]{1,0:T(8,128)S(1)}, f32[64,256]{1,0:T(8,128)S(1)}, u32[]{:S(2)}, u32[]{:S(2)}) collective-permute-start(f32[64,256]{1,0:T(8,128)S(1)} %get-tuple-element.44), channel_id=1, source_target_pairs={{0,8},{16,24},{8,0},{24,16},{1,9},{17,25},{9,1},{25,17},{2,10},{18... | collective-permute-start | bytes 196616 | tf_op jit(solution)/shard_map/ppermute | solution.py:78
  108.3 15.7 %all-to-all-start.4 = ((f32[8,64,256]{2,1,0:T(8,128)}), f32[8,64,256]{2,1,0:T(8,128)S(1)}, u32[]{:S(2)}, u32[]{:S(2)}) async-start(f32[8,64,256]{2,1,0:T(8,128)} %get-tuple-element.50), calls=%async_computation.4 | async-start | bytes 1048576 | tf_op jit(solution)/shard_map/all_to_all | solution.py:336
  111.9 11.3 %collective-permute-start.7 = (f32[64,256]{1,0:T(8,128)S(1)}, f32[64,256]{1,0:T(8,128)S(1)}, u32[]{:S(2)}, u32[]{:S(2)}) collective-permute-start(f32[64,256]{1,0:T(8,128)S(1)} %get-tuple-element.47), channel_id=1, source_target_pairs={{1,2},{3,4},{5,6},{7,0},{2,1},{4,3},{6,5},{0,7},{9,10},{11,12},{13... | collective-permute-start | bytes 196616 | tf_op jit(solution)/shard_map/ppermute | solution.py:78
  115.8 7.3 %collective-permute-start.8 = (f32[64,256]{1,0:T(8,128)S(1)}, f32[64,256]{1,0:T(8,128)S(1)}, u32[]{:S(2)}, u32[]{:S(2)}) collective-permute-start(f32[64,256]{1,0:T(8,128)S(1)} %get-tuple-element.48), channel_id=1, source_target_pairs={{32,64},{96,128},{160,192},{224,256},{288,320},{352,384},{416,448}... | collective-permute-start | bytes 196616 | tf_op jit(solution)/shard_map/ppermute | solution.py:78
  119.8 4.3 %collective-permute-start.9 = (f32[64,256]{1,0:T(8,128)S(1)}, f32[64,256]{1,0:T(8,128)S(1)}, u32[]{:S(2)}, u32[]{:S(2)}) collective-permute-start(f32[64,256]{1,0:T(8,128)S(1)} %get-tuple-element.49), channel_id=1, source_target_pairs={{0,8},{16,24},{8,0},{24,16},{1,9},{17,25},{9,1},{25,17},{2,10},{18... | collective-permute-start | bytes 196616 | tf_op jit(solution)/shard_map/ppermute | solution.py:78

commit v7 on v6

--- a/solution.py
+++ b/solution.py
@@ -181,8 +181,8 @@
         copy.wait()
 
 
-def basis_kernel(peaks_ref, u0_ref, u1_ref, u2_ref, own_ref, vectors_ref,
-                 df_ref, ft_ref, scal_ref, *refs):
+def basis_kernel(peaks_ref, u0_ref, u1_ref, u2_ref, vectors_ref,
+                 basis_ref, ft_ref, scal_ref, *refs):
     sent, (bt_ref, held_ref, sems) = refs[:-3], refs[-3:]
     top = 6.0 + jnp.max(peaks_ref[...])
     centre = (top + cutoff) / 2.0
@@ -211,25 +211,7 @@
     root = root / jnp.sqrt(sigma)
     basis = dot3(split(root), halves)
 
-    own = own_ref[:1] + SHIFT
-    cell = lanes((ROWS, WIDTH))
-    z = cell % 8
-    y = cell // 16 % 8
-    x = cell // 128 * 2 + cell // 8 % 2
-    odd = x % 2 == 1
-
-    def gate(ok, value):
-        return jnp.where(ok, value, 0.0)
-
-    total = gate(z > 0, lane_roll(basis, 1)) + gate(z < 7, lane_roll(basis, -1))
-    total = total + gate(y > 0, lane_roll(basis, 16)) + gate(y < 7, lane_roll(basis, -16))
-    total = total + jnp.where(odd, lane_roll(basis, 8), lane_roll(basis, -8))
-    total = total + gate(
-        (x > 0) & (x < 7), jnp.where(odd, lane_roll(basis, -120), lane_roll(basis, 120))
-    )
-    applied = own * basis - 0.5 * total
-    diagonal = dot3(split(basis), split(applied), (((1,), (1,)), ((), ())))
-
+    basis_ref[...] = basis
     bt_ref[...] = jnp.concatenate([basis, jnp.zeros((128 - ROWS, WIDTH), jnp.float32)], axis=0).T
     lower = (
         jnp.concatenate([bt_ref[yy * 16 : yy * 16 + 8] for yy in range(8)], axis=0),
@@ -248,10 +230,32 @@
     faces_t = jnp.concatenate(pieces, axis=0)
     ft = faces_t[:, :ROWS]
     ft_ref[...] = ft
-    df_ref[:, :BODY] = -0.5 * faces_t.T[:ROWS]
+    send_traces(ft, vectors_ref[...], sent, held_ref, sems)
+
+
+def coupling_kernel(basis_ref, own_ref, ft_ref, df_ref):
+    basis = basis_ref[...]
+    own = own_ref[:1] + SHIFT
+    cell = lanes((ROWS, WIDTH))
+    z = cell % 8
+    y = cell // 16 % 8
+    x = cell // 128 * 2 + cell // 8 % 2
+    odd = x % 2 == 1
+
+    def gate(ok, value):
+        return jnp.where(ok, value, 0.0)
+
+    total = gate(z > 0, lane_roll(basis, 1)) + gate(z < 7, lane_roll(basis, -1))
+    total = total + gate(y > 0, lane_roll(basis, 16)) + gate(y < 7, lane_roll(basis, -16))
+    total = total + jnp.where(odd, lane_roll(basis, 8), lane_roll(basis, -8))
+    total = total + gate(
+        (x > 0) & (x < 7), jnp.where(odd, lane_roll(basis, -120), lane_roll(basis, 120))
+    )
+    applied = own * basis - 0.5 * total
+    diagonal = dot3(split(basis), split(applied), (((1,), (1,)), ((), ())))
+    df_ref[:, :BODY] = -0.5 * ft_ref[...].T
     df_ref[:, BODY : BODY + ROWS] = diagonal
     df_ref[:, BODY + ROWS :] = jnp.zeros((ROWS, WIDTH - BODY - ROWS), jnp.float32)
-    send_traces(ft, vectors_ref[...], sent, held_ref, sems)
 
 
 def step_kernel(first, last, scal_ref, df_ref, ft_ref, now_ref, prior_ref, *refs):
@@ -308,7 +312,7 @@
     )(tiles)
     peaks = lax.all_to_all(peak, "gx", 0, 0)
     below = shifted(wide, "gx", 1)
-    powers = call(
+    *powers, own = call(
         filter_kernel,
         "powers",
         (of(ROWS, WIDTH),) * 3 + (of(8, WIDTH),),
@@ -320,14 +324,15 @@
     sent_shapes = (of(FLAT, COLS),) * 3 + (of(CUBE, FLAT, COLS),)
     sent_specs = (vmem(),) * 3 + (pl.BlockSpec(memory_space=pltpu.HBM),)
     staging = [pltpu.VMEM((3, FLAT, COLS), f32), pltpu.SemaphoreType.DMA((3,))]
-    df, ft, scal, *sent = call(
+    basis, ft, scal, *sent = call(
         basis_kernel,
         "basis",
         (of(ROWS, WIDTH), of(BODY, ROWS), of(2)) + sent_shapes,
-        [vmem()] * 6,
+        [vmem()] * 5,
         (vmem(), vmem(), smem()) + sent_specs,
         [pltpu.VMEM((WIDTH, 128), f32)] + staging,
     )(peaks, *powers, start)
+    df = call(coupling_kernel, "coupling", of(ROWS, WIDTH), [vmem()] * 3, vmem())(basis, own, ft)
 
     groups = cubes()
     prior, now = start, start

time: 126 us -> 126 us (level)
  transfers between devices with their start and end apart: 14 -> 14, of which waited for: 6 -> 5; matrix products, arithmetic and copies ran while one was open for 0% -> 0% of each run, Pallas kernels for 3% -> 4%
where the time goes in v7:
time: 126 us; the launch traced here: 125 us
  starting transfers between devices  69.1 us (55%)
  blocking collectives  24.3 us (19%)
  waiting for transfers between devices  14.8 us (12%)
  Pallas kernels  14.5 us (12%)
  local copies, waits for them, and re-layouts  2.17 us (2%)
    ppermute x9, starting transfers between devices, swapped(): return lax.ppermute(shard, axis, pairs + [(b, a) for a, b in pairs])  35.2 us
    all_to_all x1, blocking collectives, per_device(): tiles = lax.all_to_all(tile, ('gy', 'gz'), 0, 0)  24.3 us
    all_to_all x1, starting transfers between devices, per_device(): peaks = lax.all_to_all(peak, 'gx', 0, 0)  19.9 us
    all_to_all x3, starting transfers between devices, per_device(): halos.append(lax.all_to_all(sent[3], AXES, 0, 0, axis_index_groups=groups))  10.9 us
    all_to_all x1, waiting for transfers between devices, per_device(): peaks = lax.all_to_all(peak, 'gx', 0, 0)  10.1 us
    pallas_call x3, Pallas kernels, per_device(): call(body, f'step{step}', (of(ROWS, COLS),) + (() if last else sent_shape...  4.94 us
    pallas_call x1, Pallas kernels, per_device(): call(basis_kernel, 'basis', (of(ROWS, WIDTH), of(BODY, ROWS), of(2)) + se...  4.25 us
    pallas_call x1, Pallas kernels, per_device(): call(filter_kernel, 'powers', (of(ROWS, WIDTH),) * 3 + (of(8, WIDTH),), [...  3.82 us
  transfers between devices with their start and end apart: 14, of which 5 were waited for; matrix products, arithmetic and copies ran while one was open for 0% of the time, Pallas kernels for 4%

profile of v7, /device:TPU:1, one launch (start us, length us, event | category | flops | bytes accessed | tf_op | source)
XLA Modules:
  0.0 125.2 jit_solution(333484006271091842)
XLA Ops:
  0.9 24.3 %all_to_all.25.tiles_ref = f32[32,8,128]{2,1,0:T(8,128)S(1)} all-to-all(f32[32,8,128]{2,1,0:T(8,128)S(1)} %tile.1), channel_id=1, replica_groups=mesh['gx'=32,'gy'=4,'gz'=8] {'gy','gz'}, dimensions={0} | all-to-all | bytes 262144 | tf_op jit(solution)/shard_map/all_to_all | solution.py:309
  26.0 19.9 %all-to-all-start.1 = ((f32[32,1,128]{2,1,0:T(1,128)}), f32[32,1,128]{2,1,0:T(1,128)S(1)}, u32[]{:S(2)}, u32[]{:S(2)}) async-start(f32[32,1,128]{2,1,0:T(1,128)} %get-tuple-element.28), calls=%async_computation.1 | async-start | bytes 32768 | tf_op jit(solution)/shard_map/all_to_all | solution.py:313
  45.9 3.1 %collective-permute-start = (f32[8,256]{1,0:T(8,128)S(1)}, f32[8,256]{1,0:T(8,128)S(1)}, u32[]{:S(2)}, u32[]{:S(2)}) collective-permute-start(f32[8,256]{1,0:T(8,128)S(1)} %get-tuple-element.29.wide_ref), channel_id=1, source_target_pairs={{0,32},{32,64},{64,96},{96,128},{128,160},{160,192},{192,224},{224... | collective-permute-start | bytes 24584 | tf_op jit(solution)/shard_map/ppermute | solution.py:25
  49.0 2.8 %collective-permute-done.below_ref = f32[8,256]{1,0:T(8,128)S(1)} collective-permute-done((f32[8,256]{1,0:T(8,128)S(1)}, f32[8,256]{1,0:T(8,128)S(1)}, u32[]{:S(2)}, u32[]{:S(2)}) %collective-permute-start) | collective-permute-done | bytes 8224 | tf_op jit(solution)/shard_map/ppermute | solution.py:25
  51.8 1.4 %copy-done = f32[1,1,1,96,4096]{4,3,2,1,0:T(8,128)S(1)} copy-done((f32[1,1,1,96,4096]{4,3,2,1,0:T(8,128)S(1)}, f32[1,1,1,96,4096]{4,3,2,1,0:T(8,128)}, u32[]{:S(2)}) %copy-start) | copy-done | bytes 1572888
  53.2 3.8 %powers.1 = (f32[96,512]{1,0:T(8,128)S(1)}, f32[96,512]{1,0:T(8,128)S(1)}, f32[96,512]{1,0:T(8,128)S(1)}, f32[8,512]{1,0:T(8,128)S(1)}) custom-call(f32[8,256]{1,0:T(8,128)S(1)} %get-tuple-element.29.wide_ref, f32[8,256]{1,0:T(8,128)S(1)} %collective-permute-done.below_ref, f32[96,4096]{1,0:T(8,128)S(1)} %bitcast.3), custom_call_target="tpu_custom_call" | custom-call | tf_op jit(solution)/shard_map/powers/pallas_call | solution.py:315
  57.0 10.1 %all-to-all-done.1.peaks_ref = f32[32,1,128]{2,1,0:T(1,128)S(1)} async-done(((f32[32,1,128]{2,1,0:T(1,128)}), f32[32,1,128]{2,1,0:T(1,128)S(1)}, u32[]{:S(2)}, u32[]{:S(2)}) %all-to-all-start.1) | async-done | bytes 16416 | tf_op jit(solution)/shard_map/all_to_all | solution.py:313
  67.1 4.2 %basis.1 = (f32[96,512]{1,0:T(8,128)S(1)}, f32[384,96]{1,0:T(8,128)S(1)}, f32[2]{0:T(128)S(1)}, f32[64,256]{1,0:T(8,128)S(1)}, f32[64,256]{1,0:T(8,128)S(1)}, /*...) custom-call(f32[32,1,128]{2,1,0:T(1,128)S(1)} %all-to-all-done.1.peaks_ref, f32[96,512]{1,0:T(8,128)S(1)} %get-tuple-element.30.u0_ref, ...), custom_call_target="tpu_custom_call" | custom-call | tf_op jit(solution)/shard_map/basis/pallas_call | solution.py:327
  71.4 3.9 %all-to-all-start.2 = ((f32[8,64,256]{2,1,0:T(8,128)}), f32[8,64,256]{2,1,0:T(8,128)S(1)}, u32[]{:S(2)}, u32[]{:S(2)}) async-start(f32[8,64,256]{2,1,0:T(8,128)} %get-tuple-element.40), calls=%async_computation.2 | async-start | bytes 1048576 | tf_op jit(solution)/shard_map/all_to_all | solution.py:341
  75.3 4.9 %collective-permute-start.1 = (f32[64,256]{1,0:T(8,128)S(1)}, f32[64,256]{1,0:T(8,128)S(1)}, u32[]{:S(2)}, u32[]{:S(2)}) collective-permute-start(f32[64,256]{1,0:T(8,128)S(1)} %get-tuple-element.37), channel_id=1, source_target_pairs={{1,2},{3,4},{5,6},{7,0},{2,1},{4,3},{6,5},{0,7},{9,10},{11,12},{13... | collective-permute-start | bytes 196616 | tf_op jit(solution)/shard_map/ppermute | solution.py:78
  80.2 2.8 %collective-permute-start.2 = (f32[64,256]{1,0:T(8,128)S(1)}, f32[64,256]{1,0:T(8,128)S(1)}, u32[]{:S(2)}, u32[]{:S(2)}) collective-permute-start(f32[64,256]{1,0:T(8,128)S(1)} %get-tuple-element.38), channel_id=1, source_target_pairs={{32,64},{96,128},{160,192},{224,256},{288,320},{352,384},{416,448}... | collective-permute-start | bytes 196616 | tf_op jit(solution)/shard_map/ppermute | solution.py:78
  82.9 3.4 %collective-permute-start.3 = (f32[64,256]{1,0:T(8,128)S(1)}, f32[64,256]{1,0:T(8,128)S(1)}, u32[]{:S(2)}, u32[]{:S(2)}) collective-permute-start(f32[64,256]{1,0:T(8,128)S(1)} %get-tuple-element.39), channel_id=1, source_target_pairs={{0,8},{16,24},{8,0},{24,16},{1,9},{17,25},{9,1},{25,17},{2,10},{18... | collective-permute-start | bytes 196616 | tf_op jit(solution)/shard_map/ppermute | solution.py:78
  87.2 1.7 %step0.1 = (f32[96,256]{1,0:T(8,128)S(1)}, f32[64,256]{1,0:T(8,128)S(1)}, f32[64,256]{1,0:T(8,128)S(1)}, f32[64,256]{1,0:T(8,128)S(1)}, f32[8,64,256]{2,1,0:T(8,128)}) custom-call(f32[2]{0:T(128)S(1)} %get-tuple-element.33.refs_0_, f32[96,512]{1,0:T(8,128)S(1)} %coupling.1.refs_1_, f32[384,96]{1,0:T(8,128)S(1)} %get-tuple-element.36.ft_ref.refs_2_, ...), custom_call_target="tpu_custom_call" | custom-call | tf_op jit(solution)/shard_map/step0/pallas_call | solution.py:347
  89.0 3.5 %all-to-all-start.3 = ((f32[8,64,256]{2,1,0:T(8,128)}), f32[8,64,256]{2,1,0:T(8,128)S(1)}, u32[]{:S(2)}, u32[]{:S(2)}) async-start(f32[8,64,256]{2,1,0:T(8,128)} %get-tuple-element.45), calls=%async_computation.3 | async-start | bytes 1048576 | tf_op jit(solution)/shard_map/all_to_all | solution.py:341
  92.5 6.4 %collective-permute-start.4 = (f32[64,256]{1,0:T(8,128)S(1)}, f32[64,256]{1,0:T(8,128)S(1)}, u32[]{:S(2)}, u32[]{:S(2)}) collective-permute-start(f32[64,256]{1,0:T(8,128)S(1)} %get-tuple-element.42), channel_id=1, source_target_pairs={{1,2},{3,4},{5,6},{7,0},{2,1},{4,3},{6,5},{0,7},{9,10},{11,12},{13... | collective-permute-start | bytes 196616 | tf_op jit(solution)/shard_map/ppermute | solution.py:78
  98.8 3.4 %collective-permute-start.5 = (f32[64,256]{1,0:T(8,128)S(1)}, f32[64,256]{1,0:T(8,128)S(1)}, u32[]{:S(2)}, u32[]{:S(2)}) collective-permute-start(f32[64,256]{1,0:T(8,128)S(1)} %get-tuple-element.43), channel_id=1, source_target_pairs={{32,64},{96,128},{160,192},{224,256},{288,320},{352,384},{416,448}... | collective-permute-start | bytes 196616 | tf_op jit(solution)/shard_map/ppermute | solution.py:78
  102.3 3.1 %collective-permute-start.6 = (f32[64,256]{1,0:T(8,128)S(1)}, f32[64,256]{1,0:T(8,128)S(1)}, u32[]{:S(2)}, u32[]{:S(2)}) collective-permute-start(f32[64,256]{1,0:T(8,128)S(1)} %get-tuple-element.44), channel_id=1, source_target_pairs={{0,8},{16,24},{8,0},{24,16},{1,9},{17,25},{9,1},{25,17},{2,10},{18... | collective-permute-start | bytes 196616 | tf_op jit(solution)/shard_map/ppermute | solution.py:78
  105.4 0.9 collective-permute-done.6.refs_7_
  106.3 1.7 %step1.1 = (f32[96,256]{1,0:T(8,128)S(1)}, f32[64,256]{1,0:T(8,128)S(1)}, f32[64,256]{1,0:T(8,128)S(1)}, f32[64,256]{1,0:T(8,128)S(1)}, f32[8,64,256]{2,1,0:T(8,128)}) custom-call(f32[2]{0:T(128)S(1)} %get-tuple-element.33.refs_0_, f32[96,512]{1,0:T(8,128)S(1)} %coupling.1.refs_1_, f32[384,96]{1,0:T(8,128)S(1)} %get-tuple-element.36.ft_ref.refs_2_, ...), custom_call_target="tpu_custom_call" | custom-call | tf_op jit(solution)/shard_map/step1/pallas_call | solution.py:347
  108.0 3.5 %all-to-all-start.4 = ((f32[8,64,256]{2,1,0:T(8,128)}), f32[8,64,256]{2,1,0:T(8,128)S(1)}, u32[]{:S(2)}, u32[]{:S(2)}) async-start(f32[8,64,256]{2,1,0:T(8,128)} %get-tuple-element.50), calls=%async_computation.4 | async-start | bytes 1048576 | tf_op jit(solution)/shard_map/all_to_all | solution.py:341
  111.5 4.0 %collective-permute-start.7 = (f32[64,256]{1,0:T(8,128)S(1)}, f32[64,256]{1,0:T(8,128)S(1)}, u32[]{:S(2)}, u32[]{:S(2)}) collective-permute-start(f32[64,256]{1,0:T(8,128)S(1)} %get-tuple-element.47), channel_id=1, source_target_pairs={{1,2},{3,4},{5,6},{7,0},{2,1},{4,3},{6,5},{0,7},{9,10},{11,12},{13... | collective-permute-start | bytes 196616 | tf_op jit(solution)/shard_map/ppermute | solution.py:78
  115.5 3.9 %collective-permute-start.8 = (f32[64,256]{1,0:T(8,128)S(1)}, f32[64,256]{1,0:T(8,128)S(1)}, u32[]{:S(2)}, u32[]{:S(2)}) collective-permute-start(f32[64,256]{1,0:T(8,128)S(1)} %get-tuple-element.48), channel_id=1, source_target_pairs={{32,64},{96,128},{160,192},{224,256},{288,320},{352,384},{416,448}... | collective-permute-start | bytes 196616 | tf_op jit(solution)/shard_map/ppermute | solution.py:78
  119.4 3.4 %collective-permute-start.9 = (f32[64,256]{1,0:T(8,128)S(1)}, f32[64,256]{1,0:T(8,128)S(1)}, u32[]{:S(2)}, u32[]{:S(2)}) collective-permute-start(f32[64,256]{1,0:T(8,128)S(1)} %get-tuple-element.49), channel_id=1, source_target_pairs={{0,8},{16,24},{8,0},{24,16},{1,9},{17,25},{9,1},{25,17},{2,10},{18... | collective-permute-start | bytes 196616 | tf_op jit(solution)/shard_map/ppermute | solution.py:78
  123.7 1.4 %step2.1 = f32[96,256]{1,0:T(8,128)} custom-call(f32[2]{0:T(128)S(1)} %get-tuple-element.33.refs_0_, f32[96,512]{1,0:T(8,128)S(1)} %coupling.1.refs_1_, f32[384,96]{1,0:T(8,128)S(1)} %get-tuple-element.36.ft_ref.refs_2_, f32[96,256]{1,0:T(8,128)S(1)} %get-tuple-element.46.refs_3_, f32[96,256]{1,0:T(8,128)S(1)} %get-tuple-element.41.refs_3_.refs_4_, ...), custom_call_target="tpu_custom_call" | custom-call | tf_op jit(solution)/shard_map/step2/pallas_call | solution.py:347
  (19 shorter events, 3.4 us)
Async XLA Ops:
  0.0 0.8 copy-start.2
  0.8 66.3 %copy-start.1 = (f32[1,1,1,96,256]{4,3,2,1,0:T(8,128)S(1)}, f32[1,1,1,96,256]{4,3,2,1,0:T(8,128)}, u32[]{:S(2)}) copy-start(f32[1,1,1,96,256]{4,3,2,1,0:T(8,128)} %param.5) | copy-start | bytes 294916
  26.0 41.1 %all-to-all-start.1 = ((f32[32,1,128]{2,1,0:T(1,128)}), f32[32,1,128]{2,1,0:T(1,128)S(1)}, u32[]{:S(2)}, u32[]{:S(2)}) async-start(f32[32,1,128]{2,1,0:T(1,128)} %get-tuple-element.28), calls=%async_computation.1 | async-start | bytes 32768 | tf_op jit(solution)/shard_map/all_to_all | solution.py:313
  45.9 5.9 %collective-permute-start = (f32[8,256]{1,0:T(8,128)S(1)}, f32[8,256]{1,0:T(8,128)S(1)}, u32[]{:S(2)}, u32[]{:S(2)}) collective-permute-start(f32[8,256]{1,0:T(8,128)S(1)} %get-tuple-element.29.wide_ref), channel_id=1, source_target_pairs={{0,32},{32,64},{64,96},{96,128},{128,160},{160,192},{192,224},{224... | collective-permute-start | bytes 24584 | tf_op jit(solution)/shard_map/ppermute | solution.py:25
  51.8 1.4 %copy-start = (f32[1,1,1,96,4096]{4,3,2,1,0:T(8,128)S(1)}, f32[1,1,1,96,4096]{4,3,2,1,0:T(8,128)}, u32[]{:S(2)}) copy-start(f32[1,1,1,96,4096]{4,3,2,1,0:T(8,128)} %param.3) | copy-start | bytes 4718596
  71.4 15.9 %all-to-all-start.2 = ((f32[8,64,256]{2,1,0:T(8,128)}), f32[8,64,256]{2,1,0:T(8,128)S(1)}, u32[]{:S(2)}, u32[]{:S(2)}) async-start(f32[8,64,256]{2,1,0:T(8,128)} %get-tuple-element.40), calls=%async_computation.2 | async-start | bytes 1048576 | tf_op jit(solution)/shard_map/all_to_all | solution.py:341
  75.3 11.7 %collective-permute-start.1 = (f32[64,256]{1,0:T(8,128)S(1)}, f32[64,256]{1,0:T(8,128)S(1)}, u32[]{:S(2)}, u32[]{:S(2)}) collective-permute-start(f32[64,256]{1,0:T(8,128)S(1)} %get-tuple-element.37), channel_id=1, source_target_pairs={{1,2},{3,4},{5,6},{7,0},{2,1},{4,3},{6,5},{0,7},{9,10},{11,12},{13... | collective-permute-start | bytes 196616 | tf_op jit(solution)/shard_map/ppermute | solution.py:78
  80.2 6.8 %collective-permute-start.2 = (f32[64,256]{1,0:T(8,128)S(1)}, f32[64,256]{1,0:T(8,128)S(1)}, u32[]{:S(2)}, u32[]{:S(2)}) collective-permute-start(f32[64,256]{1,0:T(8,128)S(1)} %get-tuple-element.38), channel_id=1, source_target_pairs={{32,64},{96,128},{160,192},{224,256},{288,320},{352,384},{416,448}... | collective-permute-start | bytes 196616 | tf_op jit(solution)/shard_map/ppermute | solution.py:78
  82.9 4.3 %collective-permute-start.3 = (f32[64,256]{1,0:T(8,128)S(1)}, f32[64,256]{1,0:T(8,128)S(1)}, u32[]{:S(2)}, u32[]{:S(2)}) collective-permute-start(f32[64,256]{1,0:T(8,128)S(1)} %get-tuple-element.39), channel_id=1, source_target_pairs={{0,8},{16,24},{8,0},{24,16},{1,9},{17,25},{9,1},{25,17},{2,10},{18... | collective-permute-start | bytes 196616 | tf_op jit(solution)/shard_map/ppermute | solution.py:78
  89.0 17.3 %all-to-all-start.3 = ((f32[8,64,256]{2,1,0:T(8,128)}), f32[8,64,256]{2,1,0:T(8,128)S(1)}, u32[]{:S(2)}, u32[]{:S(2)}) async-start(f32[8,64,256]{2,1,0:T(8,128)} %get-tuple-element.45), calls=%async_computation.3 | async-start | bytes 1048576 | tf_op jit(solution)/shard_map/all_to_all | solution.py:341
  92.5 12.9 %collective-permute-start.4 = (f32[64,256]{1,0:T(8,128)S(1)}, f32[64,256]{1,0:T(8,128)S(1)}, u32[]{:S(2)}, u32[]{:S(2)}) collective-permute-start(f32[64,256]{1,0:T(8,128)S(1)} %get-tuple-element.42), channel_id=1, source_target_pairs={{1,2},{3,4},{5,6},{7,0},{2,1},{4,3},{6,5},{0,7},{9,10},{11,12},{13... | collective-permute-start | bytes 196616 | tf_op jit(solution)/shard_map/ppermute | solution.py:78
  98.8 6.6 %collective-permute-start.5 = (f32[64,256]{1,0:T(8,128)S(1)}, f32[64,256]{1,0:T(8,128)S(1)}, u32[]{:S(2)}, u32[]{:S(2)}) collective-permute-start(f32[64,256]{1,0:T(8,128)S(1)} %get-tuple-element.43), channel_id=1, source_target_pairs={{32,64},{96,128},{160,192},{224,256},{288,320},{352,384},{416,448}... | collective-permute-start | bytes 196616 | tf_op jit(solution)/shard_map/ppermute | solution.py:78
  102.3 4.0 %collective-permute-start.6 = (f32[64,256]{1,0:T(8,128)S(1)}, f32[64,256]{1,0:T(8,128)S(1)}, u32[]{:S(2)}, u32[]{:S(2)}) collective-permute-start(f32[64,256]{1,0:T(8,128)S(1)} %get-tuple-element.44), channel_id=1, source_target_pairs={{0,8},{16,24},{8,0},{24,16},{1,9},{17,25},{9,1},{25,17},{2,10},{18... | collective-permute-start | bytes 196616 | tf_op jit(solution)/shard_map/ppermute | solution.py:78
  108.0 15.7 %all-to-all-start.4 = ((f32[8,64,256]{2,1,0:T(8,128)}), f32[8,64,256]{2,1,0:T(8,128)S(1)}, u32[]{:S(2)}, u32[]{:S(2)}) async-start(f32[8,64,256]{2,1,0:T(8,128)} %get-tuple-element.50), calls=%async_computation.4 | async-start | bytes 1048576 | tf_op jit(solution)/shard_map/all_to_all | solution.py:341
  111.5 11.3 %collective-permute-start.7 = (f32[64,256]{1,0:T(8,128)S(1)}, f32[64,256]{1,0:T(8,128)S(1)}, u32[]{:S(2)}, u32[]{:S(2)}) collective-permute-start(f32[64,256]{1,0:T(8,128)S(1)} %get-tuple-element.47), channel_id=1, source_target_pairs={{1,2},{3,4},{5,6},{7,0},{2,1},{4,3},{6,5},{0,7},{9,10},{11,12},{13... | collective-permute-start | bytes 196616 | tf_op jit(solution)/shard_map/ppermute | solution.py:78
  115.5 7.3 %collective-permute-start.8 = (f32[64,256]{1,0:T(8,128)S(1)}, f32[64,256]{1,0:T(8,128)S(1)}, u32[]{:S(2)}, u32[]{:S(2)}) collective-permute-start(f32[64,256]{1,0:T(8,128)S(1)} %get-tuple-element.48), channel_id=1, source_target_pairs={{32,64},{96,128},{160,192},{224,256},{288,320},{352,384},{416,448}... | collective-permute-start | bytes 196616 | tf_op jit(solution)/shard_map/ppermute | solution.py:78
  119.4 4.3 %collective-permute-start.9 = (f32[64,256]{1,0:T(8,128)S(1)}, f32[64,256]{1,0:T(8,128)S(1)}, u32[]{:S(2)}, u32[]{:S(2)}) collective-permute-start(f32[64,256]{1,0:T(8,128)S(1)} %get-tuple-element.49), channel_id=1, source_target_pairs={{0,8},{16,24},{8,0},{24,16},{1,9},{17,25},{9,1},{25,17},{2,10},{18... | collective-permute-start | bytes 196616 | tf_op jit(solution)/shard_map/ppermute | solution.py:78

commit v8 on v7

--- a/solution.py
+++ b/solution.py
@@ -233,7 +233,7 @@
     send_traces(ft, vectors_ref[...], sent, held_ref, sems)
 
 
-def coupling_kernel(basis_ref, own_ref, ft_ref, df_ref):
+def coupling_kernel(basis_ref, own_ref, ft_ref, near_ref, swap_ref):
     basis = basis_ref[...]
     own = own_ref[:1] + SHIFT
     cell = lanes((ROWS, WIDTH))
@@ -253,23 +253,23 @@
     )
     applied = own * basis - 0.5 * total
     diagonal = dot3(split(basis), split(applied), (((1,), (1,)), ((), ())))
-    df_ref[:, :BODY] = -0.5 * ft_ref[...].T
-    df_ref[:, BODY : BODY + ROWS] = diagonal
-    df_ref[:, BODY + ROWS :] = jnp.zeros((ROWS, WIDTH - BODY - ROWS), jnp.float32)
-
-
-def step_kernel(first, last, scal_ref, df_ref, ft_ref, now_ref, prior_ref, *refs):
-    swap_refs, cube_ref, out_ref, rest = refs[:3], refs[3], refs[4], refs[5:]
+    half = BODY // 2
+    swap_ref[...] = -0.5 * ft_ref[:half].T
+    near_ref[:, :half] = -0.5 * ft_ref[half:].T
+    near_ref[:, half:] = diagonal
+
+
+def near_kernel(scal_ref, near_ref, now_ref, cube_ref, out_ref):
     now = now_ref[...]
     at = place()
-    halos = [ref[...] for ref in swap_refs] + [cube_ref[at ^ flip] for flip in FLIPS]
-    first_half = halos[:4]
-    second_half = halos[4:] + [now, jnp.zeros((WIDTH - BODY - ROWS, COLS), jnp.float32)]
-    result = dot3(
-        split(df_ref[:, : WIDTH // 2]), split(jnp.concatenate(first_half, axis=0))
-    ) + dot3(split(df_ref[:, WIDTH // 2 :]), split(jnp.concatenate(second_half, axis=0)))
-    centre, half_width = scal_ref[0], scal_ref[1]
-    following = (result - centre * now) / half_width
+    stacked = jnp.concatenate([cube_ref[at ^ flip] for flip in FLIPS] + [now], axis=0)
+    out_ref[...] = dot3(split(near_ref[...]), split(stacked)) - scal_ref[0] * now
+
+
+def step_kernel(first, last, scal_ref, swap_ref, ft_ref, part_ref, prior_ref, *refs):
+    halos = jnp.concatenate([ref[...] for ref in refs[:3]], axis=0)
+    out_ref, rest = refs[3], refs[4:]
+    following = (dot3(split(swap_ref[...]), split(halos)) + part_ref[...]) / scal_ref[1]
     if not first:
         following = 2.0 * following - prior_ref[...]
     out_ref[...] = following
@@ -332,13 +332,19 @@
         (vmem(), vmem(), smem()) + sent_specs,
         [pltpu.VMEM((WIDTH, 128), f32)] + staging,
     )(peaks, *powers, start)
-    df = call(coupling_kernel, "coupling", of(ROWS, WIDTH), [vmem()] * 3, vmem())(basis, own, ft)
+    half = BODY // 2
+    near, far = call(
+        coupling_kernel, "coupling", (of(ROWS, half + ROWS), of(ROWS, half)), [vmem()] * 3, (vmem(),) * 2
+    )(basis, own, ft)
 
     groups = cubes()
     prior, now = start, start
     for step in range(DG_STEPS):
         halos = [swapped(trace, *pairing) for trace, pairing in zip(sent, SWAPS)]
-        halos.append(lax.all_to_all(sent[3], AXES, 0, 0, axis_index_groups=groups))
+        cube = lax.all_to_all(sent[3], AXES, 0, 0, axis_index_groups=groups)
+        part = call(
+            near_kernel, f"near{step}", of(ROWS, COLS), [smem()] + [vmem()] * 3, vmem()
+        )(scal, near, now, cube)
         last = step == DG_STEPS - 1
 
         def body(*refs, step=step, last=last):
@@ -348,10 +354,10 @@
             body,
             f"step{step}",
             (of(ROWS, COLS),) + (() if last else sent_shapes),
-            [smem()] + [vmem()] * 8,
+            [smem()] + [vmem()] * 7,
             (vmem(),) + (() if last else sent_specs),
             () if last else staging,
-        )(scal, df, ft, now, prior, *halos)
+        )(scal, far, ft, part, prior, *halos)
         prior, now = now, following
     return now.reshape(coefficients.shape)
 

time: 126 us -> 126 us (level)
  Pallas kernels: 14.5 us -> 16.8 us
  waiting for transfers between devices: 14.8 us -> 13 us
    pallas_call x1 -> x4, Pallas kernels: 0.6 us -> 3.02 us  [the longest x3 2.35 us: per_device(): call(near_kernel, f'near{step}', of(ROWS, COLS), [smem()] + [vmem()] * 3,...]
    ppermute x9, waiting for transfers between devices: 1.99 us -> 0.13 us  [swapped(): return lax.ppermute(shard, axis, pairs + [(b, a) for a, b in pairs])]
  transfers between devices with their start and end apart: 14 -> 14, of which waited for: 5 -> 4; matrix products, arithmetic and copies ran while one was open for 0% -> 0% of each run, Pallas kernels for 4% -> 5%
where the time goes in v8:
time: 126 us; the launch traced here: 125 us
  starting transfers between devices  68.5 us (54%)
  blocking collectives  24.3 us (19%)
  Pallas kernels  16.8 us (13%)
  waiting for transfers between devices  13 us (10%)
  local copies, waits for them, and re-layouts  2.17 us (2%)
    ppermute x9, starting transfers between devices, swapped(): return lax.ppermute(shard, axis, pairs + [(b, a) for a, b in pairs])  34.6 us
    all_to_all x1, blocking collectives, per_device(): tiles = lax.all_to_all(tile, ('gy', 'gz'), 0, 0)  24.3 us
    all_to_all x1, starting transfers between devices, per_device(): peaks = lax.all_to_all(peak, 'gx', 0, 0)  19.9 us
    all_to_all x3, starting transfers between devices, per_device(): cube = lax.all_to_all(sent[3], AXES, 0, 0, axis_index_groups=groups)  10.9 us
    all_to_all x1, waiting for transfers between devices, per_device(): peaks = lax.all_to_all(peak, 'gx', 0, 0)  10.1 us
    pallas_call x3, Pallas kernels, per_device(): call(body, f'step{step}', (of(ROWS, COLS),) + (() if last else sent_shape...  4.86 us
    pallas_call x1, Pallas kernels, per_device(): call(basis_kernel, 'basis', (of(ROWS, WIDTH), of(BODY, ROWS), of(2)) + se...  4.27 us
    pallas_call x1, Pallas kernels, per_device(): call(filter_kernel, 'powers', (of(ROWS, WIDTH),) * 3 + (of(8, WIDTH),), [...  3.82 us
  transfers between devices with their start and end apart: 14, of which 4 were waited for; matrix products, arithmetic and copies ran while one was open for 0% of the time, Pallas kernels for 5%

profile of v8, /device:TPU:1, one launch (start us, length us, event | category | flops | bytes accessed | tf_op | source)
XLA Modules:
  0.0 125.1 jit_solution(14768587124895381123)
XLA Ops:
  0.9 24.3 %all_to_all.25.tiles_ref = f32[32,8,128]{2,1,0:T(8,128)S(1)} all-to-all(f32[32,8,128]{2,1,0:T(8,128)S(1)} %tile.1), channel_id=1, replica_groups=mesh['gx'=32,'gy'=4,'gz'=8] {'gy','gz'}, dimensions={0} | all-to-all | bytes 262144 | tf_op jit(solution)/shard_map/all_to_all | solution.py:309
  26.0 19.9 %all-to-all-start.1 = ((f32[32,1,128]{2,1,0:T(1,128)}), f32[32,1,128]{2,1,0:T(1,128)S(1)}, u32[]{:S(2)}, u32[]{:S(2)}) async-start(f32[32,1,128]{2,1,0:T(1,128)} %get-tuple-element.30), calls=%async_computation.1 | async-start | bytes 32768 | tf_op jit(solution)/shard_map/all_to_all | solution.py:313
  45.9 3.1 %collective-permute-start = (f32[8,256]{1,0:T(8,128)S(1)}, f32[8,256]{1,0:T(8,128)S(1)}, u32[]{:S(2)}, u32[]{:S(2)}) collective-permute-start(f32[8,256]{1,0:T(8,128)S(1)} %get-tuple-element.31.wide_ref), channel_id=1, source_target_pairs={{0,32},{32,64},{64,96},{96,128},{128,160},{160,192},{192,224},{224... | collective-permute-start | bytes 24584 | tf_op jit(solution)/shard_map/ppermute | solution.py:25
  49.0 2.8 %collective-permute-done.below_ref = f32[8,256]{1,0:T(8,128)S(1)} collective-permute-done((f32[8,256]{1,0:T(8,128)S(1)}, f32[8,256]{1,0:T(8,128)S(1)}, u32[]{:S(2)}, u32[]{:S(2)}) %collective-permute-start) | collective-permute-done | bytes 8224 | tf_op jit(solution)/shard_map/ppermute | solution.py:25
  51.8 1.4 %copy-done = f32[1,1,1,96,4096]{4,3,2,1,0:T(8,128)S(1)} copy-done((f32[1,1,1,96,4096]{4,3,2,1,0:T(8,128)S(1)}, f32[1,1,1,96,4096]{4,3,2,1,0:T(8,128)}, u32[]{:S(2)}) %copy-start) | copy-done | bytes 1572888
  53.2 3.8 %powers.1 = (f32[96,512]{1,0:T(8,128)S(1)}, f32[96,512]{1,0:T(8,128)S(1)}, f32[96,512]{1,0:T(8,128)S(1)}, f32[8,512]{1,0:T(8,128)S(1)}) custom-call(f32[8,256]{1,0:T(8,128)S(1)} %get-tuple-element.31.wide_ref, f32[8,256]{1,0:T(8,128)S(1)} %collective-permute-done.below_ref, f32[96,4096]{1,0:T(8,128)S(1)} %bitcast.3), custom_call_target="tpu_custom_call" | custom-call | tf_op jit(solution)/shard_map/powers/pallas_call | solution.py:315
  57.0 10.1 %all-to-all-done.1.peaks_ref = f32[32,1,128]{2,1,0:T(1,128)S(1)} async-done(((f32[32,1,128]{2,1,0:T(1,128)}), f32[32,1,128]{2,1,0:T(1,128)S(1)}, u32[]{:S(2)}, u32[]{:S(2)}) %all-to-all-start.1) | async-done | bytes 16416 | tf_op jit(solution)/shard_map/all_to_all | solution.py:313
  67.1 4.3 %basis.1 = (f32[96,512]{1,0:T(8,128)S(1)}, f32[384,96]{1,0:T(8,128)S(1)}, f32[2]{0:T(128)S(1)}, f32[64,256]{1,0:T(8,128)S(1)}, f32[64,256]{1,0:T(8,128)S(1)}, /*...) custom-call(f32[32,1,128]{2,1,0:T(1,128)S(1)} %all-to-all-done.1.peaks_ref, f32[96,512]{1,0:T(8,128)S(1)} %get-tuple-element.32.u0_ref, ...), custom_call_target="tpu_custom_call" | custom-call | tf_op jit(solution)/shard_map/basis/pallas_call | solution.py:327
  71.4 3.9 %all-to-all-start.2 = ((f32[8,64,256]{2,1,0:T(8,128)}), f32[8,64,256]{2,1,0:T(8,128)S(1)}, u32[]{:S(2)}, u32[]{:S(2)}) async-start(f32[8,64,256]{2,1,0:T(8,128)} %get-tuple-element.41), calls=%async_computation.2 | async-start | bytes 1048576 | tf_op jit(solution)/shard_map/all_to_all | solution.py:344
  75.3 4.9 %collective-permute-start.1 = (f32[64,256]{1,0:T(8,128)S(1)}, f32[64,256]{1,0:T(8,128)S(1)}, u32[]{:S(2)}, u32[]{:S(2)}) collective-permute-start(f32[64,256]{1,0:T(8,128)S(1)} %get-tuple-element.42), channel_id=1, source_target_pairs={{1,2},{3,4},{5,6},{7,0},{2,1},{4,3},{6,5},{0,7},{9,10},{11,12},{13... | collective-permute-start | bytes 196616 | tf_op jit(solution)/shard_map/ppermute | solution.py:78
  80.2 2.8 %collective-permute-start.2 = (f32[64,256]{1,0:T(8,128)S(1)}, f32[64,256]{1,0:T(8,128)S(1)}, u32[]{:S(2)}, u32[]{:S(2)}) collective-permute-start(f32[64,256]{1,0:T(8,128)S(1)} %get-tuple-element.43), channel_id=1, source_target_pairs={{32,64},{96,128},{160,192},{224,256},{288,320},{352,384},{416,448}... | collective-permute-start | bytes 196616 | tf_op jit(solution)/shard_map/ppermute | solution.py:78
  83.0 3.4 %collective-permute-start.3 = (f32[64,256]{1,0:T(8,128)S(1)}, f32[64,256]{1,0:T(8,128)S(1)}, u32[]{:S(2)}, u32[]{:S(2)}) collective-permute-start(f32[64,256]{1,0:T(8,128)S(1)} %get-tuple-element.44), channel_id=1, source_target_pairs={{0,8},{16,24},{8,0},{24,16},{1,9},{17,25},{9,1},{25,17},{2,10},{18... | collective-permute-start | bytes 196616 | tf_op jit(solution)/shard_map/ppermute | solution.py:78
  87.0 0.8 near0.1.refs_3_
  87.8 1.7 %step0.1 = (f32[96,256]{1,0:T(8,128)S(1)}, f32[64,256]{1,0:T(8,128)S(1)}, f32[64,256]{1,0:T(8,128)S(1)}, f32[64,256]{1,0:T(8,128)S(1)}, f32[8,64,256]{2,1,0:T(8,128)}) custom-call(f32[2]{0:T(128)S(1)} %get-tuple-element.35.scal_ref.refs_0_, f32[96,192]{1,0:T(8,128)S(1)} %get-tuple-element.39.refs_1_, f32[384,96]{1,0:T(8,128)S(1)} %get-tuple-element.38.ft_ref.refs_2_, ...), custom_call_target="tpu_custom_call" | custom-call | tf_op jit(solution)/shard_map/step0/pallas_call | solution.py:353
  89.6 3.5 %all-to-all-start.3 = ((f32[8,64,256]{2,1,0:T(8,128)}), f32[8,64,256]{2,1,0:T(8,128)S(1)}, u32[]{:S(2)}, u32[]{:S(2)}) async-start(f32[8,64,256]{2,1,0:T(8,128)} %get-tuple-element.46), calls=%async_computation.3 | async-start | bytes 1048576 | tf_op jit(solution)/shard_map/all_to_all | solution.py:344
  93.1 5.7 %collective-permute-start.4 = (f32[64,256]{1,0:T(8,128)S(1)}, f32[64,256]{1,0:T(8,128)S(1)}, u32[]{:S(2)}, u32[]{:S(2)}) collective-permute-start(f32[64,256]{1,0:T(8,128)S(1)} %get-tuple-element.47), channel_id=1, source_target_pairs={{1,2},{3,4},{5,6},{7,0},{2,1},{4,3},{6,5},{0,7},{9,10},{11,12},{13... | collective-permute-start | bytes 196616 | tf_op jit(solution)/shard_map/ppermute | solution.py:78
  98.8 3.7 %collective-permute-start.5 = (f32[64,256]{1,0:T(8,128)S(1)}, f32[64,256]{1,0:T(8,128)S(1)}, u32[]{:S(2)}, u32[]{:S(2)}) collective-permute-start(f32[64,256]{1,0:T(8,128)S(1)} %get-tuple-element.48), channel_id=1, source_target_pairs={{32,64},{96,128},{160,192},{224,256},{288,320},{352,384},{416,448}... | collective-permute-start | bytes 196616 | tf_op jit(solution)/shard_map/ppermute | solution.py:78
  102.5 3.1 %collective-permute-start.6 = (f32[64,256]{1,0:T(8,128)S(1)}, f32[64,256]{1,0:T(8,128)S(1)}, u32[]{:S(2)}, u32[]{:S(2)}) collective-permute-start(f32[64,256]{1,0:T(8,128)S(1)} %get-tuple-element.49), channel_id=1, source_target_pairs={{0,8},{16,24},{8,0},{24,16},{1,9},{17,25},{9,1},{25,17},{2,10},{18... | collective-permute-start | bytes 196616 | tf_op jit(solution)/shard_map/ppermute | solution.py:78
  106.5 1.7 %step1.1 = (f32[96,256]{1,0:T(8,128)S(1)}, f32[64,256]{1,0:T(8,128)S(1)}, f32[64,256]{1,0:T(8,128)S(1)}, f32[64,256]{1,0:T(8,128)S(1)}, f32[8,64,256]{2,1,0:T(8,128)}) custom-call(f32[2]{0:T(128)S(1)} %get-tuple-element.35.scal_ref.refs_0_, f32[96,192]{1,0:T(8,128)S(1)} %get-tuple-element.39.refs_1_, f32[384,96]{1,0:T(8,128)S(1)} %get-tuple-element.38.ft_ref.refs_2_, ...), custom_call_target="tpu_custom_call" | custom-call | tf_op jit(solution)/shard_map/step1/pallas_call | solution.py:353
  108.3 3.5 %all-to-all-start.4 = ((f32[8,64,256]{2,1,0:T(8,128)}), f32[8,64,256]{2,1,0:T(8,128)S(1)}, u32[]{:S(2)}, u32[]{:S(2)}) async-start(f32[8,64,256]{2,1,0:T(8,128)} %get-tuple-element.51), calls=%async_computation.4 | async-start | bytes 1048576 | tf_op jit(solution)/shard_map/all_to_all | solution.py:344
  111.8 4.3 %collective-permute-start.7 = (f32[64,256]{1,0:T(8,128)S(1)}, f32[64,256]{1,0:T(8,128)S(1)}, u32[]{:S(2)}, u32[]{:S(2)}) collective-permute-start(f32[64,256]{1,0:T(8,128)S(1)} %get-tuple-element.52), channel_id=1, source_target_pairs={{1,2},{3,4},{5,6},{7,0},{2,1},{4,3},{6,5},{0,7},{9,10},{11,12},{13... | collective-permute-start | bytes 196616 | tf_op jit(solution)/shard_map/ppermute | solution.py:78
  116.1 3.6 %collective-permute-start.8 = (f32[64,256]{1,0:T(8,128)S(1)}, f32[64,256]{1,0:T(8,128)S(1)}, u32[]{:S(2)}, u32[]{:S(2)}) collective-permute-start(f32[64,256]{1,0:T(8,128)S(1)} %get-tuple-element.53), channel_id=1, source_target_pairs={{32,64},{96,128},{160,192},{224,256},{288,320},{352,384},{416,448}... | collective-permute-start | bytes 196616 | tf_op jit(solution)/shard_map/ppermute | solution.py:78
  119.7 3.1 %collective-permute-start.9 = (f32[64,256]{1,0:T(8,128)S(1)}, f32[64,256]{1,0:T(8,128)S(1)}, u32[]{:S(2)}, u32[]{:S(2)}) collective-permute-start(f32[64,256]{1,0:T(8,128)S(1)} %get-tuple-element.54), channel_id=1, source_target_pairs={{0,8},{16,24},{8,0},{24,16},{1,9},{17,25},{9,1},{25,17},{2,10},{18... | collective-permute-start | bytes 196616 | tf_op jit(solution)/shard_map/ppermute | solution.py:78
  123.7 1.4 %step2.1 = f32[96,256]{1,0:T(8,128)} custom-call(f32[2]{0:T(128)S(1)} %get-tuple-element.35.scal_ref.refs_0_, f32[96,192]{1,0:T(8,128)S(1)} %get-tuple-element.39.refs_1_, f32[384,96]{1,0:T(8,128)S(1)} %get-tuple-element.38.ft_ref.refs_2_, f32[96,256]{1,0:T(8,128)S(1)} %near2.1.refs_3_, f32[96,256]{1,0:T(8,128)S(1)} %get-tuple-element.45.now_ref.refs_4_, ...), custom_call_target="tpu_custom_call" | custom-call | tf_op jit(solution)/shard_map/step2/pallas_call | solution.py:353
  (22 shorter events, 4.0 us)
Async XLA Ops:
  0.0 0.8 copy-start.2
  0.8 66.3 %copy-start.1 = (f32[1,1,1,96,256]{4,3,2,1,0:T(8,128)S(1)}, f32[1,1,1,96,256]{4,3,2,1,0:T(8,128)}, u32[]{:S(2)}) copy-start(f32[1,1,1,96,256]{4,3,2,1,0:T(8,128)} %param.5) | copy-start | bytes 294916
  26.0 41.1 %all-to-all-start.1 = ((f32[32,1,128]{2,1,0:T(1,128)}), f32[32,1,128]{2,1,0:T(1,128)S(1)}, u32[]{:S(2)}, u32[]{:S(2)}) async-start(f32[32,1,128]{2,1,0:T(1,128)} %get-tuple-element.30), calls=%async_computation.1 | async-start | bytes 32768 | tf_op jit(solution)/shard_map/all_to_all | solution.py:313
  45.9 5.9 %collective-permute-start = (f32[8,256]{1,0:T(8,128)S(1)}, f32[8,256]{1,0:T(8,128)S(1)}, u32[]{:S(2)}, u32[]{:S(2)}) collective-permute-start(f32[8,256]{1,0:T(8,128)S(1)} %get-tuple-element.31.wide_ref), channel_id=1, source_target_pairs={{0,32},{32,64},{64,96},{96,128},{128,160},{160,192},{192,224},{224... | collective-permute-start | bytes 24584 | tf_op jit(solution)/shard_map/ppermute | solution.py:25
  51.8 1.4 %copy-start = (f32[1,1,1,96,4096]{4,3,2,1,0:T(8,128)S(1)}, f32[1,1,1,96,4096]{4,3,2,1,0:T(8,128)}, u32[]{:S(2)}) copy-start(f32[1,1,1,96,4096]{4,3,2,1,0:T(8,128)} %param.3) | copy-start | bytes 4718596
  71.4 15.6 %all-to-all-start.2 = ((f32[8,64,256]{2,1,0:T(8,128)}), f32[8,64,256]{2,1,0:T(8,128)S(1)}, u32[]{:S(2)}, u32[]{:S(2)}) async-start(f32[8,64,256]{2,1,0:T(8,128)} %get-tuple-element.41), calls=%async_computation.2 | async-start | bytes 1048576 | tf_op jit(solution)/shard_map/all_to_all | solution.py:344
  75.3 12.5 %collective-permute-start.1 = (f32[64,256]{1,0:T(8,128)S(1)}, f32[64,256]{1,0:T(8,128)S(1)}, u32[]{:S(2)}, u32[]{:S(2)}) collective-permute-start(f32[64,256]{1,0:T(8,128)S(1)} %get-tuple-element.42), channel_id=1, source_target_pairs={{1,2},{3,4},{5,6},{7,0},{2,1},{4,3},{6,5},{0,7},{9,10},{11,12},{13... | collective-permute-start | bytes 196616 | tf_op jit(solution)/shard_map/ppermute | solution.py:78
  80.2 7.7 %collective-permute-start.2 = (f32[64,256]{1,0:T(8,128)S(1)}, f32[64,256]{1,0:T(8,128)S(1)}, u32[]{:S(2)}, u32[]{:S(2)}) collective-permute-start(f32[64,256]{1,0:T(8,128)S(1)} %get-tuple-element.43), channel_id=1, source_target_pairs={{32,64},{96,128},{160,192},{224,256},{288,320},{352,384},{416,448}... | collective-permute-start | bytes 196616 | tf_op jit(solution)/shard_map/ppermute | solution.py:78
  83.0 4.9 %collective-permute-start.3 = (f32[64,256]{1,0:T(8,128)S(1)}, f32[64,256]{1,0:T(8,128)S(1)}, u32[]{:S(2)}, u32[]{:S(2)}) collective-permute-start(f32[64,256]{1,0:T(8,128)S(1)} %get-tuple-element.44), channel_id=1, source_target_pairs={{0,8},{16,24},{8,0},{24,16},{1,9},{17,25},{9,1},{25,17},{2,10},{18... | collective-permute-start | bytes 196616 | tf_op jit(solution)/shard_map/ppermute | solution.py:78
  89.6 16.0 %all-to-all-start.3 = ((f32[8,64,256]{2,1,0:T(8,128)}), f32[8,64,256]{2,1,0:T(8,128)S(1)}, u32[]{:S(2)}, u32[]{:S(2)}) async-start(f32[8,64,256]{2,1,0:T(8,128)} %get-tuple-element.46), calls=%async_computation.3 | async-start | bytes 1048576 | tf_op jit(solution)/shard_map/all_to_all | solution.py:344
  93.1 13.3 %collective-permute-start.4 = (f32[64,256]{1,0:T(8,128)S(1)}, f32[64,256]{1,0:T(8,128)S(1)}, u32[]{:S(2)}, u32[]{:S(2)}) collective-permute-start(f32[64,256]{1,0:T(8,128)S(1)} %get-tuple-element.47), channel_id=1, source_target_pairs={{1,2},{3,4},{5,6},{7,0},{2,1},{4,3},{6,5},{0,7},{9,10},{11,12},{13... | collective-permute-start | bytes 196616 | tf_op jit(solution)/shard_map/ppermute | solution.py:78
  98.8 7.6 %collective-permute-start.5 = (f32[64,256]{1,0:T(8,128)S(1)}, f32[64,256]{1,0:T(8,128)S(1)}, u32[]{:S(2)}, u32[]{:S(2)}) collective-permute-start(f32[64,256]{1,0:T(8,128)S(1)} %get-tuple-element.48), channel_id=1, source_target_pairs={{32,64},{96,128},{160,192},{224,256},{288,320},{352,384},{416,448}... | collective-permute-start | bytes 196616 | tf_op jit(solution)/shard_map/ppermute | solution.py:78
  102.5 4.0 %collective-permute-start.6 = (f32[64,256]{1,0:T(8,128)S(1)}, f32[64,256]{1,0:T(8,128)S(1)}, u32[]{:S(2)}, u32[]{:S(2)}) collective-permute-start(f32[64,256]{1,0:T(8,128)S(1)} %get-tuple-element.49), channel_id=1, source_target_pairs={{0,8},{16,24},{8,0},{24,16},{1,9},{17,25},{9,1},{25,17},{2,10},{18... | collective-permute-start | bytes 196616 | tf_op jit(solution)/shard_map/ppermute | solution.py:78
  108.3 14.6 %all-to-all-start.4 = ((f32[8,64,256]{2,1,0:T(8,128)}), f32[8,64,256]{2,1,0:T(8,128)S(1)}, u32[]{:S(2)}, u32[]{:S(2)}) async-start(f32[8,64,256]{2,1,0:T(8,128)} %get-tuple-element.51), calls=%async_computation.4 | async-start | bytes 1048576 | tf_op jit(solution)/shard_map/all_to_all | solution.py:344
  111.8 11.9 %collective-permute-start.7 = (f32[64,256]{1,0:T(8,128)S(1)}, f32[64,256]{1,0:T(8,128)S(1)}, u32[]{:S(2)}, u32[]{:S(2)}) collective-permute-start(f32[64,256]{1,0:T(8,128)S(1)} %get-tuple-element.52), channel_id=1, source_target_pairs={{1,2},{3,4},{5,6},{7,0},{2,1},{4,3},{6,5},{0,7},{9,10},{11,12},{13... | collective-permute-start | bytes 196616 | tf_op jit(solution)/shard_map/ppermute | solution.py:78
  116.1 7.5 %collective-permute-start.8 = (f32[64,256]{1,0:T(8,128)S(1)}, f32[64,256]{1,0:T(8,128)S(1)}, u32[]{:S(2)}, u32[]{:S(2)}) collective-permute-start(f32[64,256]{1,0:T(8,128)S(1)} %get-tuple-element.53), channel_id=1, source_target_pairs={{32,64},{96,128},{160,192},{224,256},{288,320},{352,384},{416,448}... | collective-permute-start | bytes 196616 | tf_op jit(solution)/shard_map/ppermute | solution.py:78
  119.7 4.0 %collective-permute-start.9 = (f32[64,256]{1,0:T(8,128)S(1)}, f32[64,256]{1,0:T(8,128)S(1)}, u32[]{:S(2)}, u32[]{:S(2)}) collective-permute-start(f32[64,256]{1,0:T(8,128)S(1)} %get-tuple-element.54), channel_id=1, source_target_pairs={{0,8},{16,24},{8,0},{24,16},{1,9},{17,25},{9,1},{25,17},{2,10},{18... | collective-permute-start | bytes 196616 | tf_op jit(solution)/shard_map/ppermute | solution.py:78

commit v9 on v8

--- a/solution.py
+++ b/solution.py
@@ -61,7 +61,7 @@
     return lax.broadcasted_iota(jnp.int32, shape, len(shape) - 1)
 
 
-SWAPS = (("gz", 1), ("gx", 1), ("gy", 0))
+SWAPS = (("gx", 1), ("gz", 1), ("gy", 0))
 CUBE_PAIRS = (("gx", 0), ("gy", 1), ("gz", 0))
 SLOTS = SWAPS + CUBE_PAIRS
 AXES = ("gx", "gy", "gz")

time: 126 us -> 128 us (1.016)
  starting transfers between devices: 68.5 us -> 70.9 us
    ppermute x9, starting transfers between devices: 34.6 us -> 36.9 us  [swapped(): return lax.ppermute(shard, axis, pairs + [(b, a) for a, b in pairs])]
where the time goes in v9:
time: 128 us; the launch traced here: 127 us
  starting transfers between devices  70.9 us (55%)
  blocking collectives  24.3 us (19%)
  Pallas kernels  16.8 us (13%)
  waiting for transfers between devices  13 us (10%)
  local copies, waits for them, and re-layouts  2.17 us (2%)
    ppermute x9, starting transfers between devices, swapped(): return lax.ppermute(shard, axis, pairs + [(b, a) for a, b in pairs])  36.9 us
    all_to_all x1, blocking collectives, per_device(): tiles = lax.all_to_all(tile, ('gy', 'gz'), 0, 0)  24.3 us
    all_to_all x1, starting transfers between devices, per_device(): peaks = lax.all_to_all(peak, 'gx', 0, 0)  19.9 us
    all_to_all x3, starting transfers between devices, per_device(): cube = lax.all_to_all(sent[3], AXES, 0, 0, axis_index_groups=groups)  10.9 us
    all_to_all x1, waiting for transfers between devices, per_device(): peaks = lax.all_to_all(peak, 'gx', 0, 0)  10.1 us
    pallas_call x3, Pallas kernels, per_device(): call(body, f'step{step}', (of(ROWS, COLS),) + (() if last else sent_shape...  4.84 us
    pallas_call x1, Pallas kernels, per_device(): call(basis_kernel, 'basis', (of(ROWS, WIDTH), of(BODY, ROWS), of(2)) + se...  4.27 us
    pallas_call x1, Pallas kernels, per_device(): call(filter_kernel, 'powers', (of(ROWS, WIDTH),) * 3 + (of(8, WIDTH),), [...  3.82 us
  transfers between devices with their start and end apart: 14, of which 4 were waited for; matrix products, arithmetic and copies ran while one was open for 0% of the time, Pallas kernels for 5%

profile of v9, /device:TPU:1, one launch (start us, length us, event | category | flops | bytes accessed | tf_op | source)
XLA Modules:
  0.0 127.4 jit_solution(18293817710891702556)
XLA Ops:
  0.9 24.3 %all_to_all.25.tiles_ref = f32[32,8,128]{2,1,0:T(8,128)S(1)} all-to-all(f32[32,8,128]{2,1,0:T(8,128)S(1)} %tile.1), channel_id=1, replica_groups=mesh['gx'=32,'gy'=4,'gz'=8] {'gy','gz'}, dimensions={0} | all-to-all | bytes 262144 | tf_op jit(solution)/shard_map/all_to_all | solution.py:309
  26.0 19.9 %all-to-all-start.1 = ((f32[32,1,128]{2,1,0:T(1,128)}), f32[32,1,128]{2,1,0:T(1,128)S(1)}, u32[]{:S(2)}, u32[]{:S(2)}) async-start(f32[32,1,128]{2,1,0:T(1,128)} %get-tuple-element.30), calls=%async_computation.1 | async-start | bytes 32768 | tf_op jit(solution)/shard_map/all_to_all | solution.py:313
  45.9 3.1 %collective-permute-start = (f32[8,256]{1,0:T(8,128)S(1)}, f32[8,256]{1,0:T(8,128)S(1)}, u32[]{:S(2)}, u32[]{:S(2)}) collective-permute-start(f32[8,256]{1,0:T(8,128)S(1)} %get-tuple-element.31.wide_ref), channel_id=1, source_target_pairs={{0,32},{32,64},{64,96},{96,128},{128,160},{160,192},{192,224},{224... | collective-permute-start | bytes 24584 | tf_op jit(solution)/shard_map/ppermute | solution.py:25
  49.0 2.8 %collective-permute-done.below_ref = f32[8,256]{1,0:T(8,128)S(1)} collective-permute-done((f32[8,256]{1,0:T(8,128)S(1)}, f32[8,256]{1,0:T(8,128)S(1)}, u32[]{:S(2)}, u32[]{:S(2)}) %collective-permute-start) | collective-permute-done | bytes 8224 | tf_op jit(solution)/shard_map/ppermute | solution.py:25
  51.8 1.4 %copy-done = f32[1,1,1,96,4096]{4,3,2,1,0:T(8,128)S(1)} copy-done((f32[1,1,1,96,4096]{4,3,2,1,0:T(8,128)S(1)}, f32[1,1,1,96,4096]{4,3,2,1,0:T(8,128)}, u32[]{:S(2)}) %copy-start) | copy-done | bytes 1572888
  53.2 3.8 %powers.1 = (f32[96,512]{1,0:T(8,128)S(1)}, f32[96,512]{1,0:T(8,128)S(1)}, f32[96,512]{1,0:T(8,128)S(1)}, f32[8,512]{1,0:T(8,128)S(1)}) custom-call(f32[8,256]{1,0:T(8,128)S(1)} %get-tuple-element.31.wide_ref, f32[8,256]{1,0:T(8,128)S(1)} %collective-permute-done.below_ref, f32[96,4096]{1,0:T(8,128)S(1)} %bitcast.3), custom_call_target="tpu_custom_call" | custom-call | tf_op jit(solution)/shard_map/powers/pallas_call | solution.py:315
  57.0 10.1 %all-to-all-done.1.peaks_ref = f32[32,1,128]{2,1,0:T(1,128)S(1)} async-done(((f32[32,1,128]{2,1,0:T(1,128)}), f32[32,1,128]{2,1,0:T(1,128)S(1)}, u32[]{:S(2)}, u32[]{:S(2)}) %all-to-all-start.1) | async-done | bytes 16416 | tf_op jit(solution)/shard_map/all_to_all | solution.py:313
  67.1 4.3 %basis.1 = (f32[96,512]{1,0:T(8,128)S(1)}, f32[384,96]{1,0:T(8,128)S(1)}, f32[2]{0:T(128)S(1)}, f32[64,256]{1,0:T(8,128)S(1)}, f32[64,256]{1,0:T(8,128)S(1)}, /*...) custom-call(f32[32,1,128]{2,1,0:T(1,128)S(1)} %all-to-all-done.1.peaks_ref, f32[96,512]{1,0:T(8,128)S(1)} %get-tuple-element.32.u0_ref, ...), custom_call_target="tpu_custom_call" | custom-call | tf_op jit(solution)/shard_map/basis/pallas_call | solution.py:327
  71.4 3.9 %all-to-all-start.2 = ((f32[8,64,256]{2,1,0:T(8,128)}), f32[8,64,256]{2,1,0:T(8,128)S(1)}, u32[]{:S(2)}, u32[]{:S(2)}) async-start(f32[8,64,256]{2,1,0:T(8,128)} %get-tuple-element.41), calls=%async_computation.2 | async-start | bytes 1048576 | tf_op jit(solution)/shard_map/all_to_all | solution.py:344
  75.3 3.0 %collective-permute-start.1 = (f32[64,256]{1,0:T(8,128)S(1)}, f32[64,256]{1,0:T(8,128)S(1)}, u32[]{:S(2)}, u32[]{:S(2)}) collective-permute-start(f32[64,256]{1,0:T(8,128)S(1)} %get-tuple-element.42), channel_id=1, source_target_pairs={{32,64},{96,128},{160,192},{224,256},{288,320},{352,384},{416,448}... | collective-permute-start | bytes 196616 | tf_op jit(solution)/shard_map/ppermute | solution.py:78
  78.3 4.7 %collective-permute-start.2 = (f32[64,256]{1,0:T(8,128)S(1)}, f32[64,256]{1,0:T(8,128)S(1)}, u32[]{:S(2)}, u32[]{:S(2)}) collective-permute-start(f32[64,256]{1,0:T(8,128)S(1)} %get-tuple-element.43), channel_id=1, source_target_pairs={{1,2},{3,4},{5,6},{7,0},{2,1},{4,3},{6,5},{0,7},{9,10},{11,12},{13... | collective-permute-start | bytes 196616 | tf_op jit(solution)/shard_map/ppermute | solution.py:78
  83.0 3.4 %collective-permute-start.3 = (f32[64,256]{1,0:T(8,128)S(1)}, f32[64,256]{1,0:T(8,128)S(1)}, u32[]{:S(2)}, u32[]{:S(2)}) collective-permute-start(f32[64,256]{1,0:T(8,128)S(1)} %get-tuple-element.44), channel_id=1, source_target_pairs={{0,8},{16,24},{8,0},{24,16},{1,9},{17,25},{9,1},{25,17},{2,10},{18... | collective-permute-start | bytes 196616 | tf_op jit(solution)/shard_map/ppermute | solution.py:78
  87.0 0.8 near0.1.refs_3_
  87.8 1.7 %step0.1 = (f32[96,256]{1,0:T(8,128)S(1)}, f32[64,256]{1,0:T(8,128)S(1)}, f32[64,256]{1,0:T(8,128)S(1)}, f32[64,256]{1,0:T(8,128)S(1)}, f32[8,64,256]{2,1,0:T(8,128)}) custom-call(f32[2]{0:T(128)S(1)} %get-tuple-element.35.scal_ref.refs_0_, f32[96,192]{1,0:T(8,128)S(1)} %get-tuple-element.39.refs_1_, f32[384,96]{1,0:T(8,128)S(1)} %get-tuple-element.38.ft_ref.refs_2_, ...), custom_call_target="tpu_custom_call" | custom-call | tf_op jit(solution)/shard_map/step0/pallas_call | solution.py:353
  89.6 3.5 %all-to-all-start.3 = ((f32[8,64,256]{2,1,0:T(8,128)}), f32[8,64,256]{2,1,0:T(8,128)S(1)}, u32[]{:S(2)}, u32[]{:S(2)}) async-start(f32[8,64,256]{2,1,0:T(8,128)} %get-tuple-element.46), calls=%async_computation.3 | async-start | bytes 1048576 | tf_op jit(solution)/shard_map/all_to_all | solution.py:344
  93.1 5.1 %collective-permute-start.4 = (f32[64,256]{1,0:T(8,128)S(1)}, f32[64,256]{1,0:T(8,128)S(1)}, u32[]{:S(2)}, u32[]{:S(2)}) collective-permute-start(f32[64,256]{1,0:T(8,128)S(1)} %get-tuple-element.47), channel_id=1, source_target_pairs={{32,64},{96,128},{160,192},{224,256},{288,320},{352,384},{416,448}... | collective-permute-start | bytes 196616 | tf_op jit(solution)/shard_map/ppermute | solution.py:78
  98.2 5.1 %collective-permute-start.5 = (f32[64,256]{1,0:T(8,128)S(1)}, f32[64,256]{1,0:T(8,128)S(1)}, u32[]{:S(2)}, u32[]{:S(2)}) collective-permute-start(f32[64,256]{1,0:T(8,128)S(1)} %get-tuple-element.48), channel_id=1, source_target_pairs={{1,2},{3,4},{5,6},{7,0},{2,1},{4,3},{6,5},{0,7},{9,10},{11,12},{13... | collective-permute-start | bytes 196616 | tf_op jit(solution)/shard_map/ppermute | solution.py:78
  103.3 3.4 %collective-permute-start.6 = (f32[64,256]{1,0:T(8,128)S(1)}, f32[64,256]{1,0:T(8,128)S(1)}, u32[]{:S(2)}, u32[]{:S(2)}) collective-permute-start(f32[64,256]{1,0:T(8,128)S(1)} %get-tuple-element.49), channel_id=1, source_target_pairs={{0,8},{16,24},{8,0},{24,16},{1,9},{17,25},{9,1},{25,17},{2,10},{18... | collective-permute-start | bytes 196616 | tf_op jit(solution)/shard_map/ppermute | solution.py:78
  107.6 1.7 %step1.1 = (f32[96,256]{1,0:T(8,128)S(1)}, f32[64,256]{1,0:T(8,128)S(1)}, f32[64,256]{1,0:T(8,128)S(1)}, f32[64,256]{1,0:T(8,128)S(1)}, f32[8,64,256]{2,1,0:T(8,128)}) custom-call(f32[2]{0:T(128)S(1)} %get-tuple-element.35.scal_ref.refs_0_, f32[96,192]{1,0:T(8,128)S(1)} %get-tuple-element.39.refs_1_, f32[384,96]{1,0:T(8,128)S(1)} %get-tuple-element.38.ft_ref.refs_2_, ...), custom_call_target="tpu_custom_call" | custom-call | tf_op jit(solution)/shard_map/step1/pallas_call | solution.py:353
  109.3 3.5 %all-to-all-start.4 = ((f32[8,64,256]{2,1,0:T(8,128)}), f32[8,64,256]{2,1,0:T(8,128)S(1)}, u32[]{:S(2)}, u32[]{:S(2)}) async-start(f32[8,64,256]{2,1,0:T(8,128)} %get-tuple-element.51), calls=%async_computation.4 | async-start | bytes 1048576 | tf_op jit(solution)/shard_map/all_to_all | solution.py:344
  112.8 2.9 %collective-permute-start.7 = (f32[64,256]{1,0:T(8,128)S(1)}, f32[64,256]{1,0:T(8,128)S(1)}, u32[]{:S(2)}, u32[]{:S(2)}) collective-permute-start(f32[64,256]{1,0:T(8,128)S(1)} %get-tuple-element.52), channel_id=1, source_target_pairs={{32,64},{96,128},{160,192},{224,256},{288,320},{352,384},{416,448}... | collective-permute-start | bytes 196616 | tf_op jit(solution)/shard_map/ppermute | solution.py:78
  115.7 6.0 %collective-permute-start.8 = (f32[64,256]{1,0:T(8,128)S(1)}, f32[64,256]{1,0:T(8,128)S(1)}, u32[]{:S(2)}, u32[]{:S(2)}) collective-permute-start(f32[64,256]{1,0:T(8,128)S(1)} %get-tuple-element.53), channel_id=1, source_target_pairs={{1,2},{3,4},{5,6},{7,0},{2,1},{4,3},{6,5},{0,7},{9,10},{11,12},{13... | collective-permute-start | bytes 196616 | tf_op jit(solution)/shard_map/ppermute | solution.py:78
  121.8 3.4 %collective-permute-start.9 = (f32[64,256]{1,0:T(8,128)S(1)}, f32[64,256]{1,0:T(8,128)S(1)}, u32[]{:S(2)}, u32[]{:S(2)}) collective-permute-start(f32[64,256]{1,0:T(8,128)S(1)} %get-tuple-element.54), channel_id=1, source_target_pairs={{0,8},{16,24},{8,0},{24,16},{1,9},{17,25},{9,1},{25,17},{2,10},{18... | collective-permute-start | bytes 196616 | tf_op jit(solution)/shard_map/ppermute | solution.py:78
  126.0 1.4 %step2.1 = f32[96,256]{1,0:T(8,128)} custom-call(f32[2]{0:T(128)S(1)} %get-tuple-element.35.scal_ref.refs_0_, f32[96,192]{1,0:T(8,128)S(1)} %get-tuple-element.39.refs_1_, f32[384,96]{1,0:T(8,128)S(1)} %get-tuple-element.38.ft_ref.refs_2_, f32[96,256]{1,0:T(8,128)S(1)} %near2.1.refs_3_, f32[96,256]{1,0:T(8,128)S(1)} %get-tuple-element.45.now_ref.refs_4_, ...), custom_call_target="tpu_custom_call" | custom-call | tf_op jit(solution)/shard_map/step2/pallas_call | solution.py:353
  (22 shorter events, 4.0 us)
Async XLA Ops:
  0.0 0.8 copy-start.2
  0.8 66.3 %copy-start.1 = (f32[1,1,1,96,256]{4,3,2,1,0:T(8,128)S(1)}, f32[1,1,1,96,256]{4,3,2,1,0:T(8,128)}, u32[]{:S(2)}) copy-start(f32[1,1,1,96,256]{4,3,2,1,0:T(8,128)} %param.5) | copy-start | bytes 294916
  26.0 41.1 %all-to-all-start.1 = ((f32[32,1,128]{2,1,0:T(1,128)}), f32[32,1,128]{2,1,0:T(1,128)S(1)}, u32[]{:S(2)}, u32[]{:S(2)}) async-start(f32[32,1,128]{2,1,0:T(1,128)} %get-tuple-element.30), calls=%async_computation.1 | async-start | bytes 32768 | tf_op jit(solution)/shard_map/all_to_all | solution.py:313
  45.9 5.9 %collective-permute-start = (f32[8,256]{1,0:T(8,128)S(1)}, f32[8,256]{1,0:T(8,128)S(1)}, u32[]{:S(2)}, u32[]{:S(2)}) collective-permute-start(f32[8,256]{1,0:T(8,128)S(1)} %get-tuple-element.31.wide_ref), channel_id=1, source_target_pairs={{0,32},{32,64},{64,96},{96,128},{128,160},{160,192},{192,224},{224... | collective-permute-start | bytes 24584 | tf_op jit(solution)/shard_map/ppermute | solution.py:25
  51.8 1.4 %copy-start = (f32[1,1,1,96,4096]{4,3,2,1,0:T(8,128)S(1)}, f32[1,1,1,96,4096]{4,3,2,1,0:T(8,128)}, u32[]{:S(2)}) copy-start(f32[1,1,1,96,4096]{4,3,2,1,0:T(8,128)} %param.3) | copy-start | bytes 4718596
  71.4 15.6 %all-to-all-start.2 = ((f32[8,64,256]{2,1,0:T(8,128)}), f32[8,64,256]{2,1,0:T(8,128)S(1)}, u32[]{:S(2)}, u32[]{:S(2)}) async-start(f32[8,64,256]{2,1,0:T(8,128)} %get-tuple-element.41), calls=%async_computation.2 | async-start | bytes 1048576 | tf_op jit(solution)/shard_map/all_to_all | solution.py:344
  75.3 12.5 %collective-permute-start.1 = (f32[64,256]{1,0:T(8,128)S(1)}, f32[64,256]{1,0:T(8,128)S(1)}, u32[]{:S(2)}, u32[]{:S(2)}) collective-permute-start(f32[64,256]{1,0:T(8,128)S(1)} %get-tuple-element.42), channel_id=1, source_target_pairs={{32,64},{96,128},{160,192},{224,256},{288,320},{352,384},{416,448}... | collective-permute-start | bytes 196616 | tf_op jit(solution)/shard_map/ppermute | solution.py:78
  78.3 9.5 %collective-permute-start.2 = (f32[64,256]{1,0:T(8,128)S(1)}, f32[64,256]{1,0:T(8,128)S(1)}, u32[]{:S(2)}, u32[]{:S(2)}) collective-permute-start(f32[64,256]{1,0:T(8,128)S(1)} %get-tuple-element.43), channel_id=1, source_target_pairs={{1,2},{3,4},{5,6},{7,0},{2,1},{4,3},{6,5},{0,7},{9,10},{11,12},{13... | collective-permute-start | bytes 196616 | tf_op jit(solution)/shard_map/ppermute | solution.py:78
  83.0 4.9 %collective-permute-start.3 = (f32[64,256]{1,0:T(8,128)S(1)}, f32[64,256]{1,0:T(8,128)S(1)}, u32[]{:S(2)}, u32[]{:S(2)}) collective-permute-start(f32[64,256]{1,0:T(8,128)S(1)} %get-tuple-element.44), channel_id=1, source_target_pairs={{0,8},{16,24},{8,0},{24,16},{1,9},{17,25},{9,1},{25,17},{2,10},{18... | collective-permute-start | bytes 196616 | tf_op jit(solution)/shard_map/ppermute | solution.py:78
  89.6 17.1 %all-to-all-start.3 = ((f32[8,64,256]{2,1,0:T(8,128)}), f32[8,64,256]{2,1,0:T(8,128)S(1)}, u32[]{:S(2)}, u32[]{:S(2)}) async-start(f32[8,64,256]{2,1,0:T(8,128)} %get-tuple-element.46), calls=%async_computation.3 | async-start | bytes 1048576 | tf_op jit(solution)/shard_map/all_to_all | solution.py:344
  93.1 14.4 %collective-permute-start.4 = (f32[64,256]{1,0:T(8,128)S(1)}, f32[64,256]{1,0:T(8,128)S(1)}, u32[]{:S(2)}, u32[]{:S(2)}) collective-permute-start(f32[64,256]{1,0:T(8,128)S(1)} %get-tuple-element.47), channel_id=1, source_target_pairs={{32,64},{96,128},{160,192},{224,256},{288,320},{352,384},{416,448}... | collective-permute-start | bytes 196616 | tf_op jit(solution)/shard_map/ppermute | solution.py:78
  98.2 9.3 %collective-permute-start.5 = (f32[64,256]{1,0:T(8,128)S(1)}, f32[64,256]{1,0:T(8,128)S(1)}, u32[]{:S(2)}, u32[]{:S(2)}) collective-permute-start(f32[64,256]{1,0:T(8,128)S(1)} %get-tuple-element.48), channel_id=1, source_target_pairs={{1,2},{3,4},{5,6},{7,0},{2,1},{4,3},{6,5},{0,7},{9,10},{11,12},{13... | collective-permute-start | bytes 196616 | tf_op jit(solution)/shard_map/ppermute | solution.py:78
  103.3 4.3 %collective-permute-start.6 = (f32[64,256]{1,0:T(8,128)S(1)}, f32[64,256]{1,0:T(8,128)S(1)}, u32[]{:S(2)}, u32[]{:S(2)}) collective-permute-start(f32[64,256]{1,0:T(8,128)S(1)} %get-tuple-element.49), channel_id=1, source_target_pairs={{0,8},{16,24},{8,0},{24,16},{1,9},{17,25},{9,1},{25,17},{2,10},{18... | collective-permute-start | bytes 196616 | tf_op jit(solution)/shard_map/ppermute | solution.py:78
  109.3 15.9 %all-to-all-start.4 = ((f32[8,64,256]{2,1,0:T(8,128)}), f32[8,64,256]{2,1,0:T(8,128)S(1)}, u32[]{:S(2)}, u32[]{:S(2)}) async-start(f32[8,64,256]{2,1,0:T(8,128)} %get-tuple-element.51), calls=%async_computation.4 | async-start | bytes 1048576 | tf_op jit(solution)/shard_map/all_to_all | solution.py:344
  112.8 13.2 %collective-permute-start.7 = (f32[64,256]{1,0:T(8,128)S(1)}, f32[64,256]{1,0:T(8,128)S(1)}, u32[]{:S(2)}, u32[]{:S(2)}) collective-permute-start(f32[64,256]{1,0:T(8,128)S(1)} %get-tuple-element.52), channel_id=1, source_target_pairs={{32,64},{96,128},{160,192},{224,256},{288,320},{352,384},{416,448}... | collective-permute-start | bytes 196616 | tf_op jit(solution)/shard_map/ppermute | solution.py:78
  115.7 10.2 %collective-permute-start.8 = (f32[64,256]{1,0:T(8,128)S(1)}, f32[64,256]{1,0:T(8,128)S(1)}, u32[]{:S(2)}, u32[]{:S(2)}) collective-permute-start(f32[64,256]{1,0:T(8,128)S(1)} %get-tuple-element.53), channel_id=1, source_target_pairs={{1,2},{3,4},{5,6},{7,0},{2,1},{4,3},{6,5},{0,7},{9,10},{11,12},{13... | collective-permute-start | bytes 196616 | tf_op jit(solution)/shard_map/ppermute | solution.py:78
  121.8 4.3 %collective-permute-start.9 = (f32[64,256]{1,0:T(8,128)S(1)}, f32[64,256]{1,0:T(8,128)S(1)}, u32[]{:S(2)}, u32[]{:S(2)}) collective-permute-start(f32[64,256]{1,0:T(8,128)S(1)} %get-tuple-element.54), channel_id=1, source_target_pairs={{0,8},{16,24},{8,0},{24,16},{1,9},{17,25},{9,1},{25,17},{2,10},{18... | collective-permute-start | bytes 196616 | tf_op jit(solution)/shard_map/ppermute | solution.py:78
